TPU v7x, 32 devices: a whole 2x2x4 slice. The times are simulated.
32 devices in a mesh: mz: 4 (over z), px: 8 (over y, x, core).
Axes of the slice: x: 2, y: 2, z: 4, core: 2. Of those that a mesh axis runs over, the one named last changes fastest.
Arguments:
- spectra: float32 [3072, 12288], P('px', 'mz'), may hold values from 0 to 10
- w_factor: float32 [48, 3072], P(None, ('px', 'mz')), may hold values from 0.05 to 1
- h_factor: float32 [48, 12288], P(None, ('mz', 'px')), may hold values from 0.05 to 1
Outputs:
- w_final: float32 [48, 3072], P(None, ('px', 'mz'))
- h_final: float32 [48, 12288], P(None, ('mz', 'px'))
- misfit: float32 [3072], P(('px', 'mz'))
All inputs are finite; a program needn't handle non-finite values.
Results may differ from a plain program's by a relative error of at most 0.0001.
Values sent between devices are 32-bit elements; how exact they have to be, the bound alone decides.
No kernel may reach another device: no remote copies, remote signals or barrier semaphores. Data moves between devices by JAX's collectives and lax.ppermute only.
A program may use at most 64 MiB of HBM per device.

v0:
```python
import jax
import jax.numpy as jnp
from jax import lax
from jax.sharding import PartitionSpec as P

ITERS = 3


def matmul(left, right):
    return jnp.dot(left, right, preferred_element_type=jnp.float32, precision=lax.Precision.HIGHEST)


def rows_of(w_piece):
    return lax.all_gather(w_piece, "mz", axis=1, tiled=True)


def loading_gram(w_block):
    return lax.psum(matmul(w_block, w_block.T), "px")


def spectral_gram(h_block):
    return lax.psum(matmul(h_block, h_block.T), "mz")


def per_device(spectra, w_factor, h_factor):
    w_piece = w_factor
    h_piece = h_factor
    w_block = rows_of(w_piece)
    h_block = h_piece
    for iteration in range(ITERS):
        numerator = lax.psum_scatter(
            matmul(w_block, spectra), "px", scatter_dimension=1, tiled=True
        )
        gram_w = loading_gram(w_block)
        h_piece = h_piece * numerator / matmul(gram_w, h_piece)
        h_block = lax.all_gather(h_piece, "px", axis=1, tiled=True)
        numerator = lax.psum_scatter(
            matmul(h_block, spectra.T), "mz", scatter_dimension=1, tiled=True
        )
        gram_h = spectral_gram(h_block)
        w_piece = w_piece * numerator / matmul(gram_h, w_piece)
        w_block = rows_of(w_piece)
    difference = spectra - matmul(w_block.T, h_block)
    partial_error = jnp.sum(difference * difference, axis=1)
    misfit = lax.psum_scatter(partial_error, "mz", scatter_dimension=0, tiled=True)
    return (w_piece, h_piece, misfit)


def solution(mesh):
    in_specs = (P("px", "mz"), P(None, ("px", "mz")), P(None, ("mz", "px")))
    out_specs = (P(None, ("px", "mz")), P(None, ("mz", "px")), P(("px", "mz")))
    return jax.shard_map(
        per_device, mesh=mesh, in_specs=in_specs, out_specs=out_specs, check_vma=False
    )
```

profile of v0, /device:TPU:0, one launch (start us, length us, event | category | flops | bytes accessed | tf_op | source)
XLA Modules:
  0.0 318.1 jit_solution(4339543671412896273)
XLA Ops:
  7.2 15.3 %all-gather = f32[4,96,48]{1,2,0:T(8,128)S(1)} all-gather(f32[1,96,48]{1,2,0:T(8,128)} %bitcast.70), channel_id=1, replica_groups=mesh['mz'=4,'px'=8] {'mz'}, dimensions={0}, use_global_device_ids=true | all-gather | bytes 92160 | tf_op jit(solution)/shard_map/all_gather | solution.py:14
  22.7 6.1 %fusion = f32[48,3072]{1,0:T(8,128)} fusion(f32[384,48]{0,1:T(8,128)S(1)} %reshape.7, f32[384,3072]{1,0:T(8,128)} %param.3), kind=kOutput, calls=%fused_computation.10 | convolution fusion | flops 679477248 | bytes 5382144 | tf_op jit(solution)/shard_map/dot_general | solution.py:10
  29.0 22.5 %psum.42 = f32[48,48]{1,0:T(8,128)S(1)} all-reduce(f32[48,48]{1,0:T(8,128)S(1)} %fusion.1), channel_id=1, replica_groups=mesh['mz'=4,'px'=8] {'px'}, use_global_device_ids=true, to_apply=%region_1.0 | all-reduce | flops 2304 | bytes 18432 | tf_op jit(solution)/shard_map/psum | solution.py:18
  51.5 11.9 %reduce-scatter.13.cloned.1.call-done = f32[48,384]{1,0:T(8,128)} async-done(((f32[48,3072]{1,0:T(8,128)}), f32[48,384]{1,0:T(8,128)}) %reduce-scatter.13.cloned.1.call-update) | async-done | bytes 73744 | tf_op jit(solution)/shard_map/reduce_scatter | solution.py:31
  64.5 10.4 %all_gather.22 = f32[48,3072]{1,0:T(8,128)S(1)} all-gather(f32[48,384]{1,0:T(8,128)S(1)} %convolution_divide_fusion.2), channel_id=1, replica_groups=mesh['mz'=4,'px'=8] {'px'}, dimensions={1}, use_global_device_ids=true | all-gather | bytes 663552 | tf_op jit(solution)/shard_map/all_gather | solution.py:36
  74.8 6.3 %convolution_bitcast_fusion.2 = f32[384,48]{1,0:T(8,128)} fusion(f32[48,3072]{1,0:T(8,128)S(1)} %all_gather.22, f32[384,3072]{1,0:T(8,128)} %param.3), kind=kOutput, calls=%fused_computation.3 | convolution fusion | flops 679477248 | bytes 5382144
  81.8 19.1 %psum.43 = f32[48,48]{1,0:T(8,128)S(1)} all-reduce(f32[48,48]{1,0:T(8,128)S(1)} %fusion.2), channel_id=1, replica_groups=mesh['mz'=4,'px'=8] {'mz'}, use_global_device_ids=true, to_apply=%region_3.0 | all-reduce | flops 2304 | bytes 18432 | tf_op jit(solution)/shard_map/psum | solution.py:22
  102.1 13.3 %all-gather.1 = f32[4,96,48]{1,2,0:T(8,128)S(1)} all-gather(f32[1,96,48]{1,2,0:T(8,128)S(1)} %bitcast.69), channel_id=1, replica_groups=mesh['mz'=4,'px'=8] {'mz'}, dimensions={0}, use_global_device_ids=true | all-gather | bytes 92160 | tf_op jit(solution)/shard_map/all_gather | solution.py:14
  115.6 6.1 %fusion.3 = f32[48,3072]{1,0:T(8,128)} fusion(f32[384,48]{0,1:T(8,128)S(1)} %reshape.9, f32[384,3072]{1,0:T(8,128)} %param.3), kind=kOutput, calls=%fused_computation.13 | convolution fusion | flops 679477248 | bytes 5382144 | tf_op jit(solution)/shard_map/dot_general | solution.py:10
  121.9 22.5 %psum.44 = f32[48,48]{1,0:T(8,128)S(1)} all-reduce(f32[48,48]{1,0:T(8,128)S(1)} %fusion.4), channel_id=1, replica_groups=mesh['mz'=4,'px'=8] {'px'}, use_global_device_ids=true, to_apply=%region_5.0 | all-reduce | flops 2304 | bytes 18432 | tf_op jit(solution)/shard_map/psum | solution.py:18
  144.4 8.9 %reduce-scatter.15.cloned.1.call-done = f32[48,384]{1,0:T(8,128)} async-done(((f32[48,3072]{1,0:T(8,128)}), f32[48,384]{1,0:T(8,128)}) %reduce-scatter.15.cloned.1.call-update) | async-done | bytes 73744 | tf_op jit(solution)/shard_map/reduce_scatter | solution.py:31
  154.4 10.5 %all_gather.24 = f32[48,3072]{1,0:T(8,128)S(1)} all-gather(f32[48,384]{1,0:T(8,128)S(1)} %convolution_divide_fusion.1), channel_id=1, replica_groups=mesh['mz'=4,'px'=8] {'px'}, dimensions={1}, use_global_device_ids=true | all-gather | bytes 663552 | tf_op jit(solution)/shard_map/all_gather | solution.py:36
  165.0 6.3 %convolution_bitcast_fusion.1 = f32[384,48]{1,0:T(8,128)} fusion(f32[48,3072]{1,0:T(8,128)S(1)} %all_gather.24, f32[384,3072]{1,0:T(8,128)} %param.3), kind=kOutput, calls=%fused_computation.2 | convolution fusion | flops 679477248 | bytes 5382144
  172.0 19.1 %psum.45 = f32[48,48]{1,0:T(8,128)S(1)} all-reduce(f32[48,48]{1,0:T(8,128)S(1)} %fusion.5), channel_id=1, replica_groups=mesh['mz'=4,'px'=8] {'mz'}, use_global_device_ids=true, to_apply=%region_7.0 | all-reduce | flops 2304 | bytes 18432 | tf_op jit(solution)/shard_map/psum | solution.py:22
  192.2 13.3 %all-gather.2 = f32[4,96,48]{1,2,0:T(8,128)S(1)} all-gather(f32[1,96,48]{1,2,0:T(8,128)S(1)} %bitcast.68), channel_id=1, replica_groups=mesh['mz'=4,'px'=8] {'mz'}, dimensions={0}, use_global_device_ids=true | all-gather | bytes 92160 | tf_op jit(solution)/shard_map/all_gather | solution.py:14
  205.7 6.1 %fusion.6 = f32[48,3072]{1,0:T(8,128)} fusion(f32[384,48]{0,1:T(8,128)S(1)} %reshape.11, f32[384,3072]{1,0:T(8,128)} %param.3), kind=kOutput, calls=%fused_computation.16 | convolution fusion | flops 679477248 | bytes 5382144 | tf_op jit(solution)/shard_map/dot_general | solution.py:10
  213.3 22.4 %psum.46 = f32[48,48]{1,0:T(8,128)S(1)} all-reduce(f32[48,48]{1,0:T(8,128)S(1)} %fusion.7), channel_id=1, replica_groups=mesh['mz'=4,'px'=8] {'px'}, use_global_device_ids=true, to_apply=%region_9.0 | all-reduce | flops 2304 | bytes 18432 | tf_op jit(solution)/shard_map/psum | solution.py:18
  235.7 7.9 %reduce-scatter.17.cloned.1.call-done = f32[48,384]{1,0:T(8,128)} async-done(((f32[48,3072]{1,0:T(8,128)}), f32[48,384]{1,0:T(8,128)}) %reduce-scatter.17.cloned.1.call-update) | async-done | bytes 73744 | tf_op jit(solution)/shard_map/reduce_scatter | solution.py:31
  244.7 10.4 %all_gather.26 = f32[48,3072]{1,0:T(8,128)S(1)} all-gather(f32[48,384]{1,0:T(8,128)S(1)} %convolution_divide_fusion), channel_id=1, replica_groups=mesh['mz'=4,'px'=8] {'px'}, dimensions={1}, use_global_device_ids=true | all-gather | bytes 663552 | tf_op jit(solution)/shard_map/all_gather | solution.py:36
  255.0 6.3 %convolution_bitcast_fusion = f32[384,48]{1,0:T(8,128)} fusion(f32[48,3072]{1,0:T(8,128)S(1)} %all_gather.26, f32[384,3072]{1,0:T(8,128)} %param.3), kind=kOutput, calls=%fused_computation.1 | convolution fusion | flops 679477248 | bytes 5382144
  261.9 19.1 %psum.47 = f32[48,48]{1,0:T(8,128)S(1)} all-reduce(f32[48,48]{1,0:T(8,128)S(1)} %fusion.8), channel_id=1, replica_groups=mesh['mz'=4,'px'=8] {'mz'}, use_global_device_ids=true, to_apply=%region_11.0 | all-reduce | flops 2304 | bytes 18432 | tf_op jit(solution)/shard_map/psum | solution.py:22
  282.1 13.3 %all-gather.3 = f32[4,96,48]{1,2,0:T(8,128)S(1)} all-gather(f32[1,96,48]{1,2,0:T(8,128)S(1)} %bitcast.71), channel_id=1, replica_groups=mesh['mz'=4,'px'=8] {'mz'}, dimensions={0}, use_global_device_ids=true | all-gather | bytes 92160 | tf_op jit(solution)/shard_map/all_gather | solution.py:14
  295.6 6.0 %multiply_reduce_fusion = f32[384]{0:T(512)S(1)} fusion(f32[384,3072]{1,0:T(8,128)} %param.3, f32[384,48]{0,1:T(8,128)S(1)} %reshape.13, f32[48,3072]{1,0:T(8,128)S(1)} %all_gather.26), kind=kOutput, calls=%fused_computation | convolution fusion | flops 683015808 | bytes 5383680 | tf_op jit(solution)/shard_map/dot_general | solution.py:10
  301.7 8.9 %all-reduce = f32[384]{0:T(512)S(1)} all-reduce(f32[384]{0:T(512)S(1)} %multiply_reduce_fusion), channel_id=8, replica_groups=mesh['mz'=4,'px'=8] {'mz'}, use_global_device_ids=true, to_apply=%region_13.0.clone | all-reduce | flops 384 | bytes 3072
  (50 shorter events, 11.2 us)
Async XLA Ops:
  7.2 56.2 %copy-start.3 = (f32[48,384]{1,0:T(8,128)S(1)}, f32[48,384]{1,0:T(8,128)}, u32[]{:S(2)}) copy-start(f32[48,384]{1,0:T(8,128)} %param.5) | copy-start | bytes 221188
  7.2 56.2 %reduce-scatter.13.cloned.1.call-start = ((), (), s32[]{:S(2)}) async-start(), calls=%async_computation.6 | async-start | bytes 663552 | tf_op jit(solution)/shard_map/reduce_scatter | solution.py:31
  28.7 73.1 %copy-start = (f32[48,96]{1,0:T(8,128)S(1)}, f32[48,96]{1,0:T(8,128)}, u32[]{:S(2)}) copy-start(f32[48,96]{1,0:T(8,128)} %param.4) | copy-start | bytes 55300
  28.8 72.3 %reduce-scatter.19.cloned.1.call-start = ((), (), s32[]{:S(2)}) async-start(), calls=%async_computation.9 | async-start | bytes 245760
  81.1 72.2 %reduce-scatter.15.cloned.1.call-start = ((), (), s32[]{:S(2)}) async-start(), calls=%async_computation.7 | async-start | bytes 663552 | tf_op jit(solution)/shard_map/reduce_scatter | solution.py:31
  121.7 69.5 %reduce-scatter.21.cloned.1.call-start = ((), (), s32[]{:S(2)}) async-start(), calls=%async_computation.10 | async-start | bytes 245760
  171.3 40.6 %copy-start.4 = (u32[32]{0:T(128)S(1)}, u32[32]{0:T(128)}, u32[]{:S(2)}) copy-start(u32[32]{0:T(128)} %constant.4) | copy-start | bytes 388
  171.3 72.2 %reduce-scatter.17.cloned.1.call-start = ((), (), s32[]{:S(2)}) async-start(), calls=%async_computation.8 | async-start | bytes 663552 | tf_op jit(solution)/shard_map/reduce_scatter | solution.py:31
  211.8 69.3 %reduce-scatter.23.cloned.1.call-start = ((), (), s32[]{:S(2)}) async-start(), calls=%async_computation.11 | async-start | bytes 245760
  244.6 57.0 %copy-start.2 = (f32[48,384]{1,0:T(8,128)}, f32[48,384]{1,0:T(8,128)S(1)}, u32[]{:S(2)}) copy-start(f32[48,384]{1,0:T(8,128)S(1)} %convolution_divide_fusion) | copy-start | bytes 221188
  282.1 29.1 %copy-start.1 = (f32[48,96]{1,0:T(8,128)}, f32[48,96]{1,0:T(8,128)S(1)}, u32[]{:S(2)}) copy-start(f32[48,96]{1,0:T(8,128)S(1)} %convolution_divide_fusion.3) | copy-start | bytes 55300
Sparse Core Ops, SparseCore 0:
  28.9 34.4 reduce-scatter.12
  81.3 19.6 reduce-scatter.18
  121.8 31.5 reduce-scatter.14
  171.4 19.6 reduce-scatter.20
  211.9 31.5 reduce-scatter.16
  261.4 19.5 reduce-scatter.22
where the time goes:
time: 319 us; the launch traced here: 318 us
  blocking collectives  220 us (69%)
  matrix products  49.4 us (15%)
  waiting for transfers between devices  29 us (9%)
  between operations  15 us (5%)
  local copies, waits for them, and re-layouts  4.36 us (1%)
    psum x3, blocking collectives, loading_gram(): return lax.psum(matmul(w_block, w_block.T), 'px')  67.3 us
    psum x3, blocking collectives, spectral_gram(): return lax.psum(matmul(h_block, h_block.T), 'mz')  57.3 us
    all_gather x4, blocking collectives, rows_of(): return lax.all_gather(w_piece, 'mz', axis=1, tiled=True)  55.3 us
    all_gather x3, blocking collectives, per_device(): h_block = lax.all_gather(h_piece, 'px', axis=1, tiled=True)  31.2 us
    dot_general x16, matrix products, matmul(): jnp.dot(left, right, preferred_element_type=jnp.float32, precision=lax.Pr...  30.5 us
    reduce_scatter x3, waiting for transfers between devices, per_device(): lax.psum_scatter(matmul(w_block, spectra), 'px', scatter_dimension=1, til...  28.7 us
    unnamed x3, matrix products  18.9 us
    unnamed x1, blocking collectives  8.95 us
  transfers between devices with their start and end apart: 6, of which 5 were waited for; matrix products, arithmetic and copies ran while one was open for 1% of the time, Pallas kernels for 0%

commit v1 on v0

v1 whole, which is shorter than its diff:
```python
import functools

import jax
import jax.numpy as jnp
from jax import lax
from jax.experimental import pallas as pl
from jax.experimental.pallas import tpu as pltpu
from jax.sharding import PartitionSpec as P

ITERS = 3
LANES = 128
SUBLANES = 8
F32 = jnp.float32
BF16 = jnp.bfloat16
NN = (((1,), (0,)), ((), ()))
NT = (((1,), (1,)), ((), ()))
TN = (((0,), (0,)), ((), ()))


def matmul(left, right):
    return jnp.dot(left, right, preferred_element_type=F32, precision=lax.Precision.HIGHEST)


def plain_device(spectra, w_piece, h_piece):
    def rows_of(piece):
        return lax.all_gather(piece, "mz", axis=1, tiled=True)

    w_block = rows_of(w_piece)
    for _ in range(ITERS):
        numerator = lax.psum_scatter(matmul(w_block, spectra), "px", scatter_dimension=1, tiled=True)
        gram_w = lax.psum(matmul(w_block, w_block.T), "px")
        h_piece = h_piece * numerator / matmul(gram_w, h_piece)
        h_block = lax.all_gather(h_piece, "px", axis=1, tiled=True)
        numerator = lax.psum_scatter(matmul(h_block, spectra.T), "mz", scatter_dimension=1, tiled=True)
        gram_h = lax.psum(matmul(h_block, h_block.T), "mz")
        w_piece = w_piece * numerator / matmul(gram_h, w_piece)
        w_block = rows_of(w_piece)
    difference = spectra - matmul(w_block.T, h_block)
    partial_error = jnp.sum(difference * difference, axis=1)
    misfit = lax.psum_scatter(partial_error, "mz", scatter_dimension=0, tiled=True)
    return (w_piece, h_piece, misfit)


def split(value):
    high = value.astype(BF16)
    return high, (value - high.astype(F32)).astype(BF16)


def exact(left, right, dims):
    return lax.dot_general(left, right, dims, precision=lax.Precision.HIGHEST, preferred_element_type=F32)


def fast(left, right, dims):
    return lax.dot_general(left, right, dims, preferred_element_type=F32)


def stacked(value):
    high, low = split(value)
    return jnp.concatenate([high, low], axis=0), high


def product(stack, high, s_high, s_low, dims):
    rows = high.shape[0]
    both = fast(stack, s_high, dims)
    return both[:rows] + both[rows:] + fast(high, s_low, dims)


def pack_gram(ref, gram):
    rank = gram.shape[0]
    ref[rank:, :] = jnp.zeros((SUBLANES, ref.shape[1]), F32)
    for group in range(rank // SUBLANES):
        rows = slice(group * SUBLANES, (group + 1) * SUBLANES)
        ref[rank:, group * rank : (group + 1) * rank] = gram[rows, :]


def unpack_gram(packed, rank):
    return jnp.concatenate(
        [packed[:, group * rank : (group + 1) * rank] for group in range(rank // SUBLANES)], axis=0
    )


def params(**more):
    return pltpu.CompilerParams(vmem_limit_bytes=32 << 20, **more)


def vmem(count):
    return [pl.BlockSpec(memory_space=pltpu.VMEM)] * count


def cost(flops, moved):
    return pl.CostEstimate(flops=int(flops), bytes_accessed=int(moved), transcendentals=0)


def split_kernel(s_ref, high_ref, low_ref):
    high_ref[...], low_ref[...] = split(s_ref[...])


def split_call(spectra):
    rows, columns = spectra.shape
    step = min(columns, 512)
    spec = pl.BlockSpec((rows, step), lambda i: (0, i))
    return pl.pallas_call(
        split_kernel,
        grid=(columns // step,),
        in_specs=[spec],
        out_specs=[spec, spec],
        out_shape=[jax.ShapeDtypeStruct((rows, columns), BF16)] * 2,
        compiler_params=params(),
        cost_estimate=cost(4 * rows * columns, 8 * rows * columns),
        name="split_spectra",
    )(spectra)


def bins_of(relative, width):
    block = jnp.bitwise_xor(lax.axis_index("px"), relative)
    return pl.ds(pl.multiple_of(block * width, LANES), width)


def scatter_kernel(relatives, width, w_ref, high_ref, low_ref, *outs):
    w = w_ref[...]
    rank = w.shape[0]
    stack, w_high = stacked(w)
    gram = product(stack, w_high, *split(w), NT)
    for relative, out in zip(relatives, outs):
        here = bins_of(relative, width)
        out[:rank, :] = product(stack, w_high, high_ref[:, here], low_ref[:, here], NN)
        pack_gram(out, gram)


def scatter_call(relatives, width, w_block, high, low):
    rank, pixels = w_block.shape
    count = len(relatives)
    return pl.pallas_call(
        functools.partial(scatter_kernel, relatives, width),
        in_specs=vmem(3),
        out_specs=vmem(count),
        out_shape=[jax.ShapeDtypeStruct((rank + SUBLANES, width), F32)] * count,
        compiler_params=params(),
        cost_estimate=cost(6 * rank * pixels * width * count, 4 * pixels * width * count),
        name="loadings_times_spectra",
    )(w_block, high, low)


def update_kernel(factor_ref, *refs):
    parts, out = refs[:-1], refs[-1]
    factor = factor_ref[...]
    rank = factor.shape[0]
    total = parts[0][...]
    for part in parts[1:]:
        total = total + part[...]
    gram = unpack_gram(total[rank:], rank)
    out[...] = factor * total[:rank] / exact(gram, factor, NN)


def update_call(factor, *parts):
    rank, width = factor.shape
    return pl.pallas_call(
        update_kernel,
        in_specs=vmem(1 + len(parts)),
        out_specs=pl.BlockSpec(memory_space=pltpu.VMEM),
        out_shape=jax.ShapeDtypeStruct((rank, width), F32),
        compiler_params=params(),
        cost_estimate=cost(12 * rank * rank * width, 4 * rank * width * (2 + len(parts))),
        name="update",
    )(factor, *parts)


def add_kernel(left_ref, right_ref, out_ref):
    out_ref[...] = left_ref[...] + right_ref[...]


def add_call(left, right):
    return pl.pallas_call(
        add_kernel,
        in_specs=vmem(2),
        out_specs=pl.BlockSpec(memory_space=pltpu.VMEM),
        out_shape=jax.ShapeDtypeStruct(left.shape, F32),
        compiler_params=params(),
        cost_estimate=cost(left.size, 12 * left.size),
        name="add",
    )(left, right)


def gather_kernel(relatives, carried, high_ref, low_ref, *refs):
    out = refs[-1]
    pieces = refs[: len(relatives)]
    rank, width = pieces[0].shape
    total, gram = None, None
    for relative, piece in zip(relatives, pieces):
        h = piece[...]
        stack, h_high = stacked(h)
        here = bins_of(relative, width)
        term = product(stack, h_high, high_ref[:, here], low_ref[:, here], NT)
        square = product(stack, h_high, *split(h), NT)
        total = term if total is None else total + term
        gram = square if gram is None else gram + square
    out[:rank, :] = total
    pack_gram(out, gram)
    if carried:
        out[...] += refs[len(relatives)][...]


def gather_call(relatives, pieces, high, low, before):
    rank, width = pieces[0].shape
    pixels = high.shape[0]
    extra = () if before is None else (before,)
    count = len(relatives)
    return pl.pallas_call(
        functools.partial(gather_kernel, relatives, before is not None),
        in_specs=vmem(2 + count + len(extra)),
        out_specs=pl.BlockSpec(memory_space=pltpu.VMEM),
        out_shape=jax.ShapeDtypeStruct((rank + SUBLANES, pixels), F32),
        compiler_params=params(),
        cost_estimate=cost(6 * rank * pixels * width * count, 4 * pixels * width * count),
        name="spectra_times_components",
    )(high, low, *pieces, *extra)


def final_gather_kernel(relatives, groups, first, last, s_ref, w_ref, *refs):
    pieces, refs = refs[: len(relatives)], refs[len(relatives) :]
    if not first:
        before_ref, gram_before_ref, refs = refs[0], refs[1], refs[2:]
    rank, width = pieces[0].shape
    pixels = w_ref.shape[1]
    w_t = w_ref[...].T
    w0, w1 = split(w_t)
    w2 = (w_t - w0.astype(F32) - w1.astype(F32)).astype(BF16)
    left = jnp.concatenate([w0, w0, w1, w1, w0, w2], axis=1)
    lane = lax.broadcasted_iota(jnp.int32, (pixels, LANES), 1)
    zeros = functools.partial(jnp.zeros, dtype=BF16)
    total, gram = None, None
    for relative, piece in zip(relatives, pieces):
        h = piece[...]
        h0, h1 = split(h)
        h2 = (h - h0.astype(F32) - h1.astype(F32)).astype(BF16)
        s = s_ref[:, bins_of(relative, width)]
        right = jnp.concatenate([h0, h1, h0, h1, h2, h0], axis=0)
        d = s - fast(left, right, NN)
        tail = zeros((LANES - rank, width))
        tail2 = zeros((LANES - 2 * rank, width))
        pad = zeros((rank, width))
        num_high = jnp.concatenate([h0, tail], axis=0)
        num_both = jnp.concatenate([num_high, h1, tail], axis=0)
        err_high = jnp.concatenate([pad, h0, tail2], axis=0)
        err_both = jnp.concatenate([err_high, pad, h1, tail2], axis=0)
        s0, s1 = split(s)
        d0, d1 = split(d)
        both = fast(s0, num_both, NT) + fast(d0, err_both, NT)
        term = both[:, :LANES] + both[:, LANES:] + fast(s1, num_high, NT) + fast(d1, err_high, NT)
        squares = jnp.sum(d * d, axis=1, keepdims=True)
        term = jnp.where(lane == 2 * rank, squares, term)
        stack, h_high = stacked(h)
        square = product(stack, h_high, h0, h1, NT)
        total = term if total is None else total + term
        gram = square if gram is None else gram + square
    if not first:
        total = total + before_ref[...]
        gram = gram + gram_before_ref[...]
    if not last:
        refs[0][...] = total
        refs[1][...] = gram
        return
    outs, own_ref, scratch, w_scratch = refs[:groups], refs[groups], refs[-2], refs[-1]
    scratch[...] = total
    w_scratch[...] = w_t
    rows = pixels // groups
    me = lax.axis_index("mz")
    for relative, out in enumerate(outs):
        group = jnp.bitwise_xor(me, relative)
        out[:rows, :] = scratch[pl.ds(pl.multiple_of(group * rows, SUBLANES), rows), :]
        out[rows:, :] = jnp.zeros((rank, LANES), F32)
        out[rows:, :rank] = gram
    own_ref[...] = w_scratch[pl.ds(pl.multiple_of(me * rows, SUBLANES), rows), :]


def final_gather_call(relatives, groups, pieces, spectra, w_block, before, last):
    rank, width = pieces[0].shape
    pixels = w_block.shape[1]
    rows = pixels // groups
    count = len(relatives)
    first = before is None
    extra = () if first else tuple(before)
    if last:
        shapes = [jax.ShapeDtypeStruct((rows + rank, LANES), F32)] * groups
        shapes.append(jax.ShapeDtypeStruct((rows, rank), F32))
        scratch = [pltpu.VMEM((pixels, LANES), F32), pltpu.VMEM((pixels, rank), F32)]
    else:
        shapes = [jax.ShapeDtypeStruct((pixels, LANES), F32), jax.ShapeDtypeStruct((rank, rank), F32)]
        scratch = []
    return pl.pallas_call(
        functools.partial(final_gather_kernel, relatives, groups, first, last),
        in_specs=vmem(2 + count + len(extra)),
        out_specs=vmem(len(shapes)),
        out_shape=shapes,
        scratch_shapes=scratch,
        compiler_params=params(),
        cost_estimate=cost(24 * rank * pixels * width * count, 8 * pixels * width * count),
        name="final_products",
    )(spectra, w_block, *pieces, *extra)


def final_kernel(w_t_ref, *refs):
    parts, (w_out, misfit_out) = refs[:-2], refs[-2:]
    w_t = w_t_ref[...]
    rows, rank = w_t.shape
    total = parts[0][...]
    for part in parts[1:]:
        total = total + part[...]
    gram = total[rows:, :rank]
    num, err = total[:rows, :rank], total[:rows, rank : 2 * rank]
    new = w_t * num / exact(w_t, gram, NN)
    w_out[...] = new.T
    step = new - w_t
    change = step * (exact(step, gram, NN) - 2.0 * err)
    pick = (lax.broadcasted_iota(jnp.int32, (SUBLANES, LANES), 1) == 2 * rank).astype(F32)
    misfit = exact(pick, total[:rows], NT) + exact(jnp.ones((SUBLANES, rank), F32), change, NT)
    misfit_out[...] = misfit[:1]


def final_call(w_t, *parts):
    rows, rank = w_t.shape
    return pl.pallas_call(
        final_kernel,
        in_specs=vmem(1 + len(parts)),
        out_specs=vmem(2),
        out_shape=[jax.ShapeDtypeStruct((rank, rows), F32), jax.ShapeDtypeStruct((1, rows), F32)],
        compiler_params=params(),
        cost_estimate=cost(24 * rank * rank * rows, 4 * rows * LANES * len(parts)),
        name="final_update",
    )(w_t, *parts)


def join_kernel(*refs):
    pieces, out = refs[:-1], refs[-1]
    rank, width = pieces[0].shape
    whole = jnp.concatenate([piece[...] for piece in pieces], axis=1)
    out[...] = pltpu.roll(whole, lax.axis_index("mz") * width, 1)


def join_call(*pieces):
    rank, width = pieces[0].shape
    return pl.pallas_call(
        join_kernel,
        in_specs=vmem(len(pieces)),
        out_specs=pl.BlockSpec(memory_space=pltpu.VMEM),
        out_shape=jax.ShapeDtypeStruct((rank, width * len(pieces)), F32),
        compiler_params=params(),
        cost_estimate=cost(0, 8 * rank * width * len(pieces)),
        name="join",
    )(*pieces)


def swap(value, axis, size, mask):
    return lax.ppermute(value, axis, [(i, i ^ mask) for i in range(size)])


def fast_device(groups, owners, spectra, w_piece, h_piece):
    width = h_piece.shape[1]
    far = [r for r in range(owners - 1, 1, -1)]
    high, low = split_call(spectra)
    w_block = join_call(
        w_piece,
        *[
            lax.ppermute(w_piece, "mz", [(i, (i - k) % groups) for i in range(groups)])
            for k in range(1, groups)
        ],
    )
    evens = list(range(2, owners, 2))
    for iteration in range(ITERS):
        parts = scatter_call(far, width, w_block, high, low)
        sent = [swap(part, "px", owners, r) for part, r in zip(parts, far)]
        near = scatter_call([1, 0], width, w_block, high, low)
        sent.append(swap(near[0], "px", owners, 1))
        h_piece = update_call(h_piece, near[1], *sent)
        beside = swap(h_piece, "px", owners, 1)
        mine = [swap(h_piece, "px", owners, r) for r in evens]
        theirs = [swap(piece, "px", owners, 1) for piece in mine]
        odds = [r + 1 for r in evens]
        if iteration + 1 < ITERS:
            total = gather_call([0, 1], [h_piece, beside], high, low, None)
            total = gather_call(evens, mine, high, low, total)
            total = gather_call(odds, theirs, high, low, total)
            mask = 1
            while 2 * mask < groups:
                total = add_call(total, swap(total, "mz", groups, mask))
                mask *= 2
            w_block = update_call(w_block, total, swap(total, "mz", groups, mask))
        else:
            call = functools.partial(final_gather_call, spectra=spectra, w_block=w_block)
            total = call([0, 1], groups, [h_piece, beside], before=None, last=False)
            total = call(evens, groups, mine, before=total, last=False)
            *parts, w_t = call(odds, groups, theirs, before=total, last=True)
            sent = [swap(parts[k], "mz", groups, k) for k in range(1, groups)]
            w_final, misfit = final_call(w_t, parts[0], *sent)
    return w_final, h_piece, misfit.reshape(-1)


def per_device(groups, owners, spectra, w_piece, h_piece):
    rank = w_piece.shape[0]
    pixels, width = spectra.shape[0], h_piece.shape[1]

    def power(n):
        return n > 1 and n & (n - 1) == 0

    fits = (
        power(groups)
        and power(owners)
        and width % LANES == 0
        and pixels % LANES == 0
        and w_piece.shape[1] % SUBLANES == 0
        and rank % (2 * SUBLANES) == 0
        and rank // SUBLANES * rank <= min(width, pixels)
        and 2 * rank < LANES
    )
    if fits:
        return fast_device(groups, owners, spectra, w_piece, h_piece)
    return plain_device(spectra, w_piece, h_piece)


def solution(mesh):
    in_specs = (P("px", "mz"), P(None, ("px", "mz")), P(None, ("mz", "px")))
    out_specs = (P(None, ("px", "mz")), P(None, ("mz", "px")), P(("px", "mz")))
    body = functools.partial(per_device, mesh.shape["mz"], mesh.shape["px"])
    return jax.shard_map(body, mesh=mesh, in_specs=in_specs, out_specs=out_specs, check_vma=False)
```

time: 319 us -> 120 us (0.38)
  blocking collectives: 220 us -> 0 us
  matrix products: 49.4 us -> 0 us
  starting transfers between devices: 0.25 us -> 44.4 us
  waiting for transfers between devices: 29 us -> 51.6 us
  Pallas kernels: 0 us -> 19.6 us
  between operations: 15 us -> 0.95 us
    psum x6 -> x0, blocking collectives: 125 us -> none  [the longest x3 67.3 us: loading_gram(): return lax.psum(matmul(w_block, w_block.T), 'px')]
    all_gather x7 -> x0, blocking collectives: 86.5 us -> none  [the longest x4 55.3 us: rows_of(): return lax.all_gather(w_piece, 'mz', axis=1, tiled=True)]
    ppermute x0 -> x52, waiting for transfers between devices: none -> 51.6 us  [the longest x49 50.4 us: swap(): return lax.ppermute(value, axis, [(i, i ^ mask) for i in range(size)])]
    ppermute x0 -> x52, starting transfers between devices: none -> 44.4 us  [the longest x49 38.3 us: swap(): return lax.ppermute(value, axis, [(i, i ^ mask) for i in range(size)])]
    dot_general x16 -> x0, matrix products: 30.5 us -> none  [matmul(): jnp.dot(left, right, preferred_element_type=jnp.float32, precision=lax.Pr...]
    reduce_scatter x3 -> x0, waiting for transfers between devices: 28.7 us -> none  [per_device(): lax.psum_scatter(matmul(w_block, spectra), 'px', scatter_dimension=1, til...]
    pallas_call x0 -> x25, Pallas kernels: none -> 19.6 us  [the longest x3 6.59 us: final_gather_call(): pl.pallas_call(functools.partial(final_gather_kernel, relatives, groups,...]
    unnamed x3 -> x0, matrix products: 18.9 us -> none
  transfers between devices with their start and end apart: 6 -> 52, of which waited for: 5 -> 26; matrix products, arithmetic and copies ran while one was open for 1% -> 0% of each run, Pallas kernels for 0% -> 9%
where the time goes in v1:
time: 120 us
  waiting for transfers between devices  51.6 us (43%)
  starting transfers between devices  44.4 us (37%)
  Pallas kernels  19.6 us (16%)
  local copies, waits for them, and re-layouts  3.24 us (3%)
    ppermute x49, waiting for transfers between devices, swap(): return lax.ppermute(value, axis, [(i, i ^ mask) for i in range(size)])  50.4 us
    ppermute x49, starting transfers between devices, swap(): return lax.ppermute(value, axis, [(i, i ^ mask) for i in range(size)])  38.3 us
    pallas_call x3, Pallas kernels, final_gather_call(): pl.pallas_call(functools.partial(final_gather_kernel, relatives, groups,...  6.59 us
    ppermute x3, starting transfers between devices, fast_device(): lax.ppermute(w_piece, 'mz', [(i, (i - k) % groups) for i in range(groups)])  6.16 us
    pallas_call x6, Pallas kernels, gather_call(): pl.pallas_call(functools.partial(gather_kernel, relatives, before is not...  4.65 us
    pallas_call x6, Pallas kernels, scatter_call(): pl.pallas_call(functools.partial(scatter_kernel, relatives, width), in_sp...  3.38 us
    unnamed x12, local copies, waits for them, and re-layouts  3.24 us
  transfers between devices with their start and end apart: 52, of which 26 were waited for; matrix products, arithmetic and copies ran while one was open for 0% of the time, Pallas kernels for 9%

profile of v1, /device:TPU:0, one launch (start us, length us, event | category | flops | bytes accessed | tf_op | source)
XLA Modules:
  0.0 119.8 jit_solution(14667430570724466008)
XLA Ops:
  0.6 4.1 %collective-permute-start.1 = (f32[48,96]{1,0:T(8,128)}, f32[48,96]{1,0:T(8,128)S(1)}, u32[]{:S(2)}, u32[]{:S(2)}) collective-permute-start(f32[48,96]{1,0:T(8,128)} %refs_0_.1), channel_id=1, source_target_pairs={{0,16},{8,24},{16,0},{24,8},{1,17},{9,25},{17,1},{25,9},{2,18},{10... | collective-permute-start | bytes 55304 | tf_op jit(solution)/shard_map/ppermute | solution.py:364
  6.8 2.3 %copy-done = f32[384,3072]{1,0:T(8,128)S(1)} copy-done((f32[384,3072]{1,0:T(8,128)S(1)}, f32[384,3072]{1,0:T(8,128)}, u32[]{:S(2)}) %copy-start) | copy-done | bytes 4718616
  13.3 2.6 %collective-permute-start.3 = (f32[56,384]{1,0:T(8,128)S(1)}, f32[56,384]{1,0:T(8,128)S(1)}, u32[]{:S(2)}, u32[]{:S(2)}) collective-permute-start(f32[56,384]{1,0:T(8,128)S(1)} %get-tuple-element.43), channel_id=1, source_target_pairs={{0,7},{1,6},{2,5},{3,4},{4,3},{5,2},{6,1},{7,0},{8,15},{9,14},{10,... | collective-permute-start | bytes 258056 | tf_op jit(solution)/shard_map/ppermute | solution.py:354
  23.1 1.9 %collective-permute-done.6.refs_4_ = f32[56,384]{1,0:T(8,128)S(1)} collective-permute-done((f32[56,384]{1,0:T(8,128)S(1)}, f32[56,384]{1,0:T(8,128)S(1)}, u32[]{:S(2)}, u32[]{:S(2)}) %collective-permute-start.6) | collective-permute-done | bytes 86048 | tf_op jit(solution)/shard_map/ppermute | solution.py:354
  25.3 2.2 %collective-permute-start.14 = (f32[48,384]{1,0:T(8,128)S(1)}, f32[48,384]{1,0:T(8,128)S(1)}, u32[]{:S(2)}, u32[]{:S(2)}) collective-permute-start(f32[48,384]{1,0:T(8,128)S(1)} %update.5.refs_0_.factor_ref), channel_id=1, source_target_pairs={{0,6},{1,7},{2,4},{3,5},{4,2},{5,3},{6,0},{7,1},{8,14},{9,15},{10,... | collective-permute-start | bytes 221192 | tf_op jit(solution)/shard_map/ppermute | solution.py:354
  28.8 1.8 %collective-permute-done.14.refs_2_ = f32[48,384]{1,0:T(8,128)S(1)} collective-permute-done((f32[48,384]{1,0:T(8,128)S(1)}, f32[48,384]{1,0:T(8,128)S(1)}, u32[]{:S(2)}, u32[]{:S(2)}) %collective-permute-start.14) | collective-permute-done | bytes 73760 | tf_op jit(solution)/shard_map/ppermute | solution.py:354
  35.5 4.3 %collective-permute-done.17.right_ref = f32[56,384]{1,0:T(8,128)S(1)} collective-permute-done((f32[56,384]{1,0:T(8,128)S(1)}, f32[56,384]{1,0:T(8,128)S(1)}, u32[]{:S(2)}, u32[]{:S(2)}) %collective-permute-start.17) | collective-permute-done | bytes 86048 | tf_op jit(solution)/shard_map/ppermute | solution.py:354
  40.6 5.6 %collective-permute-done.18.refs_1_ = f32[56,384]{1,0:T(8,128)S(1)} collective-permute-done((f32[56,384]{1,0:T(8,128)S(1)}, f32[56,384]{1,0:T(8,128)S(1)}, u32[]{:S(2)}, u32[]{:S(2)}) %collective-permute-start.18) | collective-permute-done | bytes 86048 | tf_op jit(solution)/shard_map/ppermute | solution.py:354
  47.7 1.7 %collective-permute-start.19 = (f32[56,384]{1,0:T(8,128)S(1)}, f32[56,384]{1,0:T(8,128)S(1)}, u32[]{:S(2)}, u32[]{:S(2)}) collective-permute-start(f32[56,384]{1,0:T(8,128)S(1)} %get-tuple-element.51), channel_id=1, source_target_pairs={{0,7},{1,6},{2,5},{3,4},{4,3},{5,2},{6,1},{7,0},{8,15},{9,14},{10,... | collective-permute-start | bytes 258056 | tf_op jit(solution)/shard_map/ppermute | solution.py:354
  55.4 1.7 %collective-permute-done.21.refs_3_ = f32[56,384]{1,0:T(8,128)S(1)} collective-permute-done((f32[56,384]{1,0:T(8,128)S(1)}, f32[56,384]{1,0:T(8,128)S(1)}, u32[]{:S(2)}, u32[]{:S(2)}) %collective-permute-start.21) | collective-permute-done | bytes 86048 | tf_op jit(solution)/shard_map/ppermute | solution.py:354
  57.1 1.9 %collective-permute-done.22.refs_4_ = f32[56,384]{1,0:T(8,128)S(1)} collective-permute-done((f32[56,384]{1,0:T(8,128)S(1)}, f32[56,384]{1,0:T(8,128)S(1)}, u32[]{:S(2)}, u32[]{:S(2)}) %collective-permute-start.22) | collective-permute-done | bytes 86048 | tf_op jit(solution)/shard_map/ppermute | solution.py:354
  63.2 2.1 %collective-permute-done.30.refs_2_ = f32[48,384]{1,0:T(8,128)S(1)} collective-permute-done((f32[48,384]{1,0:T(8,128)S(1)}, f32[48,384]{1,0:T(8,128)S(1)}, u32[]{:S(2)}, u32[]{:S(2)}) %collective-permute-start.30) | collective-permute-done | bytes 73760 | tf_op jit(solution)/shard_map/ppermute | solution.py:354
  69.2 4.6 %collective-permute-done.33.right_ref = f32[56,384]{1,0:T(8,128)S(1)} collective-permute-done((f32[56,384]{1,0:T(8,128)S(1)}, f32[56,384]{1,0:T(8,128)S(1)}, u32[]{:S(2)}, u32[]{:S(2)}) %collective-permute-start.33) | collective-permute-done | bytes 86048 | tf_op jit(solution)/shard_map/ppermute | solution.py:354
  74.8 5.6 %collective-permute-done.34.refs_1_ = f32[56,384]{1,0:T(8,128)S(1)} collective-permute-done((f32[56,384]{1,0:T(8,128)S(1)}, f32[56,384]{1,0:T(8,128)S(1)}, u32[]{:S(2)}, u32[]{:S(2)}) %collective-permute-start.34) | collective-permute-done | bytes 86048 | tf_op jit(solution)/shard_map/ppermute | solution.py:354
  81.9 2.5 %collective-permute-start.35 = (f32[56,384]{1,0:T(8,128)S(1)}, f32[56,384]{1,0:T(8,128)S(1)}, u32[]{:S(2)}, u32[]{:S(2)}) collective-permute-start(f32[56,384]{1,0:T(8,128)S(1)} %get-tuple-element.59), channel_id=1, source_target_pairs={{0,7},{1,6},{2,5},{3,4},{4,3},{5,2},{6,1},{7,0},{8,15},{9,14},{10,... | collective-permute-start | bytes 258056 | tf_op jit(solution)/shard_map/ppermute | solution.py:354
  89.8 1.7 %collective-permute-done.37.refs_3_ = f32[56,384]{1,0:T(8,128)S(1)} collective-permute-done((f32[56,384]{1,0:T(8,128)S(1)}, f32[56,384]{1,0:T(8,128)S(1)}, u32[]{:S(2)}, u32[]{:S(2)}) %collective-permute-start.37) | collective-permute-done | bytes 86048 | tf_op jit(solution)/shard_map/ppermute | solution.py:354
  91.6 1.8 %collective-permute-done.38.refs_4_ = f32[56,384]{1,0:T(8,128)S(1)} collective-permute-done((f32[56,384]{1,0:T(8,128)S(1)}, f32[56,384]{1,0:T(8,128)S(1)}, u32[]{:S(2)}, u32[]{:S(2)}) %collective-permute-start.38) | collective-permute-done | bytes 86048 | tf_op jit(solution)/shard_map/ppermute | solution.py:354
  94.3 2.1 %collective-permute-start.46 = (f32[48,384]{1,0:T(8,128)}, f32[48,384]{1,0:T(8,128)S(1)}, u32[]{:S(2)}, u32[]{:S(2)}) collective-permute-start(f32[48,384]{1,0:T(8,128)} %update.9.refs_0_), channel_id=1, source_target_pairs={{0,6},{1,7},{2,4},{3,5},{4,2},{5,3},{6,0},{7,1},{8,14},{9,15},{10,... | collective-permute-start | bytes 221192 | tf_op jit(solution)/shard_map/ppermute | solution.py:354
  97.8 2.0 %collective-permute-done.46.refs_2_ = f32[48,384]{1,0:T(8,128)S(1)} collective-permute-done((f32[48,384]{1,0:T(8,128)}, f32[48,384]{1,0:T(8,128)S(1)}, u32[]{:S(2)}, u32[]{:S(2)}) %collective-permute-start.46) | collective-permute-done | bytes 73760 | tf_op jit(solution)/shard_map/ppermute | solution.py:354
  102.8 1.9 %final_products.3 = (f32[384,128]{1,0:T(8,128)S(1)}, f32[48,48]{1,0:T(8,128)S(1)}) custom-call(f32[384,3072]{1,0:T(8,128)S(1)} %bitcast.2, f32[48,384]{1,0:T(8,128)S(1)} %update.8.w_ref, f32[48,384]{1,0:T(8,128)S(1)} %copy-done.1, f32[48,384]{1,0:T(8,128)S(1)} %collective-permute-done.48.refs_1_), custom_call_target="tpu_custom_call" | custom-call | flops 339738624 | bytes 2359296 | tf_op jit(solution)/shard_map/final_products/pallas_call | solution.py:290
  104.7 2.3 %final_products.4 = (f32[384,128]{1,0:T(8,128)S(1)}, f32[48,48]{1,0:T(8,128)S(1)}) custom-call(f32[384,3072]{1,0:T(8,128)S(1)} %bitcast.2, f32[48,384]{1,0:T(8,128)S(1)} %update.8.w_ref, f32[48,384]{1,0:T(8,128)S(1)} %collective-permute-done.42.refs_0_, f32[48,384]{1,0:T(8,128)S(1)} %collective-permute-done.44.refs_1_, ...), custom_call_target="tpu_custom_call" | custom-call | flops 509607936 | bytes 3538944 | tf_op jit(solution)/shard_map/final_products/pallas_call | solution.py:290
  107.0 2.4 %final_products.5 = (f32[144,128]{1,0:T(8,128)S(1)}, f32[144,128]{1,0:T(8,128)S(1)}, f32[144,128]{1,0:T(8,128)S(1)}, f32[144,128]{1,0:T(8,128)S(1)}, f32[96,48]{1,0:T(8,128)S(1)}) custom-call(f32[384,3072]{1,0:T(8,128)S(1)} %bitcast.2, f32[48,384]{1,0:T(8,128)S(1)} %update.8.w_ref, f32[48,384]{1,0:T(8,128)S(1)} %collective-permute-done.43.refs_0_, ...), custom_call_target="tpu_custom_call" | custom-call | flops 509607936 | bytes 3538944 | tf_op jit(solution)/shard_map/final_products/pallas_call | solution.py:290
  109.5 2.7 %collective-permute-start.50 = (f32[144,128]{1,0:T(8,128)S(1)}, f32[144,128]{1,0:T(8,128)S(1)}, u32[]{:S(2)}, u32[]{:S(2)}) collective-permute-start(f32[144,128]{1,0:T(8,128)S(1)} %get-tuple-element.73), channel_id=1, source_target_pairs={{0,16},{8,24},{16,0},{24,8},{1,17},{9,25},{17,1},{25,9},{2,18},{10... | collective-permute-start | bytes 221192 | tf_op jit(solution)/shard_map/ppermute | solution.py:354
  114.9 3.7 %collective-permute-done.50.refs_2_ = f32[144,128]{1,0:T(8,128)S(1)} collective-permute-done((f32[144,128]{1,0:T(8,128)S(1)}, f32[144,128]{1,0:T(8,128)S(1)}, u32[]{:S(2)}, u32[]{:S(2)}) %collective-permute-start.50) | collective-permute-done | bytes 73760 | tf_op jit(solution)/shard_map/ppermute | solution.py:354
  (118 shorter events, 53.1 us)
Async XLA Ops:
  0.6 10.1 %collective-permute-start.1 = (f32[48,96]{1,0:T(8,128)}, f32[48,96]{1,0:T(8,128)S(1)}, u32[]{:S(2)}, u32[]{:S(2)}) collective-permute-start(f32[48,96]{1,0:T(8,128)} %refs_0_.1), channel_id=1, source_target_pairs={{0,16},{8,24},{16,0},{24,8},{1,17},{9,25},{17,1},{25,9},{2,18},{10... | collective-permute-start | bytes 55304 | tf_op jit(solution)/shard_map/ppermute | solution.py:364
  4.8 6.0 %collective-permute-start = (f32[48,96]{1,0:T(8,128)}, f32[48,96]{1,0:T(8,128)S(1)}, u32[]{:S(2)}, u32[]{:S(2)}) collective-permute-start(f32[48,96]{1,0:T(8,128)} %refs_0_.1), channel_id=1, source_target_pairs={{0,24},{8,0},{16,8},{24,16},{1,25},{9,1},{17,9},{25,17},{2,26},{10... | collective-permute-start | bytes 55304 | tf_op jit(solution)/shard_map/ppermute | solution.py:364
  6.1 5.8 %collective-permute-start.2 = (f32[48,96]{1,0:T(8,128)}, f32[48,96]{1,0:T(8,128)S(1)}, u32[]{:S(2)}, u32[]{:S(2)}) collective-permute-start(f32[48,96]{1,0:T(8,128)} %refs_0_.1), channel_id=1, source_target_pairs={{0,8},{8,16},{16,24},{24,0},{1,9},{9,17},{17,25},{25,1},{2,10},{10... | collective-permute-start | bytes 55304 | tf_op jit(solution)/shard_map/ppermute | solution.py:364
  13.3 6.1 %collective-permute-start.3 = (f32[56,384]{1,0:T(8,128)S(1)}, f32[56,384]{1,0:T(8,128)S(1)}, u32[]{:S(2)}, u32[]{:S(2)}) collective-permute-start(f32[56,384]{1,0:T(8,128)S(1)} %get-tuple-element.43), channel_id=1, source_target_pairs={{0,7},{1,6},{2,5},{3,4},{4,3},{5,2},{6,1},{7,0},{8,15},{9,14},{10,... | collective-permute-start | bytes 258056 | tf_op jit(solution)/shard_map/ppermute | solution.py:354
  16.4 6.6 %collective-permute-start.5 = (f32[56,384]{1,0:T(8,128)S(1)}, f32[56,384]{1,0:T(8,128)S(1)}, u32[]{:S(2)}, u32[]{:S(2)}) collective-permute-start(f32[56,384]{1,0:T(8,128)S(1)} %get-tuple-element.45), channel_id=1, source_target_pairs={{0,5},{1,4},{2,7},{3,6},{4,1},{5,0},{6,3},{7,2},{8,13},{9,12},{10,... | collective-permute-start | bytes 258056 | tf_op jit(solution)/shard_map/ppermute | solution.py:354
  17.3 7.7 %collective-permute-start.6 = (f32[56,384]{1,0:T(8,128)S(1)}, f32[56,384]{1,0:T(8,128)S(1)}, u32[]{:S(2)}, u32[]{:S(2)}) collective-permute-start(f32[56,384]{1,0:T(8,128)S(1)} %get-tuple-element.46), channel_id=1, source_target_pairs={{0,4},{1,5},{2,6},{3,7},{4,0},{5,1},{6,2},{7,3},{8,12},{9,13},{10,... | collective-permute-start | bytes 258056 | tf_op jit(solution)/shard_map/ppermute | solution.py:354
  18.0 7.0 %collective-permute-start.7 = (f32[56,384]{1,0:T(8,128)S(1)}, f32[56,384]{1,0:T(8,128)S(1)}, u32[]{:S(2)}, u32[]{:S(2)}) collective-permute-start(f32[56,384]{1,0:T(8,128)S(1)} %get-tuple-element.47), channel_id=1, source_target_pairs={{0,3},{1,2},{2,1},{3,0},{4,7},{5,6},{6,5},{7,4},{8,11},{9,10},{10,... | collective-permute-start | bytes 258056 | tf_op jit(solution)/shard_map/ppermute | solution.py:354
  39.8 6.4 %collective-permute-start.18 = (f32[56,384]{1,0:T(8,128)S(1)}, f32[56,384]{1,0:T(8,128)S(1)}, u32[]{:S(2)}, u32[]{:S(2)}) collective-permute-start(f32[56,384]{1,0:T(8,128)S(1)} %add.2.refs_0_), channel_id=1, source_target_pairs={{0,16},{8,24},{16,0},{24,8},{1,17},{9,25},{17,1},{25,9},{2,18},{10... | collective-permute-start | bytes 258056 | tf_op jit(solution)/shard_map/ppermute | solution.py:354
  46.8 5.7 %collective-permute-start.25 = (f32[56,384]{1,0:T(8,128)S(1)}, f32[56,384]{1,0:T(8,128)S(1)}, u32[]{:S(2)}, u32[]{:S(2)}) collective-permute-start(f32[56,384]{1,0:T(8,128)S(1)} %get-tuple-element.57), channel_id=1, source_target_pairs={{0,1},{1,0},{2,3},{3,2},{4,5},{5,4},{6,7},{7,6},{8,9},{9,8},{10,11... | collective-permute-start | bytes 258056 | tf_op jit(solution)/shard_map/ppermute | solution.py:354
  49.4 6.0 %collective-permute-start.20 = (f32[56,384]{1,0:T(8,128)S(1)}, f32[56,384]{1,0:T(8,128)S(1)}, u32[]{:S(2)}, u32[]{:S(2)}) collective-permute-start(f32[56,384]{1,0:T(8,128)S(1)} %get-tuple-element.52), channel_id=1, source_target_pairs={{0,6},{1,7},{2,4},{3,5},{4,2},{5,3},{6,0},{7,1},{8,14},{9,15},{10,... | collective-permute-start | bytes 258056 | tf_op jit(solution)/shard_map/ppermute | solution.py:354
  50.8 6.4 %collective-permute-start.21 = (f32[56,384]{1,0:T(8,128)S(1)}, f32[56,384]{1,0:T(8,128)S(1)}, u32[]{:S(2)}, u32[]{:S(2)}) collective-permute-start(f32[56,384]{1,0:T(8,128)S(1)} %get-tuple-element.53), channel_id=1, source_target_pairs={{0,5},{1,4},{2,7},{3,6},{4,1},{5,0},{6,3},{7,2},{8,13},{9,12},{10,... | collective-permute-start | bytes 258056 | tf_op jit(solution)/shard_map/ppermute | solution.py:354
  51.9 7.1 %collective-permute-start.22 = (f32[56,384]{1,0:T(8,128)S(1)}, f32[56,384]{1,0:T(8,128)S(1)}, u32[]{:S(2)}, u32[]{:S(2)}) collective-permute-start(f32[56,384]{1,0:T(8,128)S(1)} %get-tuple-element.54), channel_id=1, source_target_pairs={{0,4},{1,5},{2,6},{3,7},{4,0},{5,1},{6,2},{7,3},{8,12},{9,13},{10,... | collective-permute-start | bytes 258056 | tf_op jit(solution)/shard_map/ppermute | solution.py:354
  52.5 6.5 %collective-permute-start.23 = (f32[56,384]{1,0:T(8,128)S(1)}, f32[56,384]{1,0:T(8,128)S(1)}, u32[]{:S(2)}, u32[]{:S(2)}) collective-permute-start(f32[56,384]{1,0:T(8,128)S(1)} %get-tuple-element.55), channel_id=1, source_target_pairs={{0,3},{1,2},{2,1},{3,0},{4,7},{5,6},{6,5},{7,4},{8,11},{9,10},{10,... | collective-permute-start | bytes 258056 | tf_op jit(solution)/shard_map/ppermute | solution.py:354
  53.1 6.3 %collective-permute-start.24 = (f32[56,384]{1,0:T(8,128)S(1)}, f32[56,384]{1,0:T(8,128)S(1)}, u32[]{:S(2)}, u32[]{:S(2)}) collective-permute-start(f32[56,384]{1,0:T(8,128)S(1)} %get-tuple-element.56), channel_id=1, source_target_pairs={{0,2},{1,3},{2,0},{3,1},{4,6},{5,7},{6,4},{7,5},{8,10},{9,11},{10,... | collective-permute-start | bytes 258056 | tf_op jit(solution)/shard_map/ppermute | solution.py:354
  59.6 5.7 %collective-permute-start.30 = (f32[48,384]{1,0:T(8,128)S(1)}, f32[48,384]{1,0:T(8,128)S(1)}, u32[]{:S(2)}, u32[]{:S(2)}) collective-permute-start(f32[48,384]{1,0:T(8,128)S(1)} %update.7.refs_0_.factor_ref), channel_id=1, source_target_pairs={{0,6},{1,7},{2,4},{3,5},{4,2},{5,3},{6,0},{7,1},{8,14},{9,15},{10,... | collective-permute-start | bytes 221192 | tf_op jit(solution)/shard_map/ppermute | solution.py:354
  73.8 6.6 %collective-permute-start.34 = (f32[56,384]{1,0:T(8,128)S(1)}, f32[56,384]{1,0:T(8,128)S(1)}, u32[]{:S(2)}, u32[]{:S(2)}) collective-permute-start(f32[56,384]{1,0:T(8,128)S(1)} %add.3.refs_0_), channel_id=1, source_target_pairs={{0,16},{8,24},{16,0},{24,8},{1,17},{9,25},{17,1},{25,9},{2,18},{10... | collective-permute-start | bytes 258056 | tf_op jit(solution)/shard_map/ppermute | solution.py:354
  81.9 5.8 %collective-permute-start.35 = (f32[56,384]{1,0:T(8,128)S(1)}, f32[56,384]{1,0:T(8,128)S(1)}, u32[]{:S(2)}, u32[]{:S(2)}) collective-permute-start(f32[56,384]{1,0:T(8,128)S(1)} %get-tuple-element.59), channel_id=1, source_target_pairs={{0,7},{1,6},{2,5},{3,4},{4,3},{5,2},{6,1},{7,0},{8,15},{9,14},{10,... | collective-permute-start | bytes 258056 | tf_op jit(solution)/shard_map/ppermute | solution.py:354
  85.0 6.6 %collective-permute-start.37 = (f32[56,384]{1,0:T(8,128)S(1)}, f32[56,384]{1,0:T(8,128)S(1)}, u32[]{:S(2)}, u32[]{:S(2)}) collective-permute-start(f32[56,384]{1,0:T(8,128)S(1)} %get-tuple-element.61), channel_id=1, source_target_pairs={{0,5},{1,4},{2,7},{3,6},{4,1},{5,0},{6,3},{7,2},{8,13},{9,12},{10,... | collective-permute-start | bytes 258056 | tf_op jit(solution)/shard_map/ppermute | solution.py:354
  85.6 7.8 %collective-permute-start.38 = (f32[56,384]{1,0:T(8,128)S(1)}, f32[56,384]{1,0:T(8,128)S(1)}, u32[]{:S(2)}, u32[]{:S(2)}) collective-permute-start(f32[56,384]{1,0:T(8,128)S(1)} %get-tuple-element.62), channel_id=1, source_target_pairs={{0,4},{1,5},{2,6},{3,7},{4,0},{5,1},{6,2},{7,3},{8,12},{9,13},{10,... | collective-permute-start | bytes 258056 | tf_op jit(solution)/shard_map/ppermute | solution.py:354
  86.4 7.0 %collective-permute-start.39 = (f32[56,384]{1,0:T(8,128)S(1)}, f32[56,384]{1,0:T(8,128)S(1)}, u32[]{:S(2)}, u32[]{:S(2)}) collective-permute-start(f32[56,384]{1,0:T(8,128)S(1)} %get-tuple-element.63), channel_id=1, source_target_pairs={{0,3},{1,2},{2,1},{3,0},{4,7},{5,6},{6,5},{7,4},{8,11},{9,10},{10,... | collective-permute-start | bytes 258056 | tf_op jit(solution)/shard_map/ppermute | solution.py:354
  87.7 5.7 %collective-permute-start.40 = (f32[56,384]{1,0:T(8,128)S(1)}, f32[56,384]{1,0:T(8,128)S(1)}, u32[]{:S(2)}, u32[]{:S(2)}) collective-permute-start(f32[56,384]{1,0:T(8,128)S(1)} %get-tuple-element.64), channel_id=1, source_target_pairs={{0,2},{1,3},{2,0},{3,1},{4,6},{5,7},{6,4},{7,5},{8,10},{9,11},{10,... | collective-permute-start | bytes 258056 | tf_op jit(solution)/shard_map/ppermute | solution.py:354
  99.9 7.1 %collective-permute-start.47 = (f32[48,384]{1,0:T(8,128)S(1)}, f32[48,384]{1,0:T(8,128)S(1)}, u32[]{:S(2)}, u32[]{:S(2)}) collective-permute-start(f32[48,384]{1,0:T(8,128)S(1)} %collective-permute-done.46.refs_2_), channel_id=1, source_target_pairs={{0,1},{1,0},{2,3},{3,2},{4,5},{5,4},{6,7},{7,6},{8,9},{9,8},{10,11... | collective-permute-start | bytes 221192 | tf_op jit(solution)/shard_map/ppermute | solution.py:354
  109.5 9.1 %collective-permute-start.50 = (f32[144,128]{1,0:T(8,128)S(1)}, f32[144,128]{1,0:T(8,128)S(1)}, u32[]{:S(2)}, u32[]{:S(2)}) collective-permute-start(f32[144,128]{1,0:T(8,128)S(1)} %get-tuple-element.73), channel_id=1, source_target_pairs={{0,16},{8,24},{16,0},{24,8},{1,17},{9,25},{17,1},{25,9},{2,18},{10... | collective-permute-start | bytes 221192 | tf_op jit(solution)/shard_map/ppermute | solution.py:354
  112.2 6.5 %collective-permute-start.51 = (f32[144,128]{1,0:T(8,128)S(1)}, f32[144,128]{1,0:T(8,128)S(1)}, u32[]{:S(2)}, u32[]{:S(2)}) collective-permute-start(f32[144,128]{1,0:T(8,128)S(1)} %get-tuple-element.74), channel_id=1, source_target_pairs={{0,24},{8,16},{16,8},{24,0},{1,25},{9,17},{17,9},{25,1},{2,26},{10... | collective-permute-start | bytes 221192 | tf_op jit(solution)/shard_map/ppermute | solution.py:354
  (34 other events, 197.0 us)

commit v2 on v1

--- a/solution.py
+++ b/solution.py
@@ -79,8 +79,8 @@
     )
 
 
-def params(**more):
-    return pltpu.CompilerParams(vmem_limit_bytes=32 << 20, **more)
+def params(mib=32):
+    return pltpu.CompilerParams(vmem_limit_bytes=mib << 20)
 
 
 def vmem(count):
@@ -91,22 +91,34 @@
     return pl.CostEstimate(flops=int(flops), bytes_accessed=int(moved), transcendentals=0)
 
 
-def split_kernel(s_ref, high_ref, low_ref):
-    high_ref[...], low_ref[...] = split(s_ref[...])
+def split_kernel(step, s_ref, copy_ref, high_ref, low_ref, sems):
+    columns = s_ref.shape[1]
+    copies = []
+    for index in range(columns // step):
+        here = pl.ds(index * step, step)
+        copies.append(pltpu.make_async_copy(s_ref.at[:, here], copy_ref.at[:, here], sems.at[index]))
+        copies[-1].start()
+    for index, copy in enumerate(copies):
+        here = pl.ds(index * step, step)
+        copy.wait()
+        high_ref[:, here], low_ref[:, here] = split(copy_ref[:, here])
 
 
 def split_call(spectra):
     rows, columns = spectra.shape
-    step = min(columns, 512)
-    spec = pl.BlockSpec((rows, step), lambda i: (0, i))
-    return pl.pallas_call(
-        split_kernel,
-        grid=(columns // step,),
-        in_specs=[spec],
-        out_specs=[spec, spec],
-        out_shape=[jax.ShapeDtypeStruct((rows, columns), BF16)] * 2,
-        compiler_params=params(),
-        cost_estimate=cost(4 * rows * columns, 8 * rows * columns),
+    step = columns // 8 if columns % (8 * LANES) == 0 else columns
+    return pl.pallas_call(
+        functools.partial(split_kernel, step),
+        in_specs=[pl.BlockSpec(memory_space=pltpu.HBM)],
+        out_specs=vmem(3),
+        out_shape=[
+            jax.ShapeDtypeStruct((rows, columns), F32),
+            jax.ShapeDtypeStruct((rows, columns), BF16),
+            jax.ShapeDtypeStruct((rows, columns), BF16),
+        ],
+        scratch_shapes=[pltpu.SemaphoreType.DMA((columns // step,))],
+        compiler_params=params(44),
+        cost_estimate=cost(4 * rows * columns, 12 * rows * columns),
         name="split_spectra",
     )(spectra)
 
@@ -116,15 +128,15 @@
     return pl.ds(pl.multiple_of(block * width, LANES), width)
 
 
-def scatter_kernel(relatives, width, w_ref, high_ref, low_ref, *outs):
+def scatter_kernel(relatives, width, w_ref, high_ref, low_ref, out):
     w = w_ref[...]
     rank = w.shape[0]
     stack, w_high = stacked(w)
     gram = product(stack, w_high, *split(w), NT)
-    for relative, out in zip(relatives, outs):
+    for index, relative in enumerate(relatives):
         here = bins_of(relative, width)
-        out[:rank, :] = product(stack, w_high, high_ref[:, here], low_ref[:, here], NN)
-        pack_gram(out, gram)
+        out[index, :rank, :] = product(stack, w_high, high_ref[:, here], low_ref[:, here], NN)
+        pack_gram(out.at[index], gram)
 
 
 def scatter_call(relatives, width, w_block, high, low):
@@ -133,29 +145,49 @@
     return pl.pallas_call(
         functools.partial(scatter_kernel, relatives, width),
         in_specs=vmem(3),
-        out_specs=vmem(count),
-        out_shape=[jax.ShapeDtypeStruct((rank + SUBLANES, width), F32)] * count,
+        out_specs=pl.BlockSpec(memory_space=pltpu.VMEM),
+        out_shape=jax.ShapeDtypeStruct((count, rank + SUBLANES, width), F32),
         compiler_params=params(),
         cost_estimate=cost(6 * rank * pixels * width * count, 4 * pixels * width * count),
         name="loadings_times_spectra",
     )(w_block, high, low)
 
 
-def update_kernel(factor_ref, *refs):
+def pair_kernel(own_ref, other_ref, *outs):
+    for index, out in enumerate(outs):
+        out[...] = own_ref[index + 1] + other_ref[index + 1]
+
+
+def pair_call(own, other):
+    count = own.shape[0] - 1
+    return pl.pallas_call(
+        pair_kernel,
+        in_specs=vmem(2),
+        out_specs=vmem(count),
+        out_shape=[jax.ShapeDtypeStruct(own.shape[1:], F32)] * count,
+        compiler_params=params(),
+        cost_estimate=cost(own.size, 12 * own.size),
+        name="pair_sums",
+    )(own, other)
+
+
+def update_kernel(stacks, factor_ref, *refs):
     parts, out = refs[:-1], refs[-1]
     factor = factor_ref[...]
     rank = factor.shape[0]
-    total = parts[0][...]
-    for part in parts[1:]:
-        total = total + part[...]
+    total = None
+    for index, part in enumerate(parts):
+        value = part[0] if index < stacks else part[...]
+        total = value if total is None else total + value
     gram = unpack_gram(total[rank:], rank)
     out[...] = factor * total[:rank] / exact(gram, factor, NN)
 
 
-def update_call(factor, *parts):
+def update_call(factor, stacks, parts):
     rank, width = factor.shape
-    return pl.pallas_call(
-        update_kernel,
+    parts = (*stacks, *parts)
+    return pl.pallas_call(
+        functools.partial(update_kernel, len(stacks)),
         in_specs=vmem(1 + len(parts)),
         out_specs=pl.BlockSpec(memory_space=pltpu.VMEM),
         out_shape=jax.ShapeDtypeStruct((rank, width), F32),
@@ -218,7 +250,10 @@
 
 def final_gather_kernel(relatives, groups, first, last, s_ref, w_ref, *refs):
     pieces, refs = refs[: len(relatives)], refs[len(relatives) :]
-    if not first:
+    if first:
+        kept_ref = refs[-1]
+        kept_ref[...] = pieces[0][...]
+    else:
         before_ref, gram_before_ref, refs = refs[0], refs[1], refs[2:]
     rank, width = pieces[0].shape
     pixels = w_ref.shape[1]
@@ -227,30 +262,32 @@
     w2 = (w_t - w0.astype(F32) - w1.astype(F32)).astype(BF16)
     left = jnp.concatenate([w0, w0, w1, w1, w0, w2], axis=1)
     lane = lax.broadcasted_iota(jnp.int32, (pixels, LANES), 1)
+    half = LANES // 2
     zeros = functools.partial(jnp.zeros, dtype=BF16)
     total, gram = None, None
     for relative, piece in zip(relatives, pieces):
         h = piece[...]
         h0, h1 = split(h)
         h2 = (h - h0.astype(F32) - h1.astype(F32)).astype(BF16)
-        s = s_ref[:, bins_of(relative, width)]
         right = jnp.concatenate([h0, h1, h0, h1, h2, h0], axis=0)
-        d = s - fast(left, right, NN)
+        d = s_ref[:, bins_of(relative, width)] - fast(left, right, NN)
+        d0, d1 = split(d)
         tail = zeros((LANES - rank, width))
-        tail2 = zeros((LANES - 2 * rank, width))
-        pad = zeros((rank, width))
-        num_high = jnp.concatenate([h0, tail], axis=0)
-        num_both = jnp.concatenate([num_high, h1, tail], axis=0)
-        err_high = jnp.concatenate([pad, h0, tail2], axis=0)
-        err_both = jnp.concatenate([err_high, pad, h1, tail2], axis=0)
-        s0, s1 = split(s)
-        d0, d1 = split(d)
-        both = fast(s0, num_both, NT) + fast(d0, err_both, NT)
-        term = both[:, :LANES] + both[:, LANES:] + fast(s1, num_high, NT) + fast(d1, err_high, NT)
+        high = jnp.concatenate([h0, tail], axis=0)
+        both = fast(d0, jnp.concatenate([high, h1, tail], axis=0), NT)
+        term = both[:, :LANES] + both[:, LANES:] + fast(d1, high, NT)
         squares = jnp.sum(d * d, axis=1, keepdims=True)
-        term = jnp.where(lane == 2 * rank, squares, term)
-        stack, h_high = stacked(h)
-        square = product(stack, h_high, h0, h1, NT)
+        term = jnp.where(lane == rank, squares, term)
+        front = zeros((half, width))
+        back = zeros((half - rank, width))
+        stack = jnp.concatenate([h0, h1], axis=0)
+        square = product(
+            stack,
+            h0,
+            jnp.concatenate([front, h0, back], axis=0),
+            jnp.concatenate([front, h1, back], axis=0),
+            NT,
+        )
         total = term if total is None else total + term
         gram = square if gram is None else gram + square
     if not first:
@@ -267,9 +304,8 @@
     me = lax.axis_index("mz")
     for relative, out in enumerate(outs):
         group = jnp.bitwise_xor(me, relative)
-        out[:rows, :] = scratch[pl.ds(pl.multiple_of(group * rows, SUBLANES), rows), :]
-        out[rows:, :] = jnp.zeros((rank, LANES), F32)
-        out[rows:, :rank] = gram
+        out[...] = scratch[pl.ds(pl.multiple_of(group * rows, SUBLANES), rows), :]
+        out[:rank, :] += gram
     own_ref[...] = w_scratch[pl.ds(pl.multiple_of(me * rows, SUBLANES), rows), :]
 
 
@@ -279,15 +315,17 @@
     rows = pixels // groups
     count = len(relatives)
     first = before is None
-    extra = () if first else tuple(before)
+    extra = () if first else tuple(before[:2])
     if last:
-        shapes = [jax.ShapeDtypeStruct((rows + rank, LANES), F32)] * groups
+        shapes = [jax.ShapeDtypeStruct((rows, LANES), F32)] * groups
         shapes.append(jax.ShapeDtypeStruct((rows, rank), F32))
         scratch = [pltpu.VMEM((pixels, LANES), F32), pltpu.VMEM((pixels, rank), F32)]
     else:
-        shapes = [jax.ShapeDtypeStruct((pixels, LANES), F32), jax.ShapeDtypeStruct((rank, rank), F32)]
+        shapes = [jax.ShapeDtypeStruct((pixels, LANES), F32), jax.ShapeDtypeStruct((rank, LANES), F32)]
         scratch = []
-    return pl.pallas_call(
+    if first:
+        shapes.append(jax.ShapeDtypeStruct((rank, width), F32))
+    results = pl.pallas_call(
         functools.partial(final_gather_kernel, relatives, groups, first, last),
         in_specs=vmem(2 + count + len(extra)),
         out_specs=vmem(len(shapes)),
@@ -297,6 +335,8 @@
         cost_estimate=cost(24 * rank * pixels * width * count, 8 * pixels * width * count),
         name="final_products",
     )(spectra, w_block, *pieces, *extra)
+    kept = () if first else (before[-1],)
+    return (*results, *kept)
 
 
 def final_kernel(w_t_ref, *refs):
@@ -306,14 +346,15 @@
     total = parts[0][...]
     for part in parts[1:]:
         total = total + part[...]
-    gram = total[rows:, :rank]
-    num, err = total[:rows, :rank], total[:rows, rank : 2 * rank]
-    new = w_t * num / exact(w_t, gram, NN)
+    gram = total[:rank, LANES // 2 : LANES // 2 + rank]
+    err = total[:, :rank]
+    den = exact(w_t, gram, NN)
+    new = w_t * (err + den) / den
     w_out[...] = new.T
     step = new - w_t
     change = step * (exact(step, gram, NN) - 2.0 * err)
-    pick = (lax.broadcasted_iota(jnp.int32, (SUBLANES, LANES), 1) == 2 * rank).astype(F32)
-    misfit = exact(pick, total[:rows], NT) + exact(jnp.ones((SUBLANES, rank), F32), change, NT)
+    pick = (lax.broadcasted_iota(jnp.int32, (SUBLANES, LANES), 1) == rank).astype(F32)
+    misfit = exact(pick, total, NT) + exact(jnp.ones((SUBLANES, rank), F32), change, NT)
     misfit_out[...] = misfit[:1]
 
 
@@ -354,10 +395,37 @@
     return lax.ppermute(value, axis, [(i, i ^ mask) for i in range(size)])
 
 
+def cross(value, groups, owners, even, odd):
+    pairs = [
+        (g * owners + o, (g ^ (odd if o % 2 else even)) * owners + o)
+        for g in range(groups)
+        for o in range(owners)
+    ]
+    return lax.ppermute(value, ("mz", "px"), pairs)
+
+
+def spread(h_piece, owners, products):
+    evens = list(range(owners - 2, 0, -2))
+    beside = swap(h_piece, "px", owners, 1)
+    mine = [swap(h_piece, "px", owners, r) for r in evens]
+    total = products([0, 1], [h_piece, beside], None, False)
+    theirs, held = [], []
+    for index, (relative, piece) in enumerate(zip(evens, mine)):
+        if index:
+            piece, total = lax.optimization_barrier((piece, total))
+        theirs.append(swap(piece, "px", owners, 1))
+        held.append((relative, piece))
+        if 0 < index < len(evens) - 1:
+            total = products(*zip(*held), total, False)
+            held = []
+    held += [(r + 1, piece) for r, piece in zip(evens[:-1], theirs)]
+    total = products(*zip(*held), total, False)
+    return products([evens[-1] + 1], [theirs[-1]], total, True)
+
+
 def fast_device(groups, owners, spectra, w_piece, h_piece):
     width = h_piece.shape[1]
-    far = [r for r in range(owners - 1, 1, -1)]
-    high, low = split_call(spectra)
+    copy, high, low = split_call(spectra)
     w_block = join_call(
         w_piece,
         *[
@@ -365,34 +433,37 @@
             for k in range(1, groups)
         ],
     )
-    evens = list(range(2, owners, 2))
+    evens = list(range(owners - 2, 0, -2))
+    masks = [1 << bit for bit in range(groups.bit_length() - 1)]
     for iteration in range(ITERS):
-        parts = scatter_call(far, width, w_block, high, low)
-        sent = [swap(part, "px", owners, r) for part, r in zip(parts, far)]
-        near = scatter_call([1, 0], width, w_block, high, low)
-        sent.append(swap(near[0], "px", owners, 1))
-        h_piece = update_call(h_piece, near[1], *sent)
-        beside = swap(h_piece, "px", owners, 1)
-        mine = [swap(h_piece, "px", owners, r) for r in evens]
-        theirs = [swap(piece, "px", owners, 1) for piece in mine]
-        odds = [r + 1 for r in evens]
+        theirs = scatter_call(list(range(1, owners, 2)), width, w_block, high, low)
+        other = swap(theirs, "px", owners, 1)
+        own = scatter_call(list(range(0, owners, 2)), width, w_block, high, low)
+        sums = pair_call(own, other)
+        sent = [swap(sums[r // 2 - 1], "px", owners, r) for r in evens]
+        h_piece = update_call(h_piece, (own, other), sent)
         if iteration + 1 < ITERS:
-            total = gather_call([0, 1], [h_piece, beside], high, low, None)
-            total = gather_call(evens, mine, high, low, total)
-            total = gather_call(odds, theirs, high, low, total)
-            mask = 1
-            while 2 * mask < groups:
-                total = add_call(total, swap(total, "mz", groups, mask))
-                mask *= 2
-            w_block = update_call(w_block, total, swap(total, "mz", groups, mask))
+            total = spread(
+                h_piece,
+                owners,
+                lambda relatives, pieces, before, last: gather_call(relatives, pieces, high, low, before),
+            )
+            for even, odd in zip(masks[:-1], masks[:0:-1]):
+                total = add_call(total, cross(total, groups, owners, even, odd))
+            w_block = update_call(
+                w_block, (), (total, cross(total, groups, owners, masks[-1], masks[0]))
+            )
         else:
-            call = functools.partial(final_gather_call, spectra=spectra, w_block=w_block)
-            total = call([0, 1], groups, [h_piece, beside], before=None, last=False)
-            total = call(evens, groups, mine, before=total, last=False)
-            *parts, w_t = call(odds, groups, theirs, before=total, last=True)
+            parts = spread(
+                h_piece,
+                owners,
+                lambda relatives, pieces, before, last: final_gather_call(
+                    relatives, groups, pieces, copy, w_block, before, last
+                ),
+            )
             sent = [swap(parts[k], "mz", groups, k) for k in range(1, groups)]
-            w_final, misfit = final_call(w_t, parts[0], *sent)
-    return w_final, h_piece, misfit.reshape(-1)
+            w_final, misfit = final_call(parts[groups], parts[0], *sent)
+    return w_final, parts[-1], misfit.reshape(-1)
 
 
 def per_device(groups, owners, spectra, w_piece, h_piece):
@@ -410,7 +481,8 @@
         and w_piece.shape[1] % SUBLANES == 0
         and rank % (2 * SUBLANES) == 0
         and rank // SUBLANES * rank <= min(width, pixels)
-        and 2 * rank < LANES
+        and rank < LANES // 2
+        and rank <= w_piece.shape[1]
     )
     if fits:
         return fast_device(groups, owners, spectra, w_piece, h_piece)

time: 120 us -> 106 us (0.88)
  starting transfers between devices: 44.4 us -> 34.1 us
  local copies, waits for them, and re-layouts: 3.24 us -> 0.01 us
    ppermute x49 -> x36, waiting for transfers between devices: 50.4 us -> 27 us  [swap(): return lax.ppermute(value, axis, [(i, i ^ mask) for i in range(size)])]
    ppermute x0 -> x4, waiting for transfers between devices: none -> 21.6 us  [cross(): return lax.ppermute(value, ('mz', 'px'), pairs)]
    ppermute x49 -> x36, starting transfers between devices: 38.3 us -> 27.7 us  [swap(): return lax.ppermute(value, axis, [(i, i ^ mask) for i in range(size)])]
    unnamed x12 -> x4, local copies, waits for them, and re-layouts: 3.24 us -> 0.01 us
    ppermute x3, waiting for transfers between devices: 1.23 us -> 2.62 us  [fast_device(): lax.ppermute(w_piece, 'mz', [(i, (i - k) % groups) for i in range(groups)])]
    pallas_call x6 -> x8, Pallas kernels: 4.65 us -> 5.07 us  [gather_call(): pl.pallas_call(functools.partial(gather_kernel, relatives, before is not...]
    pallas_call x6 -> x9, Pallas kernels: 3.59 us -> 3.98 us  [the longest x1 2.51 us: split_call(): pl.pallas_call(functools.partial(split_kernel, step), in_specs=[pl.BlockS...]
    pallas_call x3 -> x4, Pallas kernels: 6.59 us -> 6.24 us  [final_gather_call(): pl.pallas_call(functools.partial(final_gather_kernel, relatives, groups,...]
  transfers between devices with their start and end apart: 52 -> 43, of which waited for: 26 -> 25; matrix products, arithmetic and copies ran while one was open for 0% -> 0% of each run, Pallas kernels for 9% -> 13%
where the time goes in v2:
time: 106 us
  waiting for transfers between devices  51.2 us (48%)
  starting transfers between devices  34.1 us (32%)
  Pallas kernels  20.1 us (19%)
    ppermute x36, starting transfers between devices, swap(): return lax.ppermute(value, axis, [(i, i ^ mask) for i in range(size)])  27.7 us
    ppermute x36, waiting for transfers between devices, swap(): return lax.ppermute(value, axis, [(i, i ^ mask) for i in range(size)])  27 us
    ppermute x4, waiting for transfers between devices, cross(): return lax.ppermute(value, ('mz', 'px'), pairs)  21.6 us
    pallas_call x4, Pallas kernels, final_gather_call(): pl.pallas_call(functools.partial(final_gather_kernel, relatives, groups,...  6.24 us
    ppermute x3, starting transfers between devices, fast_device(): lax.ppermute(w_piece, 'mz', [(i, (i - k) % groups) for i in range(groups)])  6.16 us
    pallas_call x8, Pallas kernels, gather_call(): pl.pallas_call(functools.partial(gather_kernel, relatives, before is not...  5.07 us
    pallas_call x6, Pallas kernels, scatter_call(): pl.pallas_call(functools.partial(scatter_kernel, relatives, width), in_sp...  3.36 us
    ppermute x3, waiting for transfers between devices, fast_device(): lax.ppermute(w_piece, 'mz', [(i, (i - k) % groups) for i in range(groups)])  2.62 us
  transfers between devices with their start and end apart: 43, of which 25 were waited for; matrix products, arithmetic and copies ran while one was open for 0% of the time, Pallas kernels for 13%

profile of v2, /device:TPU:0, one launch (start us, length us, event | category | flops | bytes accessed | tf_op | source)
XLA Modules:
  0.0 106.3 jit_solution(991918328702184122)
XLA Ops:
  0.6 4.1 %collective-permute-start.1 = (f32[48,96]{1,0:T(8,128)}, f32[48,96]{1,0:T(8,128)S(1)}, u32[]{:S(2)}, u32[]{:S(2)}) collective-permute-start(f32[48,96]{1,0:T(8,128)} %refs_0_.1), channel_id=1, source_target_pairs={{0,16},{8,24},{16,0},{24,8},{1,17},{9,25},{17,1},{25,9},{2,18},{10... | collective-permute-start | bytes 55304 | tf_op jit(solution)/shard_map/ppermute | solution.py:432
  6.8 2.5 %split_spectra.1 = (f32[384,3072]{1,0:T(8,128)S(1)}, bf16[384,3072]{1,0:T(8,128)(2,1)S(1)}, bf16[384,3072]{1,0:T(8,128)(2,1)S(1)}) custom-call(f32[384,3072]{1,0:T(8,128)} %s_ref.1), custom_call_target="tpu_custom_call" | custom-call | flops 4718592 | bytes 14155776 | tf_op jit(solution)/shard_map/split_spectra/pallas_call | solution.py:110
  9.3 2.6 %collective-permute-done.2.refs_3_ = f32[48,96]{1,0:T(8,128)S(1)} collective-permute-done((f32[48,96]{1,0:T(8,128)}, f32[48,96]{1,0:T(8,128)S(1)}, u32[]{:S(2)}, u32[]{:S(2)}) %collective-permute-start.2) | collective-permute-done | bytes 18464 | tf_op jit(solution)/shard_map/ppermute | solution.py:432
  14.5 2.5 %collective-permute-start.4 = (f32[56,384]{1,0:T(8,128)S(1)}, f32[56,384]{1,0:T(8,128)S(1)}, u32[]{:S(2)}, u32[]{:S(2)}) collective-permute-start(f32[56,384]{1,0:T(8,128)S(1)} %get-tuple-element.48), channel_id=1, source_target_pairs={{0,6},{1,7},{2,4},{3,5},{4,2},{5,3},{6,0},{7,1},{8,14},{9,15},{10,... | collective-permute-start | bytes 258056 | tf_op jit(solution)/shard_map/ppermute | solution.py:395
  18.0 2.0 %collective-permute-done.4.refs_2_ = f32[56,384]{1,0:T(8,128)S(1)} collective-permute-done((f32[56,384]{1,0:T(8,128)S(1)}, f32[56,384]{1,0:T(8,128)S(1)}, u32[]{:S(2)}, u32[]{:S(2)}) %collective-permute-start.4) | collective-permute-done | bytes 86048 | tf_op jit(solution)/shard_map/ppermute | solution.py:395
  20.1 1.8 %collective-permute-done.5.refs_3_ = f32[56,384]{1,0:T(8,128)S(1)} collective-permute-done((f32[56,384]{1,0:T(8,128)S(1)}, f32[56,384]{1,0:T(8,128)S(1)}, u32[]{:S(2)}, u32[]{:S(2)}) %collective-permute-start.5) | collective-permute-done | bytes 86048 | tf_op jit(solution)/shard_map/ppermute | solution.py:395
  22.3 1.6 %collective-permute-start.9 = (f32[48,384]{1,0:T(8,128)S(1)}, f32[48,384]{1,0:T(8,128)S(1)}, u32[]{:S(2)}, u32[]{:S(2)}) collective-permute-start(f32[48,384]{1,0:T(8,128)S(1)} %update.5.refs_0_.factor_ref), channel_id=1, source_target_pairs={{0,4},{1,5},{2,6},{3,7},{4,0},{5,1},{6,2},{7,3},{8,12},{9,13},{10,... | collective-permute-start | bytes 221192 | tf_op jit(solution)/shard_map/ppermute | solution.py:395
  27.5 2.5 %collective-permute-done.8.refs_0_ = f32[48,384]{1,0:T(8,128)S(1)} collective-permute-done((f32[48,384]{1,0:T(8,128)S(1)}, f32[48,384]{1,0:T(8,128)S(1)}, u32[]{:S(2)}, u32[]{:S(2)}) %collective-permute-start.8) | collective-permute-done | bytes 73760 | tf_op jit(solution)/shard_map/ppermute | solution.py:395
  32.5 5.4 %collective-permute-done.14.right_ref = f32[56,384]{1,0:T(8,128)S(1)} collective-permute-done((f32[56,384]{1,0:T(8,128)S(1)}, f32[56,384]{1,0:T(8,128)S(1)}, u32[]{:S(2)}, u32[]{:S(2)}) %collective-permute-start.14) | collective-permute-done | bytes 86048 | tf_op jit(solution)/shard_map/ppermute | solution.py:404
  38.0 5.4 %collective-permute-done.15.refs_1_ = f32[56,384]{1,0:T(8,128)S(1)} collective-permute-done((f32[56,384]{1,0:T(8,128)S(1)}, f32[56,384]{1,0:T(8,128)S(1)}, u32[]{:S(2)}, u32[]{:S(2)}) %collective-permute-start.15) | collective-permute-done | bytes 86048 | tf_op jit(solution)/shard_map/ppermute | solution.py:404
  48.0 1.6 %collective-permute-start.19 = (f32[56,384]{1,0:T(8,128)S(1)}, f32[56,384]{1,0:T(8,128)S(1)}, u32[]{:S(2)}, u32[]{:S(2)}) collective-permute-start(f32[56,384]{1,0:T(8,128)S(1)} %get-tuple-element.57), channel_id=1, source_target_pairs={{0,2},{1,3},{2,0},{3,1},{4,6},{5,7},{6,4},{7,5},{8,10},{9,11},{10,... | collective-permute-start | bytes 258056 | tf_op jit(solution)/shard_map/ppermute | solution.py:395
  49.6 2.4 %collective-permute-done.17.refs_2_ = f32[56,384]{1,0:T(8,128)S(1)} collective-permute-done((f32[56,384]{1,0:T(8,128)S(1)}, f32[56,384]{1,0:T(8,128)S(1)}, u32[]{:S(2)}, u32[]{:S(2)}) %collective-permute-start.17) | collective-permute-done | bytes 86048 | tf_op jit(solution)/shard_map/ppermute | solution.py:395
  58.0 1.8 %collective-permute-done.22.refs_1_ = f32[48,384]{1,0:T(8,128)S(1)} collective-permute-done((f32[48,384]{1,0:T(8,128)S(1)}, f32[48,384]{1,0:T(8,128)S(1)}, u32[]{:S(2)}, u32[]{:S(2)}) %collective-permute-start.22) | collective-permute-done | bytes 73760 | tf_op jit(solution)/shard_map/ppermute | solution.py:395
  63.0 5.4 %collective-permute-done.27.right_ref = f32[56,384]{1,0:T(8,128)S(1)} collective-permute-done((f32[56,384]{1,0:T(8,128)S(1)}, f32[56,384]{1,0:T(8,128)S(1)}, u32[]{:S(2)}, u32[]{:S(2)}) %collective-permute-start.27) | collective-permute-done | bytes 86048 | tf_op jit(solution)/shard_map/ppermute | solution.py:404
  68.4 5.4 %collective-permute-done.28.refs_1_ = f32[56,384]{1,0:T(8,128)S(1)} collective-permute-done((f32[56,384]{1,0:T(8,128)S(1)}, f32[56,384]{1,0:T(8,128)S(1)}, u32[]{:S(2)}, u32[]{:S(2)}) %collective-permute-start.28) | collective-permute-done | bytes 86048 | tf_op jit(solution)/shard_map/ppermute | solution.py:404
  77.9 1.6 %collective-permute-start.31 = (f32[56,384]{1,0:T(8,128)S(1)}, f32[56,384]{1,0:T(8,128)S(1)}, u32[]{:S(2)}, u32[]{:S(2)}) collective-permute-start(f32[56,384]{1,0:T(8,128)S(1)} %get-tuple-element.63), channel_id=1, source_target_pairs={{0,4},{1,5},{2,6},{3,7},{4,0},{5,1},{6,2},{7,3},{8,12},{9,13},{10,... | collective-permute-start | bytes 258056 | tf_op jit(solution)/shard_map/ppermute | solution.py:395
  80.0 2.4 %collective-permute-done.30.refs_2_ = f32[56,384]{1,0:T(8,128)S(1)} collective-permute-done((f32[56,384]{1,0:T(8,128)S(1)}, f32[56,384]{1,0:T(8,128)S(1)}, u32[]{:S(2)}, u32[]{:S(2)}) %collective-permute-start.30) | collective-permute-done | bytes 86048 | tf_op jit(solution)/shard_map/ppermute | solution.py:395
  87.9 1.9 %final_products.4 = (f32[384,128]{1,0:T(8,128)S(1)}, f32[48,128]{1,0:T(8,128)S(1)}, f32[48,384]{1,0:T(8,128)}) custom-call(f32[384,3072]{1,0:T(8,128)S(1)} %get-tuple-element.45.s_ref, f32[48,384]{1,0:T(8,128)S(1)} %update.8.w_ref, f32[48,384]{1,0:T(8,128)S(1)} %update.9.refs_0_, f32[48,384]{1,0:T(8,128)S(1)} %collective-permute-done.36.refs_1_), custom_call_target="tpu_custom_call" | custom-call | flops 339738624 | bytes 2359296 | tf_op jit(solution)/shard_map/final_products/pallas_call | solution.py:328
  89.8 2.0 %collective-permute-done.34.refs_0_ = f32[48,384]{1,0:T(8,128)S(1)} collective-permute-done((f32[48,384]{1,0:T(8,128)S(1)}, f32[48,384]{1,0:T(8,128)S(1)}, u32[]{:S(2)}, u32[]{:S(2)}) %collective-permute-start.34) | collective-permute-done | bytes 73760 | tf_op jit(solution)/shard_map/ppermute | solution.py:395
  94.0 1.9 %final_products.6 = (f32[384,128]{1,0:T(8,128)S(1)}, f32[48,128]{1,0:T(8,128)S(1)}) custom-call(f32[384,3072]{1,0:T(8,128)S(1)} %get-tuple-element.45.s_ref, f32[48,384]{1,0:T(8,128)S(1)} %update.8.w_ref, f32[48,384]{1,0:T(8,128)S(1)} %collective-permute-done.33.refs_0_, f32[48,384]{1,0:T(8,128)S(1)} %collective-permute-done.38.refs_1_, ...), custom_call_target="tpu_custom_call" | custom-call | flops 509607936 | bytes 3538944 | tf_op jit(solution)/shard_map/final_products/pallas_call | solution.py:328
  96.8 2.3 %collective-permute-start.41 = (f32[96,128]{1,0:T(8,128)S(1)}, f32[96,128]{1,0:T(8,128)S(1)}, u32[]{:S(2)}, u32[]{:S(2)}) collective-permute-start(f32[96,128]{1,0:T(8,128)S(1)} %get-tuple-element.82), channel_id=1, source_target_pairs={{0,16},{8,24},{16,0},{24,8},{1,17},{9,25},{17,1},{25,9},{2,18},{10... | collective-permute-start | bytes 147464 | tf_op jit(solution)/shard_map/ppermute | solution.py:395
  99.2 2.0 %collective-permute-start.42 = (f32[96,128]{1,0:T(8,128)S(1)}, f32[96,128]{1,0:T(8,128)S(1)}, u32[]{:S(2)}, u32[]{:S(2)}) collective-permute-start(f32[96,128]{1,0:T(8,128)S(1)} %get-tuple-element.83), channel_id=1, source_target_pairs={{0,24},{8,16},{16,8},{24,0},{1,25},{9,17},{17,9},{25,1},{2,26},{10... | collective-permute-start | bytes 147464 | tf_op jit(solution)/shard_map/ppermute | solution.py:395
  101.2 2.2 %collective-permute-done.41.refs_2_ = f32[96,128]{1,0:T(8,128)S(1)} collective-permute-done((f32[96,128]{1,0:T(8,128)S(1)}, f32[96,128]{1,0:T(8,128)S(1)}, u32[]{:S(2)}, u32[]{:S(2)}) %collective-permute-start.41) | collective-permute-done | bytes 49184 | tf_op jit(solution)/shard_map/ppermute | solution.py:395
  103.4 1.7 %collective-permute-done.42.refs_3_ = f32[96,128]{1,0:T(8,128)S(1)} collective-permute-done((f32[96,128]{1,0:T(8,128)S(1)}, f32[96,128]{1,0:T(8,128)S(1)}, u32[]{:S(2)}, u32[]{:S(2)}) %collective-permute-start.42) | collective-permute-done | bytes 49184 | tf_op jit(solution)/shard_map/ppermute | solution.py:395
  (97 shorter events, 40.4 us)
Async XLA Ops:
  0.6 8.7 %collective-permute-start.1 = (f32[48,96]{1,0:T(8,128)}, f32[48,96]{1,0:T(8,128)S(1)}, u32[]{:S(2)}, u32[]{:S(2)}) collective-permute-start(f32[48,96]{1,0:T(8,128)} %refs_0_.1), channel_id=1, source_target_pairs={{0,16},{8,24},{16,0},{24,8},{1,17},{9,25},{17,1},{25,9},{2,18},{10... | collective-permute-start | bytes 55304 | tf_op jit(solution)/shard_map/ppermute | solution.py:432
  6.1 5.8 %collective-permute-start.2 = (f32[48,96]{1,0:T(8,128)}, f32[48,96]{1,0:T(8,128)S(1)}, u32[]{:S(2)}, u32[]{:S(2)}) collective-permute-start(f32[48,96]{1,0:T(8,128)} %refs_0_.1), channel_id=1, source_target_pairs={{0,8},{8,16},{16,24},{24,0},{1,9},{9,17},{17,25},{25,1},{2,10},{10... | collective-permute-start | bytes 55304 | tf_op jit(solution)/shard_map/ppermute | solution.py:432
  14.5 5.6 %collective-permute-start.4 = (f32[56,384]{1,0:T(8,128)S(1)}, f32[56,384]{1,0:T(8,128)S(1)}, u32[]{:S(2)}, u32[]{:S(2)}) collective-permute-start(f32[56,384]{1,0:T(8,128)S(1)} %get-tuple-element.48), channel_id=1, source_target_pairs={{0,6},{1,7},{2,4},{3,5},{4,2},{5,3},{6,0},{7,1},{8,14},{9,15},{10,... | collective-permute-start | bytes 258056 | tf_op jit(solution)/shard_map/ppermute | solution.py:395
  17.0 4.9 %collective-permute-start.5 = (f32[56,384]{1,0:T(8,128)S(1)}, f32[56,384]{1,0:T(8,128)S(1)}, u32[]{:S(2)}, u32[]{:S(2)}) collective-permute-start(f32[56,384]{1,0:T(8,128)S(1)} %get-tuple-element.49), channel_id=1, source_target_pairs={{0,4},{1,5},{2,6},{3,7},{4,0},{5,1},{6,2},{7,3},{8,12},{9,13},{10,... | collective-permute-start | bytes 258056 | tf_op jit(solution)/shard_map/ppermute | solution.py:395
  22.3 5.1 %collective-permute-start.9 = (f32[48,384]{1,0:T(8,128)S(1)}, f32[48,384]{1,0:T(8,128)S(1)}, u32[]{:S(2)}, u32[]{:S(2)}) collective-permute-start(f32[48,384]{1,0:T(8,128)S(1)} %update.5.refs_0_.factor_ref), channel_id=1, source_target_pairs={{0,4},{1,5},{2,6},{3,7},{4,0},{5,1},{6,2},{7,3},{8,12},{9,13},{10,... | collective-permute-start | bytes 221192 | tf_op jit(solution)/shard_map/ppermute | solution.py:395
  23.9 6.0 %collective-permute-start.8 = (f32[48,384]{1,0:T(8,128)S(1)}, f32[48,384]{1,0:T(8,128)S(1)}, u32[]{:S(2)}, u32[]{:S(2)}) collective-permute-start(f32[48,384]{1,0:T(8,128)S(1)} %update.5.refs_0_.factor_ref), channel_id=1, source_target_pairs={{0,6},{1,7},{2,4},{3,5},{4,2},{5,3},{6,0},{7,1},{8,14},{9,15},{10,... | collective-permute-start | bytes 221192 | tf_op jit(solution)/shard_map/ppermute | solution.py:395
  25.3 5.2 %collective-permute-start.7 = (f32[48,384]{1,0:T(8,128)S(1)}, f32[48,384]{1,0:T(8,128)S(1)}, u32[]{:S(2)}, u32[]{:S(2)}) collective-permute-start(f32[48,384]{1,0:T(8,128)S(1)} %update.5.refs_0_.factor_ref), channel_id=1, source_target_pairs={{0,2},{1,3},{2,0},{3,1},{4,6},{5,7},{6,4},{7,5},{8,10},{9,11},{10,... | collective-permute-start | bytes 221192 | tf_op jit(solution)/shard_map/ppermute | solution.py:395
  32.5 5.5 %collective-permute-start.14 = (f32[56,384]{1,0:T(8,128)S(1)}, f32[56,384]{1,0:T(8,128)S(1)}, u32[]{:S(2)}, u32[]{:S(2)}) collective-permute-start(f32[56,384]{1,0:T(8,128)S(1)} %spectra_times_components.11.left_ref), channel_id=1, source_target_pairs={{0,8},{1,17},{2,10},{3,19},{4,12},{5,21},{6,14},{7,23},{8,0},{9,25... | collective-permute-start | bytes 258056 | tf_op jit(solution)/shard_map/ppermute | solution.py:404
  38.0 5.5 %collective-permute-start.15 = (f32[56,384]{1,0:T(8,128)S(1)}, f32[56,384]{1,0:T(8,128)S(1)}, u32[]{:S(2)}, u32[]{:S(2)}) collective-permute-start(f32[56,384]{1,0:T(8,128)S(1)} %add.2.refs_0_), channel_id=1, source_target_pairs={{0,16},{1,9},{2,18},{3,11},{4,20},{5,13},{6,22},{7,15},{8,24},{9,1... | collective-permute-start | bytes 258056 | tf_op jit(solution)/shard_map/ppermute | solution.py:404
  46.0 6.0 %collective-permute-start.17 = (f32[56,384]{1,0:T(8,128)S(1)}, f32[56,384]{1,0:T(8,128)S(1)}, u32[]{:S(2)}, u32[]{:S(2)}) collective-permute-start(f32[56,384]{1,0:T(8,128)S(1)} %get-tuple-element.55), channel_id=1, source_target_pairs={{0,6},{1,7},{2,4},{3,5},{4,2},{5,3},{6,0},{7,1},{8,14},{9,15},{10,... | collective-permute-start | bytes 258056 | tf_op jit(solution)/shard_map/ppermute | solution.py:395
  47.5 5.9 %collective-permute-start.18 = (f32[56,384]{1,0:T(8,128)S(1)}, f32[56,384]{1,0:T(8,128)S(1)}, u32[]{:S(2)}, u32[]{:S(2)}) collective-permute-start(f32[56,384]{1,0:T(8,128)S(1)} %get-tuple-element.56), channel_id=1, source_target_pairs={{0,4},{1,5},{2,6},{3,7},{4,0},{5,1},{6,2},{7,3},{8,12},{9,13},{10,... | collective-permute-start | bytes 258056 | tf_op jit(solution)/shard_map/ppermute | solution.py:395
  48.0 5.4 %collective-permute-start.19 = (f32[56,384]{1,0:T(8,128)S(1)}, f32[56,384]{1,0:T(8,128)S(1)}, u32[]{:S(2)}, u32[]{:S(2)}) collective-permute-start(f32[56,384]{1,0:T(8,128)S(1)} %get-tuple-element.57), channel_id=1, source_target_pairs={{0,2},{1,3},{2,0},{3,1},{4,6},{5,7},{6,4},{7,5},{8,10},{9,11},{10,... | collective-permute-start | bytes 258056 | tf_op jit(solution)/shard_map/ppermute | solution.py:395
  53.8 6.0 %collective-permute-start.22 = (f32[48,384]{1,0:T(8,128)S(1)}, f32[48,384]{1,0:T(8,128)S(1)}, u32[]{:S(2)}, u32[]{:S(2)}) collective-permute-start(f32[48,384]{1,0:T(8,128)S(1)} %update.7.refs_0_.factor_ref), channel_id=1, source_target_pairs={{0,4},{1,5},{2,6},{3,7},{4,0},{5,1},{6,2},{7,3},{8,12},{9,13},{10,... | collective-permute-start | bytes 221192 | tf_op jit(solution)/shard_map/ppermute | solution.py:395
  54.5 5.8 %collective-permute-start.21 = (f32[48,384]{1,0:T(8,128)S(1)}, f32[48,384]{1,0:T(8,128)S(1)}, u32[]{:S(2)}, u32[]{:S(2)}) collective-permute-start(f32[48,384]{1,0:T(8,128)S(1)} %update.7.refs_0_.factor_ref), channel_id=1, source_target_pairs={{0,6},{1,7},{2,4},{3,5},{4,2},{5,3},{6,0},{7,1},{8,14},{9,15},{10,... | collective-permute-start | bytes 221192 | tf_op jit(solution)/shard_map/ppermute | solution.py:395
  56.0 5.2 %collective-permute-start.20 = (f32[48,384]{1,0:T(8,128)S(1)}, f32[48,384]{1,0:T(8,128)S(1)}, u32[]{:S(2)}, u32[]{:S(2)}) collective-permute-start(f32[48,384]{1,0:T(8,128)S(1)} %update.7.refs_0_.factor_ref), channel_id=1, source_target_pairs={{0,2},{1,3},{2,0},{3,1},{4,6},{5,7},{6,4},{7,5},{8,10},{9,11},{10,... | collective-permute-start | bytes 221192 | tf_op jit(solution)/shard_map/ppermute | solution.py:395
  62.9 5.5 %collective-permute-start.27 = (f32[56,384]{1,0:T(8,128)S(1)}, f32[56,384]{1,0:T(8,128)S(1)}, u32[]{:S(2)}, u32[]{:S(2)}) collective-permute-start(f32[56,384]{1,0:T(8,128)S(1)} %spectra_times_components.15.left_ref), channel_id=1, source_target_pairs={{0,8},{1,17},{2,10},{3,19},{4,12},{5,21},{6,14},{7,23},{8,0},{9,25... | collective-permute-start | bytes 258056 | tf_op jit(solution)/shard_map/ppermute | solution.py:404
  68.4 5.4 %collective-permute-start.28 = (f32[56,384]{1,0:T(8,128)S(1)}, f32[56,384]{1,0:T(8,128)S(1)}, u32[]{:S(2)}, u32[]{:S(2)}) collective-permute-start(f32[56,384]{1,0:T(8,128)S(1)} %add.3.refs_0_), channel_id=1, source_target_pairs={{0,16},{1,9},{2,18},{3,11},{4,20},{5,13},{6,22},{7,15},{8,24},{9,1... | collective-permute-start | bytes 258056 | tf_op jit(solution)/shard_map/ppermute | solution.py:404
  76.4 5.9 %collective-permute-start.30 = (f32[56,384]{1,0:T(8,128)S(1)}, f32[56,384]{1,0:T(8,128)S(1)}, u32[]{:S(2)}, u32[]{:S(2)}) collective-permute-start(f32[56,384]{1,0:T(8,128)S(1)} %get-tuple-element.62), channel_id=1, source_target_pairs={{0,6},{1,7},{2,4},{3,5},{4,2},{5,3},{6,0},{7,1},{8,14},{9,15},{10,... | collective-permute-start | bytes 258056 | tf_op jit(solution)/shard_map/ppermute | solution.py:395
  77.9 5.9 %collective-permute-start.31 = (f32[56,384]{1,0:T(8,128)S(1)}, f32[56,384]{1,0:T(8,128)S(1)}, u32[]{:S(2)}, u32[]{:S(2)}) collective-permute-start(f32[56,384]{1,0:T(8,128)S(1)} %get-tuple-element.63), channel_id=1, source_target_pairs={{0,4},{1,5},{2,6},{3,7},{4,0},{5,1},{6,2},{7,3},{8,12},{9,13},{10,... | collective-permute-start | bytes 258056 | tf_op jit(solution)/shard_map/ppermute | solution.py:395
  84.3 5.5 %collective-permute-start.35 = (f32[48,384]{1,0:T(8,128)S(1)}, f32[48,384]{1,0:T(8,128)S(1)}, u32[]{:S(2)}, u32[]{:S(2)}) collective-permute-start(f32[48,384]{1,0:T(8,128)S(1)} %update.9.refs_0_), channel_id=1, source_target_pairs={{0,4},{1,5},{2,6},{3,7},{4,0},{5,1},{6,2},{7,3},{8,12},{9,13},{10,... | collective-permute-start | bytes 221192 | tf_op jit(solution)/shard_map/ppermute | solution.py:395
  85.8 6.0 %collective-permute-start.34 = (f32[48,384]{1,0:T(8,128)S(1)}, f32[48,384]{1,0:T(8,128)S(1)}, u32[]{:S(2)}, u32[]{:S(2)}) collective-permute-start(f32[48,384]{1,0:T(8,128)S(1)} %update.9.refs_0_), channel_id=1, source_target_pairs={{0,6},{1,7},{2,4},{3,5},{4,2},{5,3},{6,0},{7,1},{8,14},{9,15},{10,... | collective-permute-start | bytes 221192 | tf_op jit(solution)/shard_map/ppermute | solution.py:395
  87.2 6.6 %collective-permute-start.33 = (f32[48,384]{1,0:T(8,128)S(1)}, f32[48,384]{1,0:T(8,128)S(1)}, u32[]{:S(2)}, u32[]{:S(2)}) collective-permute-start(f32[48,384]{1,0:T(8,128)S(1)} %update.9.refs_0_), channel_id=1, source_target_pairs={{0,2},{1,3},{2,0},{3,1},{4,6},{5,7},{6,4},{7,5},{8,10},{9,11},{10,... | collective-permute-start | bytes 221192 | tf_op jit(solution)/shard_map/ppermute | solution.py:395
  96.8 6.6 %collective-permute-start.41 = (f32[96,128]{1,0:T(8,128)S(1)}, f32[96,128]{1,0:T(8,128)S(1)}, u32[]{:S(2)}, u32[]{:S(2)}) collective-permute-start(f32[96,128]{1,0:T(8,128)S(1)} %get-tuple-element.82), channel_id=1, source_target_pairs={{0,16},{8,24},{16,0},{24,8},{1,17},{9,25},{17,1},{25,9},{2,18},{10... | collective-permute-start | bytes 147464 | tf_op jit(solution)/shard_map/ppermute | solution.py:395
  99.2 5.9 %collective-permute-start.42 = (f32[96,128]{1,0:T(8,128)S(1)}, f32[96,128]{1,0:T(8,128)S(1)}, u32[]{:S(2)}, u32[]{:S(2)}) collective-permute-start(f32[96,128]{1,0:T(8,128)S(1)} %get-tuple-element.83), channel_id=1, source_target_pairs={{0,24},{8,16},{16,8},{24,0},{1,25},{9,17},{17,9},{25,1},{2,26},{10... | collective-permute-start | bytes 147464 | tf_op jit(solution)/shard_map/ppermute | solution.py:395
  (21 other events, 72.2 us)

commit v3 on v2

--- a/solution.py
+++ b/solution.py
@@ -6,6 +6,7 @@
 from jax.experimental import pallas as pl
 from jax.experimental.pallas import tpu as pltpu
 from jax.sharding import PartitionSpec as P
+
 
 ITERS = 3
 LANES = 128
@@ -14,7 +15,6 @@
 BF16 = jnp.bfloat16
 NN = (((1,), (0,)), ((), ()))
 NT = (((1,), (1,)), ((), ()))
-TN = (((0,), (0,)), ((), ()))
 
 
 def matmul(left, right):
@@ -248,57 +248,51 @@
     )(high, low, *pieces, *extra)
 
 
+def thirds(value):
+    high, low = split(value)
+    return high, low, (value - high.astype(F32) - low.astype(F32)).astype(BF16)
+
+
 def final_gather_kernel(relatives, groups, first, last, s_ref, w_ref, *refs):
     pieces, refs = refs[: len(relatives)], refs[len(relatives) :]
-    if first:
-        kept_ref = refs[-1]
-        kept_ref[...] = pieces[0][...]
-    else:
-        before_ref, gram_before_ref, refs = refs[0], refs[1], refs[2:]
+    carried, refs = ((), refs) if first else (refs[:3], refs[3:])
     rank, width = pieces[0].shape
     pixels = w_ref.shape[1]
     w_t = w_ref[...].T
-    w0, w1 = split(w_t)
-    w2 = (w_t - w0.astype(F32) - w1.astype(F32)).astype(BF16)
-    left = jnp.concatenate([w0, w0, w1, w1, w0, w2], axis=1)
-    lane = lax.broadcasted_iota(jnp.int32, (pixels, LANES), 1)
+    w0, w1, w2 = thirds(w_t)
+    left = jnp.concatenate([w0, w0, w1, w1, w2], axis=1)
     half = LANES // 2
-    zeros = functools.partial(jnp.zeros, dtype=BF16)
-    total, gram = None, None
+    front = jnp.zeros((half, width), BF16)
+    back = jnp.zeros((half - rank, width), BF16)
+    sums = [ref[...] for ref in carried] if carried else [None] * 3
     for relative, piece in zip(relatives, pieces):
-        h = piece[...]
-        h0, h1 = split(h)
-        h2 = (h - h0.astype(F32) - h1.astype(F32)).astype(BF16)
-        right = jnp.concatenate([h0, h1, h0, h1, h2, h0], axis=0)
+        h0, h1, _ = thirds(piece[...])
+        right = jnp.concatenate([h0, h1, h0, h1, h0], axis=0)
         d = s_ref[:, bins_of(relative, width)] - fast(left, right, NN)
-        d0, d1 = split(d)
-        tail = zeros((LANES - rank, width))
-        high = jnp.concatenate([h0, tail], axis=0)
-        both = fast(d0, jnp.concatenate([high, h1, tail], axis=0), NT)
-        term = both[:, :LANES] + both[:, LANES:] + fast(d1, high, NT)
-        squares = jnp.sum(d * d, axis=1, keepdims=True)
-        term = jnp.where(lane == rank, squares, term)
-        front = zeros((half, width))
-        back = zeros((half - rank, width))
         stack = jnp.concatenate([h0, h1], axis=0)
-        square = product(
+        error = product(stack, h0, *split(d), NT)
+        gram = product(
             stack,
             h0,
             jnp.concatenate([front, h0, back], axis=0),
             jnp.concatenate([front, h1, back], axis=0),
             NT,
         )
-        total = term if total is None else total + term
-        gram = square if gram is None else gram + square
-    if not first:
-        total = total + before_ref[...]
-        gram = gram + gram_before_ref[...]
+        square = d * d
+        folded = square[:, :LANES]
+        for start in range(LANES, width, LANES):
+            folded = folded + square[:, start : start + LANES]
+        terms = (error, folded, gram)
+        sums = [t if s is None else s + t for s, t in zip(sums, terms)]
+    error, folded, gram = sums
     if not last:
-        refs[0][...] = total
-        refs[1][...] = gram
+        for ref, value in zip(refs, sums):
+            ref[...] = value
         return
     outs, own_ref, scratch, w_scratch = refs[:groups], refs[groups], refs[-2], refs[-1]
-    scratch[...] = total
+    tall = jnp.concatenate([error, jnp.zeros((LANES - rank, pixels), F32)], axis=0)
+    lane = lax.broadcasted_iota(jnp.int32, (pixels, LANES), 1)
+    scratch[...] = jnp.where(lane == rank, jnp.sum(folded, axis=1, keepdims=True), tall.T)
     w_scratch[...] = w_t
     rows = pixels // groups
     me = lax.axis_index("mz")
@@ -315,34 +309,29 @@
     rows = pixels // groups
     count = len(relatives)
     first = before is None
-    extra = () if first else tuple(before[:2])
+    extra = () if first else tuple(before)
+    shapes = [(rank, pixels), (pixels, LANES), (rank, LANES)]
+    scratch = []
     if last:
-        shapes = [jax.ShapeDtypeStruct((rows, LANES), F32)] * groups
-        shapes.append(jax.ShapeDtypeStruct((rows, rank), F32))
+        shapes = [(rows, LANES)] * groups + [(rows, rank)]
         scratch = [pltpu.VMEM((pixels, LANES), F32), pltpu.VMEM((pixels, rank), F32)]
-    else:
-        shapes = [jax.ShapeDtypeStruct((pixels, LANES), F32), jax.ShapeDtypeStruct((rank, LANES), F32)]
-        scratch = []
-    if first:
-        shapes.append(jax.ShapeDtypeStruct((rank, width), F32))
-    results = pl.pallas_call(
+    return pl.pallas_call(
         functools.partial(final_gather_kernel, relatives, groups, first, last),
         in_specs=vmem(2 + count + len(extra)),
         out_specs=vmem(len(shapes)),
-        out_shape=shapes,
+        out_shape=[jax.ShapeDtypeStruct(shape, F32) for shape in shapes],
         scratch_shapes=scratch,
         compiler_params=params(),
-        cost_estimate=cost(24 * rank * pixels * width * count, 8 * pixels * width * count),
+        cost_estimate=cost(18 * rank * pixels * width * count, 8 * pixels * width * count),
         name="final_products",
     )(spectra, w_block, *pieces, *extra)
-    kept = () if first else (before[-1],)
-    return (*results, *kept)
-
-
-def final_kernel(w_t_ref, *refs):
-    parts, (w_out, misfit_out) = refs[:-2], refs[-2:]
+
+
+def final_kernel(w_t_ref, h_ref, *refs):
+    parts, (w_out, h_out, misfit_out) = refs[:-3], refs[-3:]
+    h_out[...] = h_ref[...]
     w_t = w_t_ref[...]
-    rows, rank = w_t.shape
+    _, rank = w_t.shape
     total = parts[0][...]
     for part in parts[1:]:
         total = total + part[...]
@@ -358,22 +347,26 @@
     misfit_out[...] = misfit[:1]
 
 
-def final_call(w_t, *parts):
+def final_call(w_t, h_piece, *parts):
     rows, rank = w_t.shape
     return pl.pallas_call(
         final_kernel,
-        in_specs=vmem(1 + len(parts)),
-        out_specs=vmem(2),
-        out_shape=[jax.ShapeDtypeStruct((rank, rows), F32), jax.ShapeDtypeStruct((1, rows), F32)],
+        in_specs=vmem(2 + len(parts)),
+        out_specs=vmem(3),
+        out_shape=[
+            jax.ShapeDtypeStruct((rank, rows), F32),
+            jax.ShapeDtypeStruct(h_piece.shape, F32),
+            jax.ShapeDtypeStruct((1, rows), F32),
+        ],
         compiler_params=params(),
         cost_estimate=cost(24 * rank * rank * rows, 4 * rows * LANES * len(parts)),
         name="final_update",
-    )(w_t, *parts)
+    )(w_t, h_piece, *parts)
 
 
 def join_kernel(*refs):
     pieces, out = refs[:-1], refs[-1]
-    rank, width = pieces[0].shape
+    _, width = pieces[0].shape
     whole = jnp.concatenate([piece[...] for piece in pieces], axis=1)
     out[...] = pltpu.roll(whole, lax.axis_index("mz") * width, 1)
 
@@ -397,7 +390,7 @@
 
 def cross(value, groups, owners, even, odd):
     pairs = [
-        (g * owners + o, (g ^ (odd if o % 2 else even)) * owners + o)
+        (g * owners + o, (g ^ (even if o % 2 else odd)) * owners + o)
         for g in range(groups)
         for o in range(owners)
     ]
@@ -405,22 +398,17 @@
 
 
 def spread(h_piece, owners, products):
-    evens = list(range(owners - 2, 0, -2))
+    evens = [owners - 2, *range(2, owners - 2, 2)]
+    mine = []
+    for relative in evens:
+        mine.append(swap(h_piece, "px", owners, relative))
     beside = swap(h_piece, "px", owners, 1)
-    mine = [swap(h_piece, "px", owners, r) for r in evens]
+    theirs = []
+    for piece in mine:
+        theirs.append(swap(piece, "px", owners, 1))
     total = products([0, 1], [h_piece, beside], None, False)
-    theirs, held = [], []
-    for index, (relative, piece) in enumerate(zip(evens, mine)):
-        if index:
-            piece, total = lax.optimization_barrier((piece, total))
-        theirs.append(swap(piece, "px", owners, 1))
-        held.append((relative, piece))
-        if 0 < index < len(evens) - 1:
-            total = products(*zip(*held), total, False)
-            held = []
-    held += [(r + 1, piece) for r, piece in zip(evens[:-1], theirs)]
-    total = products(*zip(*held), total, False)
-    return products([evens[-1] + 1], [theirs[-1]], total, True)
+    total = products(evens, mine, total, False)
+    return products([r + 1 for r in evens], theirs, total, True)
 
 
 def fast_device(groups, owners, spectra, w_piece, h_piece):
@@ -462,8 +450,8 @@
                 ),
             )
             sent = [swap(parts[k], "mz", groups, k) for k in range(1, groups)]
-            w_final, misfit = final_call(parts[groups], parts[0], *sent)
-    return w_final, parts[-1], misfit.reshape(-1)
+            w_final, h_final, misfit = final_call(parts[groups], h_piece, parts[0], *sent)
+    return w_final, h_final, misfit.reshape(-1)
 
 
 def per_device(groups, owners, spectra, w_piece, h_piece):

time: 106 us -> 105 us (level)
  Pallas kernels: 20.1 us -> 18.6 us
  starting transfers between devices: 34.1 us -> 32.9 us
  waiting for transfers between devices: 51.2 us -> 52.4 us
    ppermute x36, waiting for transfers between devices: 27 us -> 29.9 us  [swap(): return lax.ppermute(value, axis, [(i, i ^ mask) for i in range(size)])]
    ppermute x4, waiting for transfers between devices: 21.6 us -> 19.8 us  [cross(): return lax.ppermute(value, ('mz', 'px'), pairs)]
    ppermute x36, starting transfers between devices: 27.7 us -> 26 us  [swap(): return lax.ppermute(value, axis, [(i, i ^ mask) for i in range(size)])]
    pallas_call x4 -> x3, Pallas kernels: 6.24 us -> 5.22 us  [final_gather_call(): pl.pallas_call(functools.partial(final_gather_kernel, relatives, groups,...]
    pallas_call x8 -> x6, Pallas kernels: 5.07 us -> 4.66 us  [gather_call(): pl.pallas_call(functools.partial(gather_kernel, relatives, before is not...]
  transfers between devices with their start and end apart: 43 -> 43, of which waited for: 25 -> 27; matrix products, arithmetic and copies ran while one was open for 0% -> 0% of each run, Pallas kernels for 13% -> 10%
where the time goes in v3:
time: 105 us
  waiting for transfers between devices  52.4 us (50%)
  starting transfers between devices  32.9 us (31%)
  Pallas kernels  18.6 us (18%)
    ppermute x36, waiting for transfers between devices, swap(): return lax.ppermute(value, axis, [(i, i ^ mask) for i in range(size)])  29.9 us
    ppermute x36, starting transfers between devices, swap(): return lax.ppermute(value, axis, [(i, i ^ mask) for i in range(size)])  26 us
    ppermute x4, waiting for transfers between devices, cross(): return lax.ppermute(value, ('mz', 'px'), pairs)  19.8 us
    ppermute x3, starting transfers between devices, fast_device(): lax.ppermute(w_piece, 'mz', [(i, (i - k) % groups) for i in range(groups)])  6.16 us
    pallas_call x3, Pallas kernels, final_gather_call(): pl.pallas_call(functools.partial(final_gather_kernel, relatives, groups,...  5.22 us
    pallas_call x6, Pallas kernels, gather_call(): pl.pallas_call(functools.partial(gather_kernel, relatives, before is not...  4.66 us
    pallas_call x6, Pallas kernels, scatter_call(): pl.pallas_call(functools.partial(scatter_kernel, relatives, width), in_sp...  3.37 us
    ppermute x3, waiting for transfers between devices, fast_device(): lax.ppermute(w_piece, 'mz', [(i, (i - k) % groups) for i in range(groups)])  2.62 us
  transfers between devices with their start and end apart: 43, of which 27 were waited for; matrix products, arithmetic and copies ran while one was open for 0% of the time, Pallas kernels for 10%

profile of v3, /device:TPU:0, one launch (start us, length us, event | category | flops | bytes accessed | tf_op | source)
XLA Modules:
  0.0 104.9 jit_solution(5149879480961168138)
XLA Ops:
  0.6 4.1 %collective-permute-start.1 = (f32[48,96]{1,0:T(8,128)}, f32[48,96]{1,0:T(8,128)S(1)}, u32[]{:S(2)}, u32[]{:S(2)}) collective-permute-start(f32[48,96]{1,0:T(8,128)} %refs_0_.1), channel_id=1, source_target_pairs={{0,16},{8,24},{16,0},{24,8},{1,17},{9,25},{17,1},{25,9},{2,18},{10... | collective-permute-start | bytes 55304 | tf_op jit(solution)/shard_map/ppermute | solution.py:420
  6.8 2.5 %split_spectra.1 = (f32[384,3072]{1,0:T(8,128)S(1)}, bf16[384,3072]{1,0:T(8,128)(2,1)S(1)}, bf16[384,3072]{1,0:T(8,128)(2,1)S(1)}) custom-call(f32[384,3072]{1,0:T(8,128)} %s_ref.1), custom_call_target="tpu_custom_call" | custom-call | flops 4718592 | bytes 14155776 | tf_op jit(solution)/shard_map/split_spectra/pallas_call | solution.py:110
  9.3 2.6 %collective-permute-done.2.refs_3_ = f32[48,96]{1,0:T(8,128)S(1)} collective-permute-done((f32[48,96]{1,0:T(8,128)}, f32[48,96]{1,0:T(8,128)S(1)}, u32[]{:S(2)}, u32[]{:S(2)}) %collective-permute-start.2) | collective-permute-done | bytes 18464 | tf_op jit(solution)/shard_map/ppermute | solution.py:420
  14.5 2.5 %collective-permute-start.4 = (f32[56,384]{1,0:T(8,128)S(1)}, f32[56,384]{1,0:T(8,128)S(1)}, u32[]{:S(2)}, u32[]{:S(2)}) collective-permute-start(f32[56,384]{1,0:T(8,128)S(1)} %get-tuple-element.32), channel_id=1, source_target_pairs={{0,6},{1,7},{2,4},{3,5},{4,2},{5,3},{6,0},{7,1},{8,14},{9,15},{10,... | collective-permute-start | bytes 258056 | tf_op jit(solution)/shard_map/ppermute | solution.py:388
  18.0 2.0 %collective-permute-done.4.refs_2_ = f32[56,384]{1,0:T(8,128)S(1)} collective-permute-done((f32[56,384]{1,0:T(8,128)S(1)}, f32[56,384]{1,0:T(8,128)S(1)}, u32[]{:S(2)}, u32[]{:S(2)}) %collective-permute-start.4) | collective-permute-done | bytes 86048 | tf_op jit(solution)/shard_map/ppermute | solution.py:388
  20.1 1.8 %collective-permute-done.5.refs_3_ = f32[56,384]{1,0:T(8,128)S(1)} collective-permute-done((f32[56,384]{1,0:T(8,128)S(1)}, f32[56,384]{1,0:T(8,128)S(1)}, u32[]{:S(2)}, u32[]{:S(2)}) %collective-permute-start.5) | collective-permute-done | bytes 86048 | tf_op jit(solution)/shard_map/ppermute | solution.py:388
  22.3 1.6 %collective-permute-start.11 = (f32[48,384]{1,0:T(8,128)S(1)}, f32[48,384]{1,0:T(8,128)S(1)}, u32[]{:S(2)}, u32[]{:S(2)}) collective-permute-start(f32[48,384]{1,0:T(8,128)S(1)} %update.5.refs_0_.factor_ref), channel_id=1, source_target_pairs={{0,4},{1,5},{2,6},{3,7},{4,0},{5,1},{6,2},{7,3},{8,12},{9,13},{10,... | collective-permute-start | bytes 221192 | tf_op jit(solution)/shard_map/ppermute | solution.py:388
  26.7 2.1 %collective-permute-done.9.refs_1_ = f32[48,384]{1,0:T(8,128)S(1)} collective-permute-done((f32[48,384]{1,0:T(8,128)S(1)}, f32[48,384]{1,0:T(8,128)S(1)}, u32[]{:S(2)}, u32[]{:S(2)}) %collective-permute-start.9) | collective-permute-done | bytes 73760 | tf_op jit(solution)/shard_map/ppermute | solution.py:388
  32.2 5.4 %collective-permute-done.14.right_ref = f32[56,384]{1,0:T(8,128)S(1)} collective-permute-done((f32[56,384]{1,0:T(8,128)S(1)}, f32[56,384]{1,0:T(8,128)S(1)}, u32[]{:S(2)}, u32[]{:S(2)}) %collective-permute-start.14) | collective-permute-done | bytes 86048 | tf_op jit(solution)/shard_map/ppermute | solution.py:397
  37.6 4.7 %collective-permute-done.15.refs_1_ = f32[56,384]{1,0:T(8,128)S(1)} collective-permute-done((f32[56,384]{1,0:T(8,128)S(1)}, f32[56,384]{1,0:T(8,128)S(1)}, u32[]{:S(2)}, u32[]{:S(2)}) %collective-permute-start.15) | collective-permute-done | bytes 86048 | tf_op jit(solution)/shard_map/ppermute | solution.py:397
  48.5 2.5 %collective-permute-done.17.refs_2_ = f32[56,384]{1,0:T(8,128)S(1)} collective-permute-done((f32[56,384]{1,0:T(8,128)S(1)}, f32[56,384]{1,0:T(8,128)S(1)}, u32[]{:S(2)}, u32[]{:S(2)}) %collective-permute-start.17) | collective-permute-done | bytes 86048 | tf_op jit(solution)/shard_map/ppermute | solution.py:388
  54.7 1.5 %collective-permute-start.20 = (f32[48,384]{1,0:T(8,128)S(1)}, f32[48,384]{1,0:T(8,128)S(1)}, u32[]{:S(2)}, u32[]{:S(2)}) collective-permute-start(f32[48,384]{1,0:T(8,128)S(1)} %update.7.refs_0_.factor_ref), channel_id=1, source_target_pairs={{0,6},{1,7},{2,4},{3,5},{4,2},{5,3},{6,0},{7,1},{8,14},{9,15},{10,... | collective-permute-start | bytes 221192 | tf_op jit(solution)/shard_map/ppermute | solution.py:388
  57.0 2.1 %collective-permute-done.22.refs_1_ = f32[48,384]{1,0:T(8,128)S(1)} collective-permute-done((f32[48,384]{1,0:T(8,128)S(1)}, f32[48,384]{1,0:T(8,128)S(1)}, u32[]{:S(2)}, u32[]{:S(2)}) %collective-permute-start.22) | collective-permute-done | bytes 73760 | tf_op jit(solution)/shard_map/ppermute | solution.py:388
  62.8 5.3 %collective-permute-done.27.right_ref = f32[56,384]{1,0:T(8,128)S(1)} collective-permute-done((f32[56,384]{1,0:T(8,128)S(1)}, f32[56,384]{1,0:T(8,128)S(1)}, u32[]{:S(2)}, u32[]{:S(2)}) %collective-permute-start.27) | collective-permute-done | bytes 86048 | tf_op jit(solution)/shard_map/ppermute | solution.py:397
  68.2 4.5 %collective-permute-done.28.refs_1_ = f32[56,384]{1,0:T(8,128)S(1)} collective-permute-done((f32[56,384]{1,0:T(8,128)S(1)}, f32[56,384]{1,0:T(8,128)S(1)}, u32[]{:S(2)}, u32[]{:S(2)}) %collective-permute-start.28) | collective-permute-done | bytes 86048 | tf_op jit(solution)/shard_map/ppermute | solution.py:397
  75.3 1.7 %collective-permute-start.30 = (f32[56,384]{1,0:T(8,128)S(1)}, f32[56,384]{1,0:T(8,128)S(1)}, u32[]{:S(2)}, u32[]{:S(2)}) collective-permute-start(f32[56,384]{1,0:T(8,128)S(1)} %get-tuple-element.38), channel_id=1, source_target_pairs={{0,6},{1,7},{2,4},{3,5},{4,2},{5,3},{6,0},{7,1},{8,14},{9,15},{10,... | collective-permute-start | bytes 258056 | tf_op jit(solution)/shard_map/ppermute | solution.py:388
  78.9 2.2 %collective-permute-done.30.refs_2_ = f32[56,384]{1,0:T(8,128)S(1)} collective-permute-done((f32[56,384]{1,0:T(8,128)S(1)}, f32[56,384]{1,0:T(8,128)S(1)}, u32[]{:S(2)}, u32[]{:S(2)}) %collective-permute-start.30) | collective-permute-done | bytes 86048 | tf_op jit(solution)/shard_map/ppermute | solution.py:388
  81.1 1.6 %collective-permute-done.31.refs_3_ = f32[56,384]{1,0:T(8,128)S(1)} collective-permute-done((f32[56,384]{1,0:T(8,128)S(1)}, f32[56,384]{1,0:T(8,128)S(1)}, u32[]{:S(2)}, u32[]{:S(2)}) %collective-permute-start.31) | collective-permute-done | bytes 86048 | tf_op jit(solution)/shard_map/ppermute | solution.py:388
  87.5 2.1 %collective-permute-done.35.refs_1_ = f32[48,384]{1,0:T(8,128)S(1)} collective-permute-done((f32[48,384]{1,0:T(8,128)S(1)}, f32[48,384]{1,0:T(8,128)S(1)}, u32[]{:S(2)}, u32[]{:S(2)}) %collective-permute-start.35) | collective-permute-done | bytes 73760 | tf_op jit(solution)/shard_map/ppermute | solution.py:388
  91.9 2.0 %final_products.4 = (f32[48,384]{1,0:T(8,128)S(1)}, f32[384,128]{1,0:T(8,128)S(1)}, f32[48,128]{1,0:T(8,128)S(1)}) custom-call(f32[384,3072]{1,0:T(8,128)S(1)} %get-tuple-element.29.s_ref, f32[48,384]{1,0:T(8,128)S(1)} %update.8.w_ref, f32[48,384]{1,0:T(8,128)S(1)} %collective-permute-done.33.refs_0_, f32[48,384]{1,0:T(8,128)S(1)} %collective-permute-done.35.refs_1_, ...), custom_call_target="tpu_custom_call" | custom-call | flops 382205952 | bytes 3538944 | tf_op jit(solution)/shard_map/final_products/pallas_call | solution.py:318
  93.9 1.9 %final_products.5 = (f32[96,128]{1,0:T(8,128)S(1)}, f32[96,128]{1,0:T(8,128)S(1)}, f32[96,128]{1,0:T(8,128)S(1)}, f32[96,128]{1,0:T(8,128)S(1)}, f32[96,48]{1,0:T(8,128)S(1)}) custom-call(f32[384,3072]{1,0:T(8,128)S(1)} %get-tuple-element.29.s_ref, f32[48,384]{1,0:T(8,128)S(1)} %update.8.w_ref, f32[48,384]{1,0:T(8,128)S(1)} %collective-permute-done.34.refs_0_, ...), custom_call_target="tpu_custom_call" | custom-call | flops 382205952 | bytes 3538944 | tf_op jit(solution)/shard_map/final_products/pallas_call | solution.py:318
  95.9 1.9 %collective-permute-start.41 = (f32[96,128]{1,0:T(8,128)S(1)}, f32[96,128]{1,0:T(8,128)S(1)}, u32[]{:S(2)}, u32[]{:S(2)}) collective-permute-start(f32[96,128]{1,0:T(8,128)S(1)} %get-tuple-element.50), channel_id=1, source_target_pairs={{0,16},{8,24},{16,0},{24,8},{1,17},{9,25},{17,1},{25,9},{2,18},{10... | collective-permute-start | bytes 147464 | tf_op jit(solution)/shard_map/ppermute | solution.py:388
  97.8 2.4 %collective-permute-start.42 = (f32[96,128]{1,0:T(8,128)S(1)}, f32[96,128]{1,0:T(8,128)S(1)}, u32[]{:S(2)}, u32[]{:S(2)}) collective-permute-start(f32[96,128]{1,0:T(8,128)S(1)} %get-tuple-element.51), channel_id=1, source_target_pairs={{0,24},{8,16},{16,8},{24,0},{1,25},{9,17},{17,9},{25,1},{2,26},{10... | collective-permute-start | bytes 147464 | tf_op jit(solution)/shard_map/ppermute | solution.py:388
  100.2 2.8 %collective-permute-done.41.refs_2_ = f32[96,128]{1,0:T(8,128)S(1)} collective-permute-done((f32[96,128]{1,0:T(8,128)S(1)}, f32[96,128]{1,0:T(8,128)S(1)}, u32[]{:S(2)}, u32[]{:S(2)}) %collective-permute-start.41) | collective-permute-done | bytes 49184 | tf_op jit(solution)/shard_map/ppermute | solution.py:388
  (94 shorter events, 40.2 us)
Async XLA Ops:
  0.6 8.7 %collective-permute-start.1 = (f32[48,96]{1,0:T(8,128)}, f32[48,96]{1,0:T(8,128)S(1)}, u32[]{:S(2)}, u32[]{:S(2)}) collective-permute-start(f32[48,96]{1,0:T(8,128)} %refs_0_.1), channel_id=1, source_target_pairs={{0,16},{8,24},{16,0},{24,8},{1,17},{9,25},{17,1},{25,9},{2,18},{10... | collective-permute-start | bytes 55304 | tf_op jit(solution)/shard_map/ppermute | solution.py:420
  4.8 4.6 %collective-permute-start = (f32[48,96]{1,0:T(8,128)}, f32[48,96]{1,0:T(8,128)S(1)}, u32[]{:S(2)}, u32[]{:S(2)}) collective-permute-start(f32[48,96]{1,0:T(8,128)} %refs_0_.1), channel_id=1, source_target_pairs={{0,24},{8,0},{16,8},{24,16},{1,25},{9,1},{17,9},{25,17},{2,26},{10... | collective-permute-start | bytes 55304 | tf_op jit(solution)/shard_map/ppermute | solution.py:420
  6.1 5.8 %collective-permute-start.2 = (f32[48,96]{1,0:T(8,128)}, f32[48,96]{1,0:T(8,128)S(1)}, u32[]{:S(2)}, u32[]{:S(2)}) collective-permute-start(f32[48,96]{1,0:T(8,128)} %refs_0_.1), channel_id=1, source_target_pairs={{0,8},{8,16},{16,24},{24,0},{1,9},{9,17},{17,25},{25,1},{2,10},{10... | collective-permute-start | bytes 55304 | tf_op jit(solution)/shard_map/ppermute | solution.py:420
  14.5 5.6 %collective-permute-start.4 = (f32[56,384]{1,0:T(8,128)S(1)}, f32[56,384]{1,0:T(8,128)S(1)}, u32[]{:S(2)}, u32[]{:S(2)}) collective-permute-start(f32[56,384]{1,0:T(8,128)S(1)} %get-tuple-element.32), channel_id=1, source_target_pairs={{0,6},{1,7},{2,4},{3,5},{4,2},{5,3},{6,0},{7,1},{8,14},{9,15},{10,... | collective-permute-start | bytes 258056 | tf_op jit(solution)/shard_map/ppermute | solution.py:388
  17.0 4.9 %collective-permute-start.5 = (f32[56,384]{1,0:T(8,128)S(1)}, f32[56,384]{1,0:T(8,128)S(1)}, u32[]{:S(2)}, u32[]{:S(2)}) collective-permute-start(f32[56,384]{1,0:T(8,128)S(1)} %get-tuple-element.33), channel_id=1, source_target_pairs={{0,4},{1,5},{2,6},{3,7},{4,0},{5,1},{6,2},{7,3},{8,12},{9,13},{10,... | collective-permute-start | bytes 258056 | tf_op jit(solution)/shard_map/ppermute | solution.py:388
  17.5 4.5 %collective-permute-start.6 = (f32[56,384]{1,0:T(8,128)S(1)}, f32[56,384]{1,0:T(8,128)S(1)}, u32[]{:S(2)}, u32[]{:S(2)}) collective-permute-start(f32[56,384]{1,0:T(8,128)S(1)} %get-tuple-element.34), channel_id=1, source_target_pairs={{0,2},{1,3},{2,0},{3,1},{4,6},{5,7},{6,4},{7,5},{8,10},{9,11},{10,... | collective-permute-start | bytes 258056 | tf_op jit(solution)/shard_map/ppermute | solution.py:388
  23.8 4.9 %collective-permute-start.9 = (f32[48,384]{1,0:T(8,128)S(1)}, f32[48,384]{1,0:T(8,128)S(1)}, u32[]{:S(2)}, u32[]{:S(2)}) collective-permute-start(f32[48,384]{1,0:T(8,128)S(1)} %update.5.refs_0_.factor_ref), channel_id=1, source_target_pairs={{0,2},{1,3},{2,0},{3,1},{4,6},{5,7},{6,4},{7,5},{8,10},{9,11},{10,... | collective-permute-start | bytes 221192 | tf_op jit(solution)/shard_map/ppermute | solution.py:388
  24.5 5.3 %collective-permute-start.7 = (f32[48,384]{1,0:T(8,128)S(1)}, f32[48,384]{1,0:T(8,128)S(1)}, u32[]{:S(2)}, u32[]{:S(2)}) collective-permute-start(f32[48,384]{1,0:T(8,128)S(1)} %update.5.refs_0_.factor_ref), channel_id=1, source_target_pairs={{0,6},{1,7},{2,4},{3,5},{4,2},{5,3},{6,0},{7,1},{8,14},{9,15},{10,... | collective-permute-start | bytes 221192 | tf_op jit(solution)/shard_map/ppermute | solution.py:388
  26.7 4.6 %collective-permute-start.12 = (f32[48,384]{1,0:T(8,128)S(1)}, f32[48,384]{1,0:T(8,128)S(1)}, u32[]{:S(2)}, u32[]{:S(2)}) collective-permute-start(f32[48,384]{1,0:T(8,128)S(1)} %collective-permute-done.11.refs_2_), channel_id=1, source_target_pairs={{0,1},{1,0},{2,3},{3,2},{4,5},{5,4},{6,7},{7,6},{8,9},{9,8},{10,11... | collective-permute-start | bytes 221192 | tf_op jit(solution)/shard_map/ppermute | solution.py:388
  32.1 5.4 %collective-permute-start.14 = (f32[56,384]{1,0:T(8,128)S(1)}, f32[56,384]{1,0:T(8,128)S(1)}, u32[]{:S(2)}, u32[]{:S(2)}) collective-permute-start(f32[56,384]{1,0:T(8,128)S(1)} %spectra_times_components.8.left_ref), channel_id=1, source_target_pairs={{0,16},{1,9},{2,18},{3,11},{4,20},{5,13},{6,22},{7,15},{8,24},{9,1... | collective-permute-start | bytes 258056 | tf_op jit(solution)/shard_map/ppermute | solution.py:397
  37.6 4.8 %collective-permute-start.15 = (f32[56,384]{1,0:T(8,128)S(1)}, f32[56,384]{1,0:T(8,128)S(1)}, u32[]{:S(2)}, u32[]{:S(2)}) collective-permute-start(f32[56,384]{1,0:T(8,128)S(1)} %add.2.refs_0_), channel_id=1, source_target_pairs={{0,8},{1,17},{2,10},{3,19},{4,12},{5,21},{6,14},{7,23},{8,0},{9,25... | collective-permute-start | bytes 258056 | tf_op jit(solution)/shard_map/ppermute | solution.py:397
  44.9 6.0 %collective-permute-start.17 = (f32[56,384]{1,0:T(8,128)S(1)}, f32[56,384]{1,0:T(8,128)S(1)}, u32[]{:S(2)}, u32[]{:S(2)}) collective-permute-start(f32[56,384]{1,0:T(8,128)S(1)} %get-tuple-element.35), channel_id=1, source_target_pairs={{0,6},{1,7},{2,4},{3,5},{4,2},{5,3},{6,0},{7,1},{8,14},{9,15},{10,... | collective-permute-start | bytes 258056 | tf_op jit(solution)/shard_map/ppermute | solution.py:388
  46.3 6.0 %collective-permute-start.18 = (f32[56,384]{1,0:T(8,128)S(1)}, f32[56,384]{1,0:T(8,128)S(1)}, u32[]{:S(2)}, u32[]{:S(2)}) collective-permute-start(f32[56,384]{1,0:T(8,128)S(1)} %get-tuple-element.36), channel_id=1, source_target_pairs={{0,4},{1,5},{2,6},{3,7},{4,0},{5,1},{6,2},{7,3},{8,12},{9,13},{10,... | collective-permute-start | bytes 258056 | tf_op jit(solution)/shard_map/ppermute | solution.py:388
  54.0 5.1 %collective-permute-start.22 = (f32[48,384]{1,0:T(8,128)S(1)}, f32[48,384]{1,0:T(8,128)S(1)}, u32[]{:S(2)}, u32[]{:S(2)}) collective-permute-start(f32[48,384]{1,0:T(8,128)S(1)} %update.7.refs_0_.factor_ref), channel_id=1, source_target_pairs={{0,2},{1,3},{2,0},{3,1},{4,6},{5,7},{6,4},{7,5},{8,10},{9,11},{10,... | collective-permute-start | bytes 221192 | tf_op jit(solution)/shard_map/ppermute | solution.py:388
  54.7 5.3 %collective-permute-start.20 = (f32[48,384]{1,0:T(8,128)S(1)}, f32[48,384]{1,0:T(8,128)S(1)}, u32[]{:S(2)}, u32[]{:S(2)}) collective-permute-start(f32[48,384]{1,0:T(8,128)S(1)} %update.7.refs_0_.factor_ref), channel_id=1, source_target_pairs={{0,6},{1,7},{2,4},{3,5},{4,2},{5,3},{6,0},{7,1},{8,14},{9,15},{10,... | collective-permute-start | bytes 221192 | tf_op jit(solution)/shard_map/ppermute | solution.py:388
  62.3 5.9 %collective-permute-start.27 = (f32[56,384]{1,0:T(8,128)S(1)}, f32[56,384]{1,0:T(8,128)S(1)}, u32[]{:S(2)}, u32[]{:S(2)}) collective-permute-start(f32[56,384]{1,0:T(8,128)S(1)} %spectra_times_components.11.left_ref), channel_id=1, source_target_pairs={{0,16},{1,9},{2,18},{3,11},{4,20},{5,13},{6,22},{7,15},{8,24},{9,1... | collective-permute-start | bytes 258056 | tf_op jit(solution)/shard_map/ppermute | solution.py:397
  68.1 4.6 %collective-permute-start.28 = (f32[56,384]{1,0:T(8,128)S(1)}, f32[56,384]{1,0:T(8,128)S(1)}, u32[]{:S(2)}, u32[]{:S(2)}) collective-permute-start(f32[56,384]{1,0:T(8,128)S(1)} %add.3.refs_0_), channel_id=1, source_target_pairs={{0,8},{1,17},{2,10},{3,19},{4,12},{5,21},{6,14},{7,23},{8,0},{9,25... | collective-permute-start | bytes 258056 | tf_op jit(solution)/shard_map/ppermute | solution.py:397
  75.3 5.8 %collective-permute-start.30 = (f32[56,384]{1,0:T(8,128)S(1)}, f32[56,384]{1,0:T(8,128)S(1)}, u32[]{:S(2)}, u32[]{:S(2)}) collective-permute-start(f32[56,384]{1,0:T(8,128)S(1)} %get-tuple-element.38), channel_id=1, source_target_pairs={{0,6},{1,7},{2,4},{3,5},{4,2},{5,3},{6,0},{7,1},{8,14},{9,15},{10,... | collective-permute-start | bytes 258056 | tf_op jit(solution)/shard_map/ppermute | solution.py:388
  77.0 5.7 %collective-permute-start.31 = (f32[56,384]{1,0:T(8,128)S(1)}, f32[56,384]{1,0:T(8,128)S(1)}, u32[]{:S(2)}, u32[]{:S(2)}) collective-permute-start(f32[56,384]{1,0:T(8,128)S(1)} %get-tuple-element.39), channel_id=1, source_target_pairs={{0,4},{1,5},{2,6},{3,7},{4,0},{5,1},{6,2},{7,3},{8,12},{9,13},{10,... | collective-permute-start | bytes 258056 | tf_op jit(solution)/shard_map/ppermute | solution.py:388
  84.5 5.1 %collective-permute-start.35 = (f32[48,384]{1,0:T(8,128)S(1)}, f32[48,384]{1,0:T(8,128)S(1)}, u32[]{:S(2)}, u32[]{:S(2)}) collective-permute-start(f32[48,384]{1,0:T(8,128)S(1)} %update.9.refs_0_.h_ref), channel_id=1, source_target_pairs={{0,2},{1,3},{2,0},{3,1},{4,6},{5,7},{6,4},{7,5},{8,10},{9,11},{10,... | collective-permute-start | bytes 221192 | tf_op jit(solution)/shard_map/ppermute | solution.py:388
  85.2 5.3 %collective-permute-start.33 = (f32[48,384]{1,0:T(8,128)S(1)}, f32[48,384]{1,0:T(8,128)S(1)}, u32[]{:S(2)}, u32[]{:S(2)}) collective-permute-start(f32[48,384]{1,0:T(8,128)S(1)} %update.9.refs_0_.h_ref), channel_id=1, source_target_pairs={{0,6},{1,7},{2,4},{3,5},{4,2},{5,3},{6,0},{7,1},{8,14},{9,15},{10,... | collective-permute-start | bytes 221192 | tf_op jit(solution)/shard_map/ppermute | solution.py:388
  87.5 6.4 %collective-permute-start.38 = (f32[48,384]{1,0:T(8,128)S(1)}, f32[48,384]{1,0:T(8,128)S(1)}, u32[]{:S(2)}, u32[]{:S(2)}) collective-permute-start(f32[48,384]{1,0:T(8,128)S(1)} %collective-permute-done.37.refs_2_), channel_id=1, source_target_pairs={{0,1},{1,0},{2,3},{3,2},{4,5},{5,4},{6,7},{7,6},{8,9},{9,8},{10,11... | collective-permute-start | bytes 221192 | tf_op jit(solution)/shard_map/ppermute | solution.py:388
  95.9 7.2 %collective-permute-start.41 = (f32[96,128]{1,0:T(8,128)S(1)}, f32[96,128]{1,0:T(8,128)S(1)}, u32[]{:S(2)}, u32[]{:S(2)}) collective-permute-start(f32[96,128]{1,0:T(8,128)S(1)} %get-tuple-element.50), channel_id=1, source_target_pairs={{0,16},{8,24},{16,0},{24,8},{1,17},{9,25},{17,1},{25,9},{2,18},{10... | collective-permute-start | bytes 147464 | tf_op jit(solution)/shard_map/ppermute | solution.py:388
  97.8 5.9 %collective-permute-start.42 = (f32[96,128]{1,0:T(8,128)S(1)}, f32[96,128]{1,0:T(8,128)S(1)}, u32[]{:S(2)}, u32[]{:S(2)}) collective-permute-start(f32[96,128]{1,0:T(8,128)S(1)} %get-tuple-element.51), channel_id=1, source_target_pairs={{0,24},{8,16},{16,8},{24,0},{1,25},{9,17},{17,9},{25,1},{2,26},{10... | collective-permute-start | bytes 147464 | tf_op jit(solution)/shard_map/ppermute | solution.py:388
  (21 other events, 84.4 us)

commit v4 on v3

--- a/solution.py
+++ b/solution.py
@@ -195,22 +195,6 @@
         cost_estimate=cost(12 * rank * rank * width, 4 * rank * width * (2 + len(parts))),
         name="update",
     )(factor, *parts)
-
-
-def add_kernel(left_ref, right_ref, out_ref):
-    out_ref[...] = left_ref[...] + right_ref[...]
-
-
-def add_call(left, right):
-    return pl.pallas_call(
-        add_kernel,
-        in_specs=vmem(2),
-        out_specs=pl.BlockSpec(memory_space=pltpu.VMEM),
-        out_shape=jax.ShapeDtypeStruct(left.shape, F32),
-        compiler_params=params(),
-        cost_estimate=cost(left.size, 12 * left.size),
-        name="add",
-    )(left, right)
 
 
 def gather_kernel(relatives, carried, high_ref, low_ref, *refs):
@@ -258,15 +242,15 @@
     carried, refs = ((), refs) if first else (refs[:3], refs[3:])
     rank, width = pieces[0].shape
     pixels = w_ref.shape[1]
-    w_t = w_ref[...].T
-    w0, w1, w2 = thirds(w_t)
+    span = pixels // groups
+    w = w_ref[...]
+    w0, w1, w2 = thirds(w.T)
     left = jnp.concatenate([w0, w0, w1, w1, w2], axis=1)
-    half = LANES // 2
-    front = jnp.zeros((half, width), BF16)
-    back = jnp.zeros((half - rank, width), BF16)
+    front = jnp.zeros((span, width), BF16)
+    back = jnp.zeros((2 * LANES - span - rank, width), BF16)
     sums = [ref[...] for ref in carried] if carried else [None] * 3
     for relative, piece in zip(relatives, pieces):
-        h0, h1, _ = thirds(piece[...])
+        h0, h1 = split(piece[...])
         right = jnp.concatenate([h0, h1, h0, h1, h0], axis=0)
         d = s_ref[:, bins_of(relative, width)] - fast(left, right, NN)
         stack = jnp.concatenate([h0, h1], axis=0)
@@ -289,79 +273,82 @@
         for ref, value in zip(refs, sums):
             ref[...] = value
         return
-    outs, own_ref, scratch, w_scratch = refs[:groups], refs[groups], refs[-2], refs[-1]
-    tall = jnp.concatenate([error, jnp.zeros((LANES - rank, pixels), F32)], axis=0)
-    lane = lax.broadcasted_iota(jnp.int32, (pixels, LANES), 1)
-    scratch[...] = jnp.where(lane == rank, jnp.sum(folded, axis=1, keepdims=True), tall.T)
-    w_scratch[...] = w_t
-    rows = pixels // groups
+    outs, own_ref = refs[:groups], refs[groups]
+    squares = exact(jnp.ones((SUBLANES, LANES), F32), folded, NT)
+    table = jnp.concatenate([error, squares, w], axis=0)
     me = lax.axis_index("mz")
+    free = LANES - span
+    lane = lax.broadcasted_iota(jnp.int32, (rank, LANES), 1)
     for relative, out in enumerate(outs):
         group = jnp.bitwise_xor(me, relative)
-        out[...] = scratch[pl.ds(pl.multiple_of(group * rows, SUBLANES), rows), :]
-        out[:rank, :] += gram
-    own_ref[...] = w_scratch[pl.ds(pl.multiple_of(me * rows, SUBLANES), rows), :]
+        here = pltpu.roll(table, lax.rem(groups - group, groups) * span, 1)[:, :LANES]
+        out[:rank, :] = jnp.where(lane < span, here[:rank], gram[:, :LANES])
+        out[rank : rank + SUBLANES, :] = here[rank : rank + SUBLANES]
+        out[rank + SUBLANES :, :] = jnp.zeros((SUBLANES, LANES), F32)
+        rest = rank - free
+        for index in range(rank // SUBLANES):
+            rows = slice(index * SUBLANES, (index + 1) * SUBLANES)
+            out[rank + SUBLANES :, index * rest : (index + 1) * rest] = gram[rows, LANES : LANES + rest]
+        if relative == 0:
+            own_ref[...] = here[rank + SUBLANES :, :span]
 
 
 def final_gather_call(relatives, groups, pieces, spectra, w_block, before, last):
     rank, width = pieces[0].shape
     pixels = w_block.shape[1]
-    rows = pixels // groups
     count = len(relatives)
     first = before is None
     extra = () if first else tuple(before)
-    shapes = [(rank, pixels), (pixels, LANES), (rank, LANES)]
-    scratch = []
+    shapes = [(rank, pixels), (pixels, LANES), (rank, 2 * LANES)]
     if last:
-        shapes = [(rows, LANES)] * groups + [(rows, rank)]
-        scratch = [pltpu.VMEM((pixels, LANES), F32), pltpu.VMEM((pixels, rank), F32)]
+        shapes = [(rank + 2 * SUBLANES, LANES)] * groups + [(rank, pixels // groups)]
     return pl.pallas_call(
         functools.partial(final_gather_kernel, relatives, groups, first, last),
         in_specs=vmem(2 + count + len(extra)),
         out_specs=vmem(len(shapes)),
         out_shape=[jax.ShapeDtypeStruct(shape, F32) for shape in shapes],
-        scratch_shapes=scratch,
         compiler_params=params(),
         cost_estimate=cost(18 * rank * pixels * width * count, 8 * pixels * width * count),
         name="final_products",
     )(spectra, w_block, *pieces, *extra)
 
 
-def final_kernel(w_t_ref, h_ref, *refs):
+def final_kernel(w_ref, h_ref, *refs):
     parts, (w_out, h_out, misfit_out) = refs[:-3], refs[-3:]
     h_out[...] = h_ref[...]
-    w_t = w_t_ref[...]
-    _, rank = w_t.shape
+    w = w_ref[...]
+    rank, span = w.shape
     total = parts[0][...]
     for part in parts[1:]:
         total = total + part[...]
-    gram = total[:rank, LANES // 2 : LANES // 2 + rank]
-    err = total[:, :rank]
-    den = exact(w_t, gram, NN)
-    new = w_t * (err + den) / den
-    w_out[...] = new.T
-    step = new - w_t
-    change = step * (exact(step, gram, NN) - 2.0 * err)
-    pick = (lax.broadcasted_iota(jnp.int32, (SUBLANES, LANES), 1) == rank).astype(F32)
-    misfit = exact(pick, total, NT) + exact(jnp.ones((SUBLANES, rank), F32), change, NT)
-    misfit_out[...] = misfit[:1]
-
-
-def final_call(w_t, h_piece, *parts):
-    rows, rank = w_t.shape
+    rest = rank - (LANES - span)
+    low = total[rank + SUBLANES :]
+    tail = [low[:, index * rest : (index + 1) * rest] for index in range(rank // SUBLANES)]
+    gram = jnp.concatenate([total[:rank, span:], jnp.concatenate(tail, axis=0)], axis=1)
+    error = total[:rank, :span]
+    den = exact(gram, w, NN)
+    new = w * (error + den) / den
+    w_out[...] = new
+    step = new - w
+    change = step * (exact(gram, step, NN) - 2.0 * error)
+    misfit_out[...] = total[rank : rank + 1, :span] + jnp.sum(change, axis=0, keepdims=True)
+
+
+def final_call(w_piece, h_piece, *parts):
+    rank, span = w_piece.shape
     return pl.pallas_call(
         final_kernel,
         in_specs=vmem(2 + len(parts)),
         out_specs=vmem(3),
         out_shape=[
-            jax.ShapeDtypeStruct((rank, rows), F32),
+            jax.ShapeDtypeStruct((rank, span), F32),
             jax.ShapeDtypeStruct(h_piece.shape, F32),
-            jax.ShapeDtypeStruct((1, rows), F32),
+            jax.ShapeDtypeStruct((1, span), F32),
         ],
         compiler_params=params(),
-        cost_estimate=cost(24 * rank * rank * rows, 4 * rows * LANES * len(parts)),
+        cost_estimate=cost(24 * rank * rank * span, 4 * rank * LANES * len(parts)),
         name="final_update",
-    )(w_t, h_piece, *parts)
+    )(w_piece, h_piece, *parts)
 
 
 def join_kernel(*refs):
@@ -422,7 +409,9 @@
         ],
     )
     evens = list(range(owners - 2, 0, -2))
-    masks = [1 << bit for bit in range(groups.bit_length() - 1)]
+    steps = [(1, 1)]
+    if groups > 2:
+        steps = [*[(k, k) for k in range(groups - 1, 2, -1)], (1, 2), (2, 1)]
     for iteration in range(ITERS):
         theirs = scatter_call(list(range(1, owners, 2)), width, w_block, high, low)
         other = swap(theirs, "px", owners, 1)
@@ -436,11 +425,10 @@
                 owners,
                 lambda relatives, pieces, before, last: gather_call(relatives, pieces, high, low, before),
             )
-            for even, odd in zip(masks[:-1], masks[:0:-1]):
-                total = add_call(total, cross(total, groups, owners, even, odd))
-            w_block = update_call(
-                w_block, (), (total, cross(total, groups, owners, masks[-1], masks[0]))
-            )
+            sent = []
+            for even, odd in steps:
+                sent.append(cross(total, groups, owners, even, odd))
+            w_block = update_call(w_block, (), (total, *sent))
         else:
             parts = spread(
                 h_piece,
@@ -449,7 +437,9 @@
                     relatives, groups, pieces, copy, w_block, before, last
                 ),
             )
-            sent = [swap(parts[k], "mz", groups, k) for k in range(1, groups)]
+            sent = []
+            for k in [*range(2, groups), 1]:
+                sent.append(swap(parts[k], "mz", groups, k))
             w_final, h_final, misfit = final_call(parts[groups], h_piece, parts[0], *sent)
     return w_final, h_final, misfit.reshape(-1)
 
@@ -469,8 +459,9 @@
         and w_piece.shape[1] % SUBLANES == 0
         and rank % (2 * SUBLANES) == 0
         and rank // SUBLANES * rank <= min(width, pixels)
-        and rank < LANES // 2
-        and rank <= w_piece.shape[1]
+        and w_piece.shape[1] < LANES
+        and LANES - w_piece.shape[1] < rank
+        and (rank - LANES + w_piece.shape[1]) * (rank // SUBLANES) <= LANES
     )
     if fits:
         return fast_device(groups, owners, spectra, w_piece, h_piece)

time: 105 us -> 105 us (level)
  waiting for transfers between devices: 52.4 us -> 44.5 us
  starting transfers between devices: 32.9 us -> 40.5 us
    ppermute x4 -> x6, waiting for transfers between devices: 19.8 us -> 11.5 us  [cross(): return lax.ppermute(value, ('mz', 'px'), pairs)]
    ppermute x4 -> x6, starting transfers between devices: 0.75 us -> 8.86 us  [cross(): return lax.ppermute(value, ('mz', 'px'), pairs)]
  transfers between devices with their start and end apart: 43 -> 45, of which waited for: 27 -> 28; matrix products, arithmetic and copies ran while one was open for 0% -> 0% of each run, Pallas kernels for 10% -> 10%
where the time goes in v4:
time: 105 us
  waiting for transfers between devices  44.5 us (42%)
  starting transfers between devices  40.5 us (39%)
  Pallas kernels  18.6 us (18%)
    ppermute x36, waiting for transfers between devices, swap(): return lax.ppermute(value, axis, [(i, i ^ mask) for i in range(size)])  30.4 us
    ppermute x36, starting transfers between devices, swap(): return lax.ppermute(value, axis, [(i, i ^ mask) for i in range(size)])  25.5 us
    ppermute x6, waiting for transfers between devices, cross(): return lax.ppermute(value, ('mz', 'px'), pairs)  11.5 us
    ppermute x6, starting transfers between devices, cross(): return lax.ppermute(value, ('mz', 'px'), pairs)  8.86 us
    ppermute x3, starting transfers between devices, fast_device(): lax.ppermute(w_piece, 'mz', [(i, (i - k) % groups) for i in range(groups)])  6.16 us
    pallas_call x3, Pallas kernels, final_gather_call(): pl.pallas_call(functools.partial(final_gather_kernel, relatives, groups,...  5.42 us
    pallas_call x6, Pallas kernels, gather_call(): pl.pallas_call(functools.partial(gather_kernel, relatives, before is not...  4.66 us
    pallas_call x6, Pallas kernels, scatter_call(): pl.pallas_call(functools.partial(scatter_kernel, relatives, width), in_sp...  3.36 us
  transfers between devices with their start and end apart: 45, of which 28 were waited for; matrix products, arithmetic and copies ran while one was open for 0% of the time, Pallas kernels for 10%

profile of v4, /device:TPU:0, one launch (start us, length us, event | category | flops | bytes accessed | tf_op | source)
XLA Modules:
  0.0 104.5 jit_solution(17149343227459530089)
XLA Ops:
  0.6 4.1 %collective-permute-start.1 = (f32[48,96]{1,0:T(8,128)}, f32[48,96]{1,0:T(8,128)S(1)}, u32[]{:S(2)}, u32[]{:S(2)}) collective-permute-start(f32[48,96]{1,0:T(8,128)} %refs_0_.1), channel_id=1, source_target_pairs={{0,16},{8,24},{16,0},{24,8},{1,17},{9,25},{17,1},{25,9},{2,18},{10... | collective-permute-start | bytes 55304 | tf_op jit(solution)/shard_map/ppermute | solution.py:407
  6.8 2.5 %split_spectra.1 = (f32[384,3072]{1,0:T(8,128)S(1)}, bf16[384,3072]{1,0:T(8,128)(2,1)S(1)}, bf16[384,3072]{1,0:T(8,128)(2,1)S(1)}) custom-call(f32[384,3072]{1,0:T(8,128)} %s_ref.1), custom_call_target="tpu_custom_call" | custom-call | flops 4718592 | bytes 14155776 | tf_op jit(solution)/shard_map/split_spectra/pallas_call | solution.py:110
  9.3 2.6 %collective-permute-done.2.refs_3_ = f32[48,96]{1,0:T(8,128)S(1)} collective-permute-done((f32[48,96]{1,0:T(8,128)}, f32[48,96]{1,0:T(8,128)S(1)}, u32[]{:S(2)}, u32[]{:S(2)}) %collective-permute-start.2) | collective-permute-done | bytes 18464 | tf_op jit(solution)/shard_map/ppermute | solution.py:407
  14.5 2.5 %collective-permute-start.4 = (f32[56,384]{1,0:T(8,128)S(1)}, f32[56,384]{1,0:T(8,128)S(1)}, u32[]{:S(2)}, u32[]{:S(2)}) collective-permute-start(f32[56,384]{1,0:T(8,128)S(1)} %get-tuple-element.32), channel_id=1, source_target_pairs={{0,6},{1,7},{2,4},{3,5},{4,2},{5,3},{6,0},{7,1},{8,14},{9,15},{10,... | collective-permute-start | bytes 258056 | tf_op jit(solution)/shard_map/ppermute | solution.py:375
  18.0 2.0 %collective-permute-done.4.refs_2_ = f32[56,384]{1,0:T(8,128)S(1)} collective-permute-done((f32[56,384]{1,0:T(8,128)S(1)}, f32[56,384]{1,0:T(8,128)S(1)}, u32[]{:S(2)}, u32[]{:S(2)}) %collective-permute-start.4) | collective-permute-done | bytes 86048 | tf_op jit(solution)/shard_map/ppermute | solution.py:375
  20.1 1.8 %collective-permute-done.5.refs_3_ = f32[56,384]{1,0:T(8,128)S(1)} collective-permute-done((f32[56,384]{1,0:T(8,128)S(1)}, f32[56,384]{1,0:T(8,128)S(1)}, u32[]{:S(2)}, u32[]{:S(2)}) %collective-permute-start.5) | collective-permute-done | bytes 86048 | tf_op jit(solution)/shard_map/ppermute | solution.py:375
  22.3 1.6 %collective-permute-start.11 = (f32[48,384]{1,0:T(8,128)S(1)}, f32[48,384]{1,0:T(8,128)S(1)}, u32[]{:S(2)}, u32[]{:S(2)}) collective-permute-start(f32[48,384]{1,0:T(8,128)S(1)} %update.5.refs_0_.factor_ref), channel_id=1, source_target_pairs={{0,4},{1,5},{2,6},{3,7},{4,0},{5,1},{6,2},{7,3},{8,12},{9,13},{10,... | collective-permute-start | bytes 221192 | tf_op jit(solution)/shard_map/ppermute | solution.py:375
  26.7 2.1 %collective-permute-done.9.refs_1_ = f32[48,384]{1,0:T(8,128)S(1)} collective-permute-done((f32[48,384]{1,0:T(8,128)S(1)}, f32[48,384]{1,0:T(8,128)S(1)}, u32[]{:S(2)}, u32[]{:S(2)}) %collective-permute-start.9) | collective-permute-done | bytes 73760 | tf_op jit(solution)/shard_map/ppermute | solution.py:375
  33.3 3.3 %collective-permute-start.14 = (f32[56,384]{1,0:T(8,128)S(1)}, f32[56,384]{1,0:T(8,128)S(1)}, u32[]{:S(2)}, u32[]{:S(2)}) collective-permute-start(f32[56,384]{1,0:T(8,128)S(1)} %spectra_times_components.8.refs_0_), channel_id=1, source_target_pairs={{0,24},{1,25},{2,26},{3,27},{4,28},{5,29},{6,30},{7,31},{8,16},{9,... | collective-permute-start | bytes 258056 | tf_op jit(solution)/shard_map/ppermute | solution.py:384
  36.6 2.7 %collective-permute-done.16.refs_3_ = f32[56,384]{1,0:T(8,128)S(1)} collective-permute-done((f32[56,384]{1,0:T(8,128)S(1)}, f32[56,384]{1,0:T(8,128)S(1)}, u32[]{:S(2)}, u32[]{:S(2)}) %collective-permute-start.16) | collective-permute-done | bytes 86048 | tf_op jit(solution)/shard_map/ppermute | solution.py:384
  39.3 2.1 %collective-permute-done.15.refs_2_ = f32[56,384]{1,0:T(8,128)S(1)} collective-permute-done((f32[56,384]{1,0:T(8,128)S(1)}, f32[56,384]{1,0:T(8,128)S(1)}, u32[]{:S(2)}, u32[]{:S(2)}) %collective-permute-start.15) | collective-permute-done | bytes 86048 | tf_op jit(solution)/shard_map/ppermute | solution.py:384
  47.5 2.5 %collective-permute-done.18.refs_2_ = f32[56,384]{1,0:T(8,128)S(1)} collective-permute-done((f32[56,384]{1,0:T(8,128)S(1)}, f32[56,384]{1,0:T(8,128)S(1)}, u32[]{:S(2)}, u32[]{:S(2)}) %collective-permute-start.18) | collective-permute-done | bytes 86048 | tf_op jit(solution)/shard_map/ppermute | solution.py:375
  56.1 2.1 %collective-permute-done.23.refs_1_ = f32[48,384]{1,0:T(8,128)S(1)} collective-permute-done((f32[48,384]{1,0:T(8,128)S(1)}, f32[48,384]{1,0:T(8,128)S(1)}, u32[]{:S(2)}, u32[]{:S(2)}) %collective-permute-start.23) | collective-permute-done | bytes 73760 | tf_op jit(solution)/shard_map/ppermute | solution.py:375
  61.3 1.9 %collective-permute-start.30 = (f32[56,384]{1,0:T(8,128)S(1)}, f32[56,384]{1,0:T(8,128)S(1)}, u32[]{:S(2)}, u32[]{:S(2)}) collective-permute-start(f32[56,384]{1,0:T(8,128)S(1)} %spectra_times_components.11.refs_0_), channel_id=1, source_target_pairs={{0,8},{1,17},{2,10},{3,19},{4,12},{5,21},{6,14},{7,23},{8,0},{9,25... | collective-permute-start | bytes 258056 | tf_op jit(solution)/shard_map/ppermute | solution.py:384
  63.4 2.3 %collective-permute-start.28 = (f32[56,384]{1,0:T(8,128)S(1)}, f32[56,384]{1,0:T(8,128)S(1)}, u32[]{:S(2)}, u32[]{:S(2)}) collective-permute-start(f32[56,384]{1,0:T(8,128)S(1)} %spectra_times_components.11.refs_0_), channel_id=1, source_target_pairs={{0,24},{1,25},{2,26},{3,27},{4,28},{5,29},{6,30},{7,31},{8,16},{9,... | collective-permute-start | bytes 258056 | tf_op jit(solution)/shard_map/ppermute | solution.py:384
  67.1 5.3 %collective-permute-done.29.refs_2_ = f32[56,384]{1,0:T(8,128)S(1)} collective-permute-done((f32[56,384]{1,0:T(8,128)S(1)}, f32[56,384]{1,0:T(8,128)S(1)}, u32[]{:S(2)}, u32[]{:S(2)}) %collective-permute-start.29) | collective-permute-done | bytes 86048 | tf_op jit(solution)/shard_map/ppermute | solution.py:384
  75.0 1.7 %collective-permute-start.32 = (f32[56,384]{1,0:T(8,128)S(1)}, f32[56,384]{1,0:T(8,128)S(1)}, u32[]{:S(2)}, u32[]{:S(2)}) collective-permute-start(f32[56,384]{1,0:T(8,128)S(1)} %get-tuple-element.38), channel_id=1, source_target_pairs={{0,6},{1,7},{2,4},{3,5},{4,2},{5,3},{6,0},{7,1},{8,14},{9,15},{10,... | collective-permute-start | bytes 258056 | tf_op jit(solution)/shard_map/ppermute | solution.py:375
  78.6 2.2 %collective-permute-done.32.refs_2_ = f32[56,384]{1,0:T(8,128)S(1)} collective-permute-done((f32[56,384]{1,0:T(8,128)S(1)}, f32[56,384]{1,0:T(8,128)S(1)}, u32[]{:S(2)}, u32[]{:S(2)}) %collective-permute-start.32) | collective-permute-done | bytes 86048 | tf_op jit(solution)/shard_map/ppermute | solution.py:375
  80.8 1.6 %collective-permute-done.33.refs_3_ = f32[56,384]{1,0:T(8,128)S(1)} collective-permute-done((f32[56,384]{1,0:T(8,128)S(1)}, f32[56,384]{1,0:T(8,128)S(1)}, u32[]{:S(2)}, u32[]{:S(2)}) %collective-permute-start.33) | collective-permute-done | bytes 86048 | tf_op jit(solution)/shard_map/ppermute | solution.py:375
  87.2 2.1 %collective-permute-done.37.refs_1_ = f32[48,384]{1,0:T(8,128)S(1)} collective-permute-done((f32[48,384]{1,0:T(8,128)S(1)}, f32[48,384]{1,0:T(8,128)S(1)}, u32[]{:S(2)}, u32[]{:S(2)}) %collective-permute-start.37) | collective-permute-done | bytes 73760 | tf_op jit(solution)/shard_map/ppermute | solution.py:375
  91.6 2.0 %final_products.4 = (f32[48,384]{1,0:T(8,128)S(1)}, f32[384,128]{1,0:T(8,128)S(1)}, f32[48,256]{1,0:T(8,128)S(1)}) custom-call(f32[384,3072]{1,0:T(8,128)S(1)} %get-tuple-element.29.s_ref, f32[48,384]{1,0:T(8,128)S(1)} %update.8.w_ref, f32[48,384]{1,0:T(8,128)S(1)} %collective-permute-done.35.refs_0_, f32[48,384]{1,0:T(8,128)S(1)} %collective-permute-done.37.refs_1_, ...), custom_call_target="tpu_custom_call" | custom-call | flops 382205952 | bytes 3538944 | tf_op jit(solution)/shard_map/final_products/pallas_call | solution.py:305
  93.6 2.1 %final_products.5 = (f32[64,128]{1,0:T(8,128)S(1)}, f32[64,128]{1,0:T(8,128)S(1)}, f32[64,128]{1,0:T(8,128)S(1)}, f32[64,128]{1,0:T(8,128)S(1)}, f32[48,96]{1,0:T(8,128)S(1)}) custom-call(f32[384,3072]{1,0:T(8,128)S(1)} %get-tuple-element.29.s_ref, f32[48,384]{1,0:T(8,128)S(1)} %update.8.w_ref, f32[48,384]{1,0:T(8,128)S(1)} %collective-permute-done.36.refs_0_, ...), custom_call_target="tpu_custom_call" | custom-call | flops 382205952 | bytes 3538944 | tf_op jit(solution)/shard_map/final_products/pallas_call | solution.py:305
  97.2 2.4 %collective-permute-start.43 = (f32[64,128]{1,0:T(8,128)S(1)}, f32[64,128]{1,0:T(8,128)S(1)}, u32[]{:S(2)}, u32[]{:S(2)}) collective-permute-start(f32[64,128]{1,0:T(8,128)S(1)} %get-tuple-element.50), channel_id=1, source_target_pairs={{0,24},{8,16},{16,8},{24,0},{1,25},{9,17},{17,9},{25,1},{2,26},{10... | collective-permute-start | bytes 98312 | tf_op jit(solution)/shard_map/ppermute | solution.py:375
  99.6 1.9 %collective-permute-done.42.refs_1_ = f32[64,128]{1,0:T(8,128)S(1)} collective-permute-done((f32[64,128]{1,0:T(8,128)S(1)}, f32[64,128]{1,0:T(8,128)S(1)}, u32[]{:S(2)}, u32[]{:S(2)}) %collective-permute-start.42) | collective-permute-done | bytes 32800 | tf_op jit(solution)/shard_map/ppermute | solution.py:375
  (96 shorter events, 46.1 us)
Async XLA Ops:
  0.6 8.7 %collective-permute-start.1 = (f32[48,96]{1,0:T(8,128)}, f32[48,96]{1,0:T(8,128)S(1)}, u32[]{:S(2)}, u32[]{:S(2)}) collective-permute-start(f32[48,96]{1,0:T(8,128)} %refs_0_.1), channel_id=1, source_target_pairs={{0,16},{8,24},{16,0},{24,8},{1,17},{9,25},{17,1},{25,9},{2,18},{10... | collective-permute-start | bytes 55304 | tf_op jit(solution)/shard_map/ppermute | solution.py:407
  6.1 5.8 %collective-permute-start.2 = (f32[48,96]{1,0:T(8,128)}, f32[48,96]{1,0:T(8,128)S(1)}, u32[]{:S(2)}, u32[]{:S(2)}) collective-permute-start(f32[48,96]{1,0:T(8,128)} %refs_0_.1), channel_id=1, source_target_pairs={{0,8},{8,16},{16,24},{24,0},{1,9},{9,17},{17,25},{25,1},{2,10},{10... | collective-permute-start | bytes 55304 | tf_op jit(solution)/shard_map/ppermute | solution.py:407
  14.5 5.6 %collective-permute-start.4 = (f32[56,384]{1,0:T(8,128)S(1)}, f32[56,384]{1,0:T(8,128)S(1)}, u32[]{:S(2)}, u32[]{:S(2)}) collective-permute-start(f32[56,384]{1,0:T(8,128)S(1)} %get-tuple-element.32), channel_id=1, source_target_pairs={{0,6},{1,7},{2,4},{3,5},{4,2},{5,3},{6,0},{7,1},{8,14},{9,15},{10,... | collective-permute-start | bytes 258056 | tf_op jit(solution)/shard_map/ppermute | solution.py:375
  17.0 4.9 %collective-permute-start.5 = (f32[56,384]{1,0:T(8,128)S(1)}, f32[56,384]{1,0:T(8,128)S(1)}, u32[]{:S(2)}, u32[]{:S(2)}) collective-permute-start(f32[56,384]{1,0:T(8,128)S(1)} %get-tuple-element.33), channel_id=1, source_target_pairs={{0,4},{1,5},{2,6},{3,7},{4,0},{5,1},{6,2},{7,3},{8,12},{9,13},{10,... | collective-permute-start | bytes 258056 | tf_op jit(solution)/shard_map/ppermute | solution.py:375
  23.8 4.9 %collective-permute-start.9 = (f32[48,384]{1,0:T(8,128)S(1)}, f32[48,384]{1,0:T(8,128)S(1)}, u32[]{:S(2)}, u32[]{:S(2)}) collective-permute-start(f32[48,384]{1,0:T(8,128)S(1)} %update.5.refs_0_.factor_ref), channel_id=1, source_target_pairs={{0,2},{1,3},{2,0},{3,1},{4,6},{5,7},{6,4},{7,5},{8,10},{9,11},{10,... | collective-permute-start | bytes 221192 | tf_op jit(solution)/shard_map/ppermute | solution.py:375
  24.5 5.3 %collective-permute-start.7 = (f32[48,384]{1,0:T(8,128)S(1)}, f32[48,384]{1,0:T(8,128)S(1)}, u32[]{:S(2)}, u32[]{:S(2)}) collective-permute-start(f32[48,384]{1,0:T(8,128)S(1)} %update.5.refs_0_.factor_ref), channel_id=1, source_target_pairs={{0,6},{1,7},{2,4},{3,5},{4,2},{5,3},{6,0},{7,1},{8,14},{9,15},{10,... | collective-permute-start | bytes 221192 | tf_op jit(solution)/shard_map/ppermute | solution.py:375
  26.7 4.6 %collective-permute-start.12 = (f32[48,384]{1,0:T(8,128)S(1)}, f32[48,384]{1,0:T(8,128)S(1)}, u32[]{:S(2)}, u32[]{:S(2)}) collective-permute-start(f32[48,384]{1,0:T(8,128)S(1)} %collective-permute-done.11.refs_2_), channel_id=1, source_target_pairs={{0,1},{1,0},{2,3},{3,2},{4,5},{5,4},{6,7},{7,6},{8,9},{9,8},{10,11... | collective-permute-start | bytes 221192 | tf_op jit(solution)/shard_map/ppermute | solution.py:375
  32.1 7.2 %collective-permute-start.16 = (f32[56,384]{1,0:T(8,128)S(1)}, f32[56,384]{1,0:T(8,128)S(1)}, u32[]{:S(2)}, u32[]{:S(2)}) collective-permute-start(f32[56,384]{1,0:T(8,128)S(1)} %spectra_times_components.8.refs_0_), channel_id=1, source_target_pairs={{0,8},{1,17},{2,10},{3,19},{4,12},{5,21},{6,14},{7,23},{8,0},{9,25... | collective-permute-start | bytes 258056 | tf_op jit(solution)/shard_map/ppermute | solution.py:384
  32.2 9.2 %collective-permute-start.15 = (f32[56,384]{1,0:T(8,128)S(1)}, f32[56,384]{1,0:T(8,128)S(1)}, u32[]{:S(2)}, u32[]{:S(2)}) collective-permute-start(f32[56,384]{1,0:T(8,128)S(1)} %spectra_times_components.8.refs_0_), channel_id=1, source_target_pairs={{0,16},{1,9},{2,18},{3,11},{4,20},{5,13},{6,22},{7,15},{8,24},{9,1... | collective-permute-start | bytes 258056 | tf_op jit(solution)/shard_map/ppermute | solution.py:384
  33.3 8.1 %collective-permute-start.14 = (f32[56,384]{1,0:T(8,128)S(1)}, f32[56,384]{1,0:T(8,128)S(1)}, u32[]{:S(2)}, u32[]{:S(2)}) collective-permute-start(f32[56,384]{1,0:T(8,128)S(1)} %spectra_times_components.8.refs_0_), channel_id=1, source_target_pairs={{0,24},{1,25},{2,26},{3,27},{4,28},{5,29},{6,30},{7,31},{8,16},{9,... | collective-permute-start | bytes 258056 | tf_op jit(solution)/shard_map/ppermute | solution.py:384
  44.0 6.1 %collective-permute-start.18 = (f32[56,384]{1,0:T(8,128)S(1)}, f32[56,384]{1,0:T(8,128)S(1)}, u32[]{:S(2)}, u32[]{:S(2)}) collective-permute-start(f32[56,384]{1,0:T(8,128)S(1)} %get-tuple-element.35), channel_id=1, source_target_pairs={{0,6},{1,7},{2,4},{3,5},{4,2},{5,3},{6,0},{7,1},{8,14},{9,15},{10,... | collective-permute-start | bytes 258056 | tf_op jit(solution)/shard_map/ppermute | solution.py:375
  45.4 6.0 %collective-permute-start.19 = (f32[56,384]{1,0:T(8,128)S(1)}, f32[56,384]{1,0:T(8,128)S(1)}, u32[]{:S(2)}, u32[]{:S(2)}) collective-permute-start(f32[56,384]{1,0:T(8,128)S(1)} %get-tuple-element.36), channel_id=1, source_target_pairs={{0,4},{1,5},{2,6},{3,7},{4,0},{5,1},{6,2},{7,3},{8,12},{9,13},{10,... | collective-permute-start | bytes 258056 | tf_op jit(solution)/shard_map/ppermute | solution.py:375
  53.0 5.1 %collective-permute-start.23 = (f32[48,384]{1,0:T(8,128)S(1)}, f32[48,384]{1,0:T(8,128)S(1)}, u32[]{:S(2)}, u32[]{:S(2)}) collective-permute-start(f32[48,384]{1,0:T(8,128)S(1)} %update.7.refs_0_.factor_ref), channel_id=1, source_target_pairs={{0,2},{1,3},{2,0},{3,1},{4,6},{5,7},{6,4},{7,5},{8,10},{9,11},{10,... | collective-permute-start | bytes 221192 | tf_op jit(solution)/shard_map/ppermute | solution.py:375
  53.7 5.3 %collective-permute-start.21 = (f32[48,384]{1,0:T(8,128)S(1)}, f32[48,384]{1,0:T(8,128)S(1)}, u32[]{:S(2)}, u32[]{:S(2)}) collective-permute-start(f32[48,384]{1,0:T(8,128)S(1)} %update.7.refs_0_.factor_ref), channel_id=1, source_target_pairs={{0,6},{1,7},{2,4},{3,5},{4,2},{5,3},{6,0},{7,1},{8,14},{9,15},{10,... | collective-permute-start | bytes 221192 | tf_op jit(solution)/shard_map/ppermute | solution.py:375
  61.3 5.8 %collective-permute-start.30 = (f32[56,384]{1,0:T(8,128)S(1)}, f32[56,384]{1,0:T(8,128)S(1)}, u32[]{:S(2)}, u32[]{:S(2)}) collective-permute-start(f32[56,384]{1,0:T(8,128)S(1)} %spectra_times_components.11.refs_0_), channel_id=1, source_target_pairs={{0,8},{1,17},{2,10},{3,19},{4,12},{5,21},{6,14},{7,23},{8,0},{9,25... | collective-permute-start | bytes 258056 | tf_op jit(solution)/shard_map/ppermute | solution.py:384
  63.2 9.2 %collective-permute-start.29 = (f32[56,384]{1,0:T(8,128)S(1)}, f32[56,384]{1,0:T(8,128)S(1)}, u32[]{:S(2)}, u32[]{:S(2)}) collective-permute-start(f32[56,384]{1,0:T(8,128)S(1)} %spectra_times_components.11.refs_0_), channel_id=1, source_target_pairs={{0,16},{1,9},{2,18},{3,11},{4,20},{5,13},{6,22},{7,15},{8,24},{9,1... | collective-permute-start | bytes 258056 | tf_op jit(solution)/shard_map/ppermute | solution.py:384
  63.4 9.0 %collective-permute-start.28 = (f32[56,384]{1,0:T(8,128)S(1)}, f32[56,384]{1,0:T(8,128)S(1)}, u32[]{:S(2)}, u32[]{:S(2)}) collective-permute-start(f32[56,384]{1,0:T(8,128)S(1)} %spectra_times_components.11.refs_0_), channel_id=1, source_target_pairs={{0,24},{1,25},{2,26},{3,27},{4,28},{5,29},{6,30},{7,31},{8,16},{9,... | collective-permute-start | bytes 258056 | tf_op jit(solution)/shard_map/ppermute | solution.py:384
  75.0 5.8 %collective-permute-start.32 = (f32[56,384]{1,0:T(8,128)S(1)}, f32[56,384]{1,0:T(8,128)S(1)}, u32[]{:S(2)}, u32[]{:S(2)}) collective-permute-start(f32[56,384]{1,0:T(8,128)S(1)} %get-tuple-element.38), channel_id=1, source_target_pairs={{0,6},{1,7},{2,4},{3,5},{4,2},{5,3},{6,0},{7,1},{8,14},{9,15},{10,... | collective-permute-start | bytes 258056 | tf_op jit(solution)/shard_map/ppermute | solution.py:375
  76.7 5.7 %collective-permute-start.33 = (f32[56,384]{1,0:T(8,128)S(1)}, f32[56,384]{1,0:T(8,128)S(1)}, u32[]{:S(2)}, u32[]{:S(2)}) collective-permute-start(f32[56,384]{1,0:T(8,128)S(1)} %get-tuple-element.39), channel_id=1, source_target_pairs={{0,4},{1,5},{2,6},{3,7},{4,0},{5,1},{6,2},{7,3},{8,12},{9,13},{10,... | collective-permute-start | bytes 258056 | tf_op jit(solution)/shard_map/ppermute | solution.py:375
  84.3 5.1 %collective-permute-start.37 = (f32[48,384]{1,0:T(8,128)S(1)}, f32[48,384]{1,0:T(8,128)S(1)}, u32[]{:S(2)}, u32[]{:S(2)}) collective-permute-start(f32[48,384]{1,0:T(8,128)S(1)} %update.9.refs_0_.h_ref), channel_id=1, source_target_pairs={{0,2},{1,3},{2,0},{3,1},{4,6},{5,7},{6,4},{7,5},{8,10},{9,11},{10,... | collective-permute-start | bytes 221192 | tf_op jit(solution)/shard_map/ppermute | solution.py:375
  84.9 5.3 %collective-permute-start.35 = (f32[48,384]{1,0:T(8,128)S(1)}, f32[48,384]{1,0:T(8,128)S(1)}, u32[]{:S(2)}, u32[]{:S(2)}) collective-permute-start(f32[48,384]{1,0:T(8,128)S(1)} %update.9.refs_0_.h_ref), channel_id=1, source_target_pairs={{0,6},{1,7},{2,4},{3,5},{4,2},{5,3},{6,0},{7,1},{8,14},{9,15},{10,... | collective-permute-start | bytes 221192 | tf_op jit(solution)/shard_map/ppermute | solution.py:375
  87.2 6.4 %collective-permute-start.40 = (f32[48,384]{1,0:T(8,128)S(1)}, f32[48,384]{1,0:T(8,128)S(1)}, u32[]{:S(2)}, u32[]{:S(2)}) collective-permute-start(f32[48,384]{1,0:T(8,128)S(1)} %collective-permute-done.39.refs_2_), channel_id=1, source_target_pairs={{0,1},{1,0},{2,3},{3,2},{4,5},{5,4},{6,7},{7,6},{8,9},{9,8},{10,11... | collective-permute-start | bytes 221192 | tf_op jit(solution)/shard_map/ppermute | solution.py:375
  95.7 5.8 %collective-permute-start.42 = (f32[64,128]{1,0:T(8,128)S(1)}, f32[64,128]{1,0:T(8,128)S(1)}, u32[]{:S(2)}, u32[]{:S(2)}) collective-permute-start(f32[64,128]{1,0:T(8,128)S(1)} %get-tuple-element.49), channel_id=1, source_target_pairs={{0,16},{8,24},{16,0},{24,8},{1,17},{9,25},{17,1},{25,9},{2,18},{10... | collective-permute-start | bytes 98312 | tf_op jit(solution)/shard_map/ppermute | solution.py:375
  97.2 5.7 %collective-permute-start.43 = (f32[64,128]{1,0:T(8,128)S(1)}, f32[64,128]{1,0:T(8,128)S(1)}, u32[]{:S(2)}, u32[]{:S(2)}) collective-permute-start(f32[64,128]{1,0:T(8,128)S(1)} %get-tuple-element.50), channel_id=1, source_target_pairs={{0,24},{8,16},{16,8},{24,0},{1,25},{9,17},{17,9},{25,1},{2,26},{10... | collective-permute-start | bytes 98312 | tf_op jit(solution)/shard_map/ppermute | solution.py:375
  (23 other events, 92.9 us)

commit v5 on v4

--- a/solution.py
+++ b/solution.py
@@ -128,25 +128,29 @@
     return pl.ds(pl.multiple_of(block * width, LANES), width)
 
 
-def scatter_kernel(relatives, width, w_ref, high_ref, low_ref, out):
+def scatter_kernel(relatives, width, w_ref, high_ref, low_ref, *outs):
+    if len(outs[0].shape) == 3:
+        outs = [outs[0].at[index] for index in range(len(relatives))]
     w = w_ref[...]
     rank = w.shape[0]
     stack, w_high = stacked(w)
     gram = product(stack, w_high, *split(w), NT)
-    for index, relative in enumerate(relatives):
+    for relative, out in zip(relatives, outs):
         here = bins_of(relative, width)
-        out[index, :rank, :] = product(stack, w_high, high_ref[:, here], low_ref[:, here], NN)
-        pack_gram(out.at[index], gram)
-
-
-def scatter_call(relatives, width, w_block, high, low):
+        out[:rank, :] = product(stack, w_high, high_ref[:, here], low_ref[:, here], NN)
+        pack_gram(out, gram)
+
+
+def scatter_call(relatives, width, w_block, high, low, joined=True):
     rank, pixels = w_block.shape
     count = len(relatives)
+    shape = (rank + SUBLANES, width)
+    shapes = [(count, *shape)] if joined else [shape] * count
     return pl.pallas_call(
         functools.partial(scatter_kernel, relatives, width),
         in_specs=vmem(3),
-        out_specs=pl.BlockSpec(memory_space=pltpu.VMEM),
-        out_shape=jax.ShapeDtypeStruct((count, rank + SUBLANES, width), F32),
+        out_specs=vmem(len(shapes)),
+        out_shape=[jax.ShapeDtypeStruct(shape, F32) for shape in shapes],
         compiler_params=params(),
         cost_estimate=cost(6 * rank * pixels * width * count, 4 * pixels * width * count),
         name="loadings_times_spectra",
@@ -155,11 +159,11 @@
 
 def pair_kernel(own_ref, other_ref, *outs):
     for index, out in enumerate(outs):
-        out[...] = own_ref[index + 1] + other_ref[index + 1]
+        out[...] = own_ref[index] + other_ref[index]
 
 
 def pair_call(own, other):
-    count = own.shape[0] - 1
+    count = own.shape[0]
     return pl.pallas_call(
         pair_kernel,
         in_specs=vmem(2),
@@ -171,23 +175,21 @@
     )(own, other)
 
 
-def update_kernel(stacks, factor_ref, *refs):
+def update_kernel(factor_ref, *refs):
     parts, out = refs[:-1], refs[-1]
     factor = factor_ref[...]
     rank = factor.shape[0]
-    total = None
-    for index, part in enumerate(parts):
-        value = part[0] if index < stacks else part[...]
-        total = value if total is None else total + value
+    total = parts[0][...]
+    for part in parts[1:]:
+        total = total + part[...]
     gram = unpack_gram(total[rank:], rank)
     out[...] = factor * total[:rank] / exact(gram, factor, NN)
 
 
-def update_call(factor, stacks, parts):
+def update_call(factor, *parts):
     rank, width = factor.shape
-    parts = (*stacks, *parts)
-    return pl.pallas_call(
-        functools.partial(update_kernel, len(stacks)),
+    return pl.pallas_call(
+        update_kernel,
         in_specs=vmem(1 + len(parts)),
         out_specs=pl.BlockSpec(memory_space=pltpu.VMEM),
         out_shape=jax.ShapeDtypeStruct((rank, width), F32),
@@ -413,12 +415,19 @@
     if groups > 2:
         steps = [*[(k, k) for k in range(groups - 1, 2, -1)], (1, 2), (2, 1)]
     for iteration in range(ITERS):
-        theirs = scatter_call(list(range(1, owners, 2)), width, w_block, high, low)
-        other = swap(theirs, "px", owners, 1)
-        own = scatter_call(list(range(0, owners, 2)), width, w_block, high, low)
-        sums = pair_call(own, other)
-        sent = [swap(sums[r // 2 - 1], "px", owners, r) for r in evens]
-        h_piece = update_call(h_piece, (own, other), sent)
+        batches = [evens[:1], evens[1:]] if len(evens) > 1 else [evens]
+        others = []
+        for batch in batches:
+            (theirs,) = scatter_call([r + 1 for r in batch], width, w_block, high, low)
+            others.append(swap(theirs, "px", owners, 1))
+        sent = []
+        for batch, other in zip(batches, others):
+            (own,) = scatter_call(batch, width, w_block, high, low)
+            for relative, value in zip(batch, pair_call(own, other)):
+                sent.append(swap(value, "px", owners, relative))
+        beside, near = scatter_call([1, 0], width, w_block, high, low, False)
+        beside = swap(beside, "px", owners, 1)
+        h_piece = update_call(h_piece, near, beside, *sent)
         if iteration + 1 < ITERS:
             total = spread(
                 h_piece,
@@ -428,7 +437,7 @@
             sent = []
             for even, odd in steps:
                 sent.append(cross(total, groups, owners, even, odd))
-            w_block = update_call(w_block, (), (total, *sent))
+            w_block = update_call(w_block, total, *sent)
         else:
             parts = spread(
                 h_piece,

time: 105 us -> 104 us (level)
  waiting for transfers between devices: 44.5 us -> 39.8 us
  starting transfers between devices: 40.5 us -> 43.1 us
  Pallas kernels: 18.6 us -> 20 us
    ppermute x36 -> x42, waiting for transfers between devices: 30.4 us -> 25.3 us  [swap(): return lax.ppermute(value, axis, [(i, i ^ mask) for i in range(size)])]
    ppermute x36 -> x42, starting transfers between devices: 25.5 us -> 28 us  [swap(): return lax.ppermute(value, axis, [(i, i ^ mask) for i in range(size)])]
    pallas_call x6 -> x15, Pallas kernels: 3.36 us -> 4.92 us  [scatter_call(): pl.pallas_call(functools.partial(scatter_kernel, relatives, width), in_sp...]
  transfers between devices with their start and end apart: 45 -> 51, of which waited for: 28 -> 25; matrix products, arithmetic and copies ran while one was open for 0% -> 0% of each run, Pallas kernels for 10% -> 12%
where the time goes in v5:
time: 104 us
  starting transfers between devices  43.1 us (41%)
  waiting for transfers between devices  39.8 us (38%)
  Pallas kernels  20 us (19%)
    ppermute x42, starting transfers between devices, swap(): return lax.ppermute(value, axis, [(i, i ^ mask) for i in range(size)])  28 us
    ppermute x42, waiting for transfers between devices, swap(): return lax.ppermute(value, axis, [(i, i ^ mask) for i in range(size)])  25.3 us
    ppermute x6, waiting for transfers between devices, cross(): return lax.ppermute(value, ('mz', 'px'), pairs)  12.1 us
    ppermute x6, starting transfers between devices, cross(): return lax.ppermute(value, ('mz', 'px'), pairs)  8.87 us
    ppermute x3, starting transfers between devices, fast_device(): lax.ppermute(w_piece, 'mz', [(i, (i - k) % groups) for i in range(groups)])  6.14 us
    pallas_call x3, Pallas kernels, final_gather_call(): pl.pallas_call(functools.partial(final_gather_kernel, relatives, groups,...  5.25 us
    pallas_call x15, Pallas kernels, scatter_call(): pl.pallas_call(functools.partial(scatter_kernel, relatives, width), in_sp...  4.92 us
    pallas_call x6, Pallas kernels, gather_call(): pl.pallas_call(functools.partial(gather_kernel, relatives, before is not...  4.65 us
  transfers between devices with their start and end apart: 51, of which 25 were waited for; matrix products, arithmetic and copies ran while one was open for 0% of the time, Pallas kernels for 12%

profile of v5, /device:TPU:0, one launch (start us, length us, event | category | flops | bytes accessed | tf_op | source)
XLA Modules:
  0.0 103.8 jit_solution(13110787680597594187)
XLA Ops:
  0.6 5.1 %collective-permute-start = (f32[48,96]{1,0:T(8,128)}, f32[48,96]{1,0:T(8,128)S(1)}, u32[]{:S(2)}, u32[]{:S(2)}) collective-permute-start(f32[48,96]{1,0:T(8,128)} %refs_0_.1), channel_id=1, source_target_pairs={{0,24},{8,0},{16,8},{24,16},{1,25},{9,1},{17,9},{25,17},{2,26},{10... | collective-permute-start | bytes 55304 | tf_op jit(solution)/shard_map/ppermute | solution.py:409
  6.8 2.5 %split_spectra.1 = (f32[384,3072]{1,0:T(8,128)S(1)}, bf16[384,3072]{1,0:T(8,128)(2,1)S(1)}, bf16[384,3072]{1,0:T(8,128)(2,1)S(1)}) custom-call(f32[384,3072]{1,0:T(8,128)} %s_ref.1), custom_call_target="tpu_custom_call" | custom-call | flops 4718592 | bytes 14155776 | tf_op jit(solution)/shard_map/split_spectra/pallas_call | solution.py:110
  14.2 2.5 %collective-permute-start.5 = (f32[56,384]{1,0:T(8,128)S(1)}, f32[56,384]{1,0:T(8,128)S(1)}, u32[]{:S(2)}, u32[]{:S(2)}) collective-permute-start(f32[56,384]{1,0:T(8,128)S(1)} %pair_sums.6), channel_id=1, source_target_pairs={{0,6},{1,7},{2,4},{3,5},{4,2},{5,3},{6,0},{7,1},{8,14},{9,15},{10,... | collective-permute-start | bytes 258056 | tf_op jit(solution)/shard_map/ppermute | solution.py:377
  17.9 2.3 %collective-permute-done.5.refs_2_ = f32[56,384]{1,0:T(8,128)S(1)} collective-permute-done((f32[56,384]{1,0:T(8,128)S(1)}, f32[56,384]{1,0:T(8,128)S(1)}, u32[]{:S(2)}, u32[]{:S(2)}) %collective-permute-start.5) | collective-permute-done | bytes 86048 | tf_op jit(solution)/shard_map/ppermute | solution.py:377
  20.2 1.8 %collective-permute-done.7.refs_3_ = f32[56,384]{1,0:T(8,128)S(1)} collective-permute-done((f32[56,384]{1,0:T(8,128)S(1)}, f32[56,384]{1,0:T(8,128)S(1)}, u32[]{:S(2)}, u32[]{:S(2)}) %collective-permute-start.7) | collective-permute-done | bytes 86048 | tf_op jit(solution)/shard_map/ppermute | solution.py:377
  22.3 1.9 %collective-permute-start.9 = (f32[48,384]{1,0:T(8,128)S(1)}, f32[48,384]{1,0:T(8,128)S(1)}, u32[]{:S(2)}, u32[]{:S(2)}) collective-permute-start(f32[48,384]{1,0:T(8,128)S(1)} %update.5.refs_0_.factor_ref), channel_id=1, source_target_pairs={{0,6},{1,7},{2,4},{3,5},{4,2},{5,3},{6,0},{7,1},{8,14},{9,15},{10,... | collective-permute-start | bytes 221192 | tf_op jit(solution)/shard_map/ppermute | solution.py:377
  25.9 2.3 %collective-permute-done.9.refs_0_ = f32[48,384]{1,0:T(8,128)S(1)} collective-permute-done((f32[48,384]{1,0:T(8,128)S(1)}, f32[48,384]{1,0:T(8,128)S(1)}, u32[]{:S(2)}, u32[]{:S(2)}) %collective-permute-start.9) | collective-permute-done | bytes 73760 | tf_op jit(solution)/shard_map/ppermute | solution.py:377
  33.7 2.7 %collective-permute-start.18 = (f32[56,384]{1,0:T(8,128)S(1)}, f32[56,384]{1,0:T(8,128)S(1)}, u32[]{:S(2)}, u32[]{:S(2)}) collective-permute-start(f32[56,384]{1,0:T(8,128)S(1)} %spectra_times_components.8.refs_0_), channel_id=1, source_target_pairs={{0,8},{1,17},{2,10},{3,19},{4,12},{5,21},{6,14},{7,23},{8,0},{9,25... | collective-permute-start | bytes 258056 | tf_op jit(solution)/shard_map/ppermute | solution.py:386
  36.4 2.9 %collective-permute-done.16.refs_1_ = f32[56,384]{1,0:T(8,128)S(1)} collective-permute-done((f32[56,384]{1,0:T(8,128)S(1)}, f32[56,384]{1,0:T(8,128)S(1)}, u32[]{:S(2)}, u32[]{:S(2)}) %collective-permute-start.16) | collective-permute-done | bytes 86048 | tf_op jit(solution)/shard_map/ppermute | solution.py:386
  39.4 3.1 %collective-permute-done.17.refs_2_ = f32[56,384]{1,0:T(8,128)S(1)} collective-permute-done((f32[56,384]{1,0:T(8,128)S(1)}, f32[56,384]{1,0:T(8,128)S(1)}, u32[]{:S(2)}, u32[]{:S(2)}) %collective-permute-start.17) | collective-permute-done | bytes 86048 | tf_op jit(solution)/shard_map/ppermute | solution.py:386
  48.9 2.4 %collective-permute-done.21.refs_2_ = f32[56,384]{1,0:T(8,128)S(1)} collective-permute-done((f32[56,384]{1,0:T(8,128)S(1)}, f32[56,384]{1,0:T(8,128)S(1)}, u32[]{:S(2)}, u32[]{:S(2)}) %collective-permute-start.21) | collective-permute-done | bytes 86048 | tf_op jit(solution)/shard_map/ppermute | solution.py:377
  51.4 1.6 %collective-permute-done.23.refs_3_ = f32[56,384]{1,0:T(8,128)S(1)} collective-permute-done((f32[56,384]{1,0:T(8,128)S(1)}, f32[56,384]{1,0:T(8,128)S(1)}, u32[]{:S(2)}, u32[]{:S(2)}) %collective-permute-start.23) | collective-permute-done | bytes 86048 | tf_op jit(solution)/shard_map/ppermute | solution.py:377
  56.8 2.5 %collective-permute-done.25.refs_0_ = f32[48,384]{1,0:T(8,128)S(1)} collective-permute-done((f32[48,384]{1,0:T(8,128)S(1)}, f32[48,384]{1,0:T(8,128)S(1)}, u32[]{:S(2)}, u32[]{:S(2)}) %collective-permute-start.25) | collective-permute-done | bytes 73760 | tf_op jit(solution)/shard_map/ppermute | solution.py:377
  62.4 2.1 %collective-permute-start.32 = (f32[56,384]{1,0:T(8,128)S(1)}, f32[56,384]{1,0:T(8,128)S(1)}, u32[]{:S(2)}, u32[]{:S(2)}) collective-permute-start(f32[56,384]{1,0:T(8,128)S(1)} %spectra_times_components.11.refs_0_), channel_id=1, source_target_pairs={{0,24},{1,25},{2,26},{3,27},{4,28},{5,29},{6,30},{7,31},{8,16},{9,... | collective-permute-start | bytes 258056 | tf_op jit(solution)/shard_map/ppermute | solution.py:386
  64.6 2.3 %collective-permute-start.34 = (f32[56,384]{1,0:T(8,128)S(1)}, f32[56,384]{1,0:T(8,128)S(1)}, u32[]{:S(2)}, u32[]{:S(2)}) collective-permute-start(f32[56,384]{1,0:T(8,128)S(1)} %spectra_times_components.11.refs_0_), channel_id=1, source_target_pairs={{0,8},{1,17},{2,10},{3,19},{4,12},{5,21},{6,14},{7,23},{8,0},{9,25... | collective-permute-start | bytes 258056 | tf_op jit(solution)/shard_map/ppermute | solution.py:386
  66.9 2.9 %collective-permute-done.32.refs_1_ = f32[56,384]{1,0:T(8,128)S(1)} collective-permute-done((f32[56,384]{1,0:T(8,128)S(1)}, f32[56,384]{1,0:T(8,128)S(1)}, u32[]{:S(2)}, u32[]{:S(2)}) %collective-permute-start.32) | collective-permute-done | bytes 86048 | tf_op jit(solution)/shard_map/ppermute | solution.py:386
  69.7 3.2 %collective-permute-done.33.refs_2_ = f32[56,384]{1,0:T(8,128)S(1)} collective-permute-done((f32[56,384]{1,0:T(8,128)S(1)}, f32[56,384]{1,0:T(8,128)S(1)}, u32[]{:S(2)}, u32[]{:S(2)}) %collective-permute-start.33) | collective-permute-done | bytes 86048 | tf_op jit(solution)/shard_map/ppermute | solution.py:386
  79.3 2.5 %collective-permute-done.37.refs_2_ = f32[56,384]{1,0:T(8,128)S(1)} collective-permute-done((f32[56,384]{1,0:T(8,128)S(1)}, f32[56,384]{1,0:T(8,128)S(1)}, u32[]{:S(2)}, u32[]{:S(2)}) %collective-permute-start.37) | collective-permute-done | bytes 86048 | tf_op jit(solution)/shard_map/ppermute | solution.py:377
  83.7 1.7 %collective-permute-start.41 = (f32[48,384]{1,0:T(8,128)S(1)}, f32[48,384]{1,0:T(8,128)S(1)}, u32[]{:S(2)}, u32[]{:S(2)}) collective-permute-start(f32[48,384]{1,0:T(8,128)S(1)} %update.9.refs_0_.h_ref), channel_id=1, source_target_pairs={{0,6},{1,7},{2,4},{3,5},{4,2},{5,3},{6,0},{7,1},{8,14},{9,15},{10,... | collective-permute-start | bytes 221192 | tf_op jit(solution)/shard_map/ppermute | solution.py:377
  87.4 2.5 %collective-permute-done.41.refs_0_ = f32[48,384]{1,0:T(8,128)S(1)} collective-permute-done((f32[48,384]{1,0:T(8,128)S(1)}, f32[48,384]{1,0:T(8,128)S(1)}, u32[]{:S(2)}, u32[]{:S(2)}) %collective-permute-start.41) | collective-permute-done | bytes 73760 | tf_op jit(solution)/shard_map/ppermute | solution.py:377
  92.1 1.9 %final_products.4 = (f32[48,384]{1,0:T(8,128)S(1)}, f32[384,128]{1,0:T(8,128)S(1)}, f32[48,256]{1,0:T(8,128)S(1)}) custom-call(f32[384,3072]{1,0:T(8,128)S(1)} %get-tuple-element.32.s_ref, f32[48,384]{1,0:T(8,128)S(1)} %update.8.w_ref, f32[48,384]{1,0:T(8,128)S(1)} %collective-permute-done.41.refs_0_, f32[48,384]{1,0:T(8,128)S(1)} %collective-permute-done.43.refs_1_, ...), custom_call_target="tpu_custom_call" | custom-call | flops 382205952 | bytes 3538944 | tf_op jit(solution)/shard_map/final_products/pallas_call | solution.py:307
  94.0 2.1 %final_products.5 = (f32[64,128]{1,0:T(8,128)S(1)}, f32[64,128]{1,0:T(8,128)S(1)}, f32[64,128]{1,0:T(8,128)S(1)}, f32[64,128]{1,0:T(8,128)S(1)}, f32[48,96]{1,0:T(8,128)S(1)}) custom-call(f32[384,3072]{1,0:T(8,128)S(1)} %get-tuple-element.32.s_ref, f32[48,384]{1,0:T(8,128)S(1)} %update.8.w_ref, f32[48,384]{1,0:T(8,128)S(1)} %collective-permute-done.42.refs_0_, ...), custom_call_target="tpu_custom_call" | custom-call | flops 382205952 | bytes 3538944 | tf_op jit(solution)/shard_map/final_products/pallas_call | solution.py:307
  96.7 2.1 %collective-permute-start.49 = (f32[64,128]{1,0:T(8,128)S(1)}, f32[64,128]{1,0:T(8,128)S(1)}, u32[]{:S(2)}, u32[]{:S(2)}) collective-permute-start(f32[64,128]{1,0:T(8,128)S(1)} %get-tuple-element.56), channel_id=1, source_target_pairs={{0,24},{8,16},{16,8},{24,0},{1,25},{9,17},{17,9},{25,1},{2,26},{10... | collective-permute-start | bytes 98312 | tf_op jit(solution)/shard_map/ppermute | solution.py:377
  99.7 1.7 %collective-permute-done.48.refs_1_ = f32[64,128]{1,0:T(8,128)S(1)} collective-permute-done((f32[64,128]{1,0:T(8,128)S(1)}, f32[64,128]{1,0:T(8,128)S(1)}, u32[]{:S(2)}, u32[]{:S(2)}) %collective-permute-start.48) | collective-permute-done | bytes 32800 | tf_op jit(solution)/shard_map/ppermute | solution.py:377
  (120 shorter events, 44.1 us)
Async XLA Ops:
  0.6 8.7 %collective-permute-start = (f32[48,96]{1,0:T(8,128)}, f32[48,96]{1,0:T(8,128)S(1)}, u32[]{:S(2)}, u32[]{:S(2)}) collective-permute-start(f32[48,96]{1,0:T(8,128)} %refs_0_.1), channel_id=1, source_target_pairs={{0,24},{8,0},{16,8},{24,16},{1,25},{9,1},{17,9},{25,17},{2,26},{10... | collective-permute-start | bytes 55304 | tf_op jit(solution)/shard_map/ppermute | solution.py:409
  5.8 4.9 %collective-permute-start.1 = (f32[48,96]{1,0:T(8,128)}, f32[48,96]{1,0:T(8,128)S(1)}, u32[]{:S(2)}, u32[]{:S(2)}) collective-permute-start(f32[48,96]{1,0:T(8,128)} %refs_0_.1), channel_id=1, source_target_pairs={{0,16},{8,24},{16,0},{24,8},{1,17},{9,25},{17,1},{25,9},{2,18},{10... | collective-permute-start | bytes 55304 | tf_op jit(solution)/shard_map/ppermute | solution.py:409
  5.8 5.8 %collective-permute-start.2 = (f32[48,96]{1,0:T(8,128)}, f32[48,96]{1,0:T(8,128)S(1)}, u32[]{:S(2)}, u32[]{:S(2)}) collective-permute-start(f32[48,96]{1,0:T(8,128)} %refs_0_.1), channel_id=1, source_target_pairs={{0,8},{8,16},{16,24},{24,0},{1,9},{9,17},{17,25},{25,1},{2,10},{10... | collective-permute-start | bytes 55304 | tf_op jit(solution)/shard_map/ppermute | solution.py:409
  14.2 5.9 %collective-permute-start.5 = (f32[56,384]{1,0:T(8,128)S(1)}, f32[56,384]{1,0:T(8,128)S(1)}, u32[]{:S(2)}, u32[]{:S(2)}) collective-permute-start(f32[56,384]{1,0:T(8,128)S(1)} %pair_sums.6), channel_id=1, source_target_pairs={{0,6},{1,7},{2,4},{3,5},{4,2},{5,3},{6,0},{7,1},{8,14},{9,15},{10,... | collective-permute-start | bytes 258056 | tf_op jit(solution)/shard_map/ppermute | solution.py:377
  16.7 5.2 %collective-permute-start.7 = (f32[56,384]{1,0:T(8,128)S(1)}, f32[56,384]{1,0:T(8,128)S(1)}, u32[]{:S(2)}, u32[]{:S(2)}) collective-permute-start(f32[56,384]{1,0:T(8,128)S(1)} %get-tuple-element.37), channel_id=1, source_target_pairs={{0,4},{1,5},{2,6},{3,7},{4,0},{5,1},{6,2},{7,3},{8,12},{9,13},{10,... | collective-permute-start | bytes 258056 | tf_op jit(solution)/shard_map/ppermute | solution.py:377
  22.3 5.9 %collective-permute-start.9 = (f32[48,384]{1,0:T(8,128)S(1)}, f32[48,384]{1,0:T(8,128)S(1)}, u32[]{:S(2)}, u32[]{:S(2)}) collective-permute-start(f32[48,384]{1,0:T(8,128)S(1)} %update.5.refs_0_.factor_ref), channel_id=1, source_target_pairs={{0,6},{1,7},{2,4},{3,5},{4,2},{5,3},{6,0},{7,1},{8,14},{9,15},{10,... | collective-permute-start | bytes 221192 | tf_op jit(solution)/shard_map/ppermute | solution.py:377
  24.2 4.9 %collective-permute-start.11 = (f32[48,384]{1,0:T(8,128)S(1)}, f32[48,384]{1,0:T(8,128)S(1)}, u32[]{:S(2)}, u32[]{:S(2)}) collective-permute-start(f32[48,384]{1,0:T(8,128)S(1)} %update.5.refs_0_.factor_ref), channel_id=1, source_target_pairs={{0,2},{1,3},{2,0},{3,1},{4,6},{5,7},{6,4},{7,5},{8,10},{9,11},{10,... | collective-permute-start | bytes 221192 | tf_op jit(solution)/shard_map/ppermute | solution.py:377
  32.0 7.3 %collective-permute-start.16 = (f32[56,384]{1,0:T(8,128)S(1)}, f32[56,384]{1,0:T(8,128)S(1)}, u32[]{:S(2)}, u32[]{:S(2)}) collective-permute-start(f32[56,384]{1,0:T(8,128)S(1)} %spectra_times_components.8.refs_0_), channel_id=1, source_target_pairs={{0,24},{1,25},{2,26},{3,27},{4,28},{5,29},{6,30},{7,31},{8,16},{9,... | collective-permute-start | bytes 258056 | tf_op jit(solution)/shard_map/ppermute | solution.py:386
  32.7 9.8 %collective-permute-start.17 = (f32[56,384]{1,0:T(8,128)S(1)}, f32[56,384]{1,0:T(8,128)S(1)}, u32[]{:S(2)}, u32[]{:S(2)}) collective-permute-start(f32[56,384]{1,0:T(8,128)S(1)} %spectra_times_components.8.refs_0_), channel_id=1, source_target_pairs={{0,16},{1,9},{2,18},{3,11},{4,20},{5,13},{6,22},{7,15},{8,24},{9,1... | collective-permute-start | bytes 258056 | tf_op jit(solution)/shard_map/ppermute | solution.py:386
  33.7 8.8 %collective-permute-start.18 = (f32[56,384]{1,0:T(8,128)S(1)}, f32[56,384]{1,0:T(8,128)S(1)}, u32[]{:S(2)}, u32[]{:S(2)}) collective-permute-start(f32[56,384]{1,0:T(8,128)S(1)} %spectra_times_components.8.refs_0_), channel_id=1, source_target_pairs={{0,8},{1,17},{2,10},{3,19},{4,12},{5,21},{6,14},{7,23},{8,0},{9,25... | collective-permute-start | bytes 258056 | tf_op jit(solution)/shard_map/ppermute | solution.py:386
  45.3 6.1 %collective-permute-start.21 = (f32[56,384]{1,0:T(8,128)S(1)}, f32[56,384]{1,0:T(8,128)S(1)}, u32[]{:S(2)}, u32[]{:S(2)}) collective-permute-start(f32[56,384]{1,0:T(8,128)S(1)} %pair_sums.8), channel_id=1, source_target_pairs={{0,6},{1,7},{2,4},{3,5},{4,2},{5,3},{6,0},{7,1},{8,14},{9,15},{10,... | collective-permute-start | bytes 258056 | tf_op jit(solution)/shard_map/ppermute | solution.py:377
  46.9 6.1 %collective-permute-start.23 = (f32[56,384]{1,0:T(8,128)S(1)}, f32[56,384]{1,0:T(8,128)S(1)}, u32[]{:S(2)}, u32[]{:S(2)}) collective-permute-start(f32[56,384]{1,0:T(8,128)S(1)} %get-tuple-element.41), channel_id=1, source_target_pairs={{0,4},{1,5},{2,6},{3,7},{4,0},{5,1},{6,2},{7,3},{8,12},{9,13},{10,... | collective-permute-start | bytes 258056 | tf_op jit(solution)/shard_map/ppermute | solution.py:377
  47.8 5.2 %collective-permute-start.24 = (f32[56,384]{1,0:T(8,128)S(1)}, f32[56,384]{1,0:T(8,128)S(1)}, u32[]{:S(2)}, u32[]{:S(2)}) collective-permute-start(f32[56,384]{1,0:T(8,128)S(1)} %get-tuple-element.42), channel_id=1, source_target_pairs={{0,2},{1,3},{2,0},{3,1},{4,6},{5,7},{6,4},{7,5},{8,10},{9,11},{10,... | collective-permute-start | bytes 258056 | tf_op jit(solution)/shard_map/ppermute | solution.py:377
  53.2 6.1 %collective-permute-start.25 = (f32[48,384]{1,0:T(8,128)S(1)}, f32[48,384]{1,0:T(8,128)S(1)}, u32[]{:S(2)}, u32[]{:S(2)}) collective-permute-start(f32[48,384]{1,0:T(8,128)S(1)} %update.7.refs_0_.factor_ref), channel_id=1, source_target_pairs={{0,6},{1,7},{2,4},{3,5},{4,2},{5,3},{6,0},{7,1},{8,14},{9,15},{10,... | collective-permute-start | bytes 221192 | tf_op jit(solution)/shard_map/ppermute | solution.py:377
  62.4 7.3 %collective-permute-start.32 = (f32[56,384]{1,0:T(8,128)S(1)}, f32[56,384]{1,0:T(8,128)S(1)}, u32[]{:S(2)}, u32[]{:S(2)}) collective-permute-start(f32[56,384]{1,0:T(8,128)S(1)} %spectra_times_components.11.refs_0_), channel_id=1, source_target_pairs={{0,24},{1,25},{2,26},{3,27},{4,28},{5,29},{6,30},{7,31},{8,16},{9,... | collective-permute-start | bytes 258056 | tf_op jit(solution)/shard_map/ppermute | solution.py:386
  64.6 8.4 %collective-permute-start.33 = (f32[56,384]{1,0:T(8,128)S(1)}, f32[56,384]{1,0:T(8,128)S(1)}, u32[]{:S(2)}, u32[]{:S(2)}) collective-permute-start(f32[56,384]{1,0:T(8,128)S(1)} %spectra_times_components.11.refs_0_), channel_id=1, source_target_pairs={{0,16},{1,9},{2,18},{3,11},{4,20},{5,13},{6,22},{7,15},{8,24},{9,1... | collective-permute-start | bytes 258056 | tf_op jit(solution)/shard_map/ppermute | solution.py:386
  64.6 8.4 %collective-permute-start.34 = (f32[56,384]{1,0:T(8,128)S(1)}, f32[56,384]{1,0:T(8,128)S(1)}, u32[]{:S(2)}, u32[]{:S(2)}) collective-permute-start(f32[56,384]{1,0:T(8,128)S(1)} %spectra_times_components.11.refs_0_), channel_id=1, source_target_pairs={{0,8},{1,17},{2,10},{3,19},{4,12},{5,21},{6,14},{7,23},{8,0},{9,25... | collective-permute-start | bytes 258056 | tf_op jit(solution)/shard_map/ppermute | solution.py:386
  75.6 6.2 %collective-permute-start.37 = (f32[56,384]{1,0:T(8,128)S(1)}, f32[56,384]{1,0:T(8,128)S(1)}, u32[]{:S(2)}, u32[]{:S(2)}) collective-permute-start(f32[56,384]{1,0:T(8,128)S(1)} %pair_sums.10), channel_id=1, source_target_pairs={{0,6},{1,7},{2,4},{3,5},{4,2},{5,3},{6,0},{7,1},{8,14},{9,15},{10,... | collective-permute-start | bytes 258056 | tf_op jit(solution)/shard_map/ppermute | solution.py:377
  77.2 6.2 %collective-permute-start.39 = (f32[56,384]{1,0:T(8,128)S(1)}, f32[56,384]{1,0:T(8,128)S(1)}, u32[]{:S(2)}, u32[]{:S(2)}) collective-permute-start(f32[56,384]{1,0:T(8,128)S(1)} %get-tuple-element.45), channel_id=1, source_target_pairs={{0,4},{1,5},{2,6},{3,7},{4,0},{5,1},{6,2},{7,3},{8,12},{9,13},{10,... | collective-permute-start | bytes 258056 | tf_op jit(solution)/shard_map/ppermute | solution.py:377
  78.3 5.0 %collective-permute-start.40 = (f32[56,384]{1,0:T(8,128)S(1)}, f32[56,384]{1,0:T(8,128)S(1)}, u32[]{:S(2)}, u32[]{:S(2)}) collective-permute-start(f32[56,384]{1,0:T(8,128)S(1)} %get-tuple-element.46), channel_id=1, source_target_pairs={{0,2},{1,3},{2,0},{3,1},{4,6},{5,7},{6,4},{7,5},{8,10},{9,11},{10,... | collective-permute-start | bytes 258056 | tf_op jit(solution)/shard_map/ppermute | solution.py:377
  83.7 6.3 %collective-permute-start.41 = (f32[48,384]{1,0:T(8,128)S(1)}, f32[48,384]{1,0:T(8,128)S(1)}, u32[]{:S(2)}, u32[]{:S(2)}) collective-permute-start(f32[48,384]{1,0:T(8,128)S(1)} %update.9.refs_0_.h_ref), channel_id=1, source_target_pairs={{0,6},{1,7},{2,4},{3,5},{4,2},{5,3},{6,0},{7,1},{8,14},{9,15},{10,... | collective-permute-start | bytes 221192 | tf_op jit(solution)/shard_map/ppermute | solution.py:377
  85.4 4.8 %collective-permute-start.43 = (f32[48,384]{1,0:T(8,128)S(1)}, f32[48,384]{1,0:T(8,128)S(1)}, u32[]{:S(2)}, u32[]{:S(2)}) collective-permute-start(f32[48,384]{1,0:T(8,128)S(1)} %update.9.refs_0_.h_ref), channel_id=1, source_target_pairs={{0,2},{1,3},{2,0},{3,1},{4,6},{5,7},{6,4},{7,5},{8,10},{9,11},{10,... | collective-permute-start | bytes 221192 | tf_op jit(solution)/shard_map/ppermute | solution.py:377
  96.1 5.3 %collective-permute-start.48 = (f32[64,128]{1,0:T(8,128)S(1)}, f32[64,128]{1,0:T(8,128)S(1)}, u32[]{:S(2)}, u32[]{:S(2)}) collective-permute-start(f32[64,128]{1,0:T(8,128)S(1)} %get-tuple-element.55), channel_id=1, source_target_pairs={{0,16},{8,24},{16,0},{24,8},{1,17},{9,25},{17,1},{25,9},{2,18},{10... | collective-permute-start | bytes 98312 | tf_op jit(solution)/shard_map/ppermute | solution.py:377
  96.7 5.8 %collective-permute-start.49 = (f32[64,128]{1,0:T(8,128)S(1)}, f32[64,128]{1,0:T(8,128)S(1)}, u32[]{:S(2)}, u32[]{:S(2)}) collective-permute-start(f32[64,128]{1,0:T(8,128)S(1)} %get-tuple-element.56), channel_id=1, source_target_pairs={{0,24},{8,16},{16,8},{24,0},{1,25},{9,17},{17,9},{25,1},{2,26},{10... | collective-permute-start | bytes 98312 | tf_op jit(solution)/shard_map/ppermute | solution.py:377
  (29 other events, 110.2 us)

commit v6 on v5

--- a/solution.py
+++ b/solution.py
@@ -354,10 +354,13 @@
 
 
 def join_kernel(*refs):
-    pieces, out = refs[:-1], refs[-1]
-    _, width = pieces[0].shape
-    whole = jnp.concatenate([piece[...] for piece in pieces], axis=1)
-    out[...] = pltpu.roll(whole, lax.axis_index("mz") * width, 1)
+    pieces, out, table = refs[:-2], refs[-2], refs[-1]
+    width = pieces[0].shape[1]
+    for index, piece in enumerate(pieces):
+        table[index] = piece[...]
+    me = lax.axis_index("mz")
+    for index in range(len(pieces)):
+        out[:, index * width : (index + 1) * width] = table[jnp.bitwise_xor(me, index)]
 
 
 def join_call(*pieces):
@@ -367,6 +370,7 @@
         in_specs=vmem(len(pieces)),
         out_specs=pl.BlockSpec(memory_space=pltpu.VMEM),
         out_shape=jax.ShapeDtypeStruct((rank, width * len(pieces)), F32),
+        scratch_shapes=[pltpu.VMEM((len(pieces), rank, width), F32)],
         compiler_params=params(),
         cost_estimate=cost(0, 8 * rank * width * len(pieces)),
         name="join",
@@ -403,14 +407,11 @@
 def fast_device(groups, owners, spectra, w_piece, h_piece):
     width = h_piece.shape[1]
     copy, high, low = split_call(spectra)
-    w_block = join_call(
-        w_piece,
-        *[
-            lax.ppermute(w_piece, "mz", [(i, (i - k) % groups) for i in range(groups)])
-            for k in range(1, groups)
-        ],
-    )
-    evens = list(range(owners - 2, 0, -2))
+    pieces = [w_piece] * groups
+    for k in range(1, groups):
+        pieces[k] = swap(w_piece, "mz", groups, k)
+    w_block = join_call(*pieces)
+    evens = [owners - 2, *range(2, owners - 2, 2)]
     steps = [(1, 1)]
     if groups > 2:
         steps = [*[(k, k) for k in range(groups - 1, 2, -1)], (1, 2), (2, 1)]

time: 104 us -> 104 us (level)
    ppermute x3 -> x0, starting transfers between devices: 6.14 us -> none  [fast_device(): lax.ppermute(w_piece, 'mz', [(i, (i - k) % groups) for i in range(groups)])]
    ppermute x42 -> x45, starting transfers between devices: 28 us -> 33.7 us  [swap(): return lax.ppermute(value, axis, [(i, i ^ mask) for i in range(size)])]
    ppermute x42 -> x45, waiting for transfers between devices: 25.3 us -> 28.3 us  [swap(): return lax.ppermute(value, axis, [(i, i ^ mask) for i in range(size)])]
    ppermute x3 -> x0, waiting for transfers between devices: 2.3 us -> none  [fast_device(): lax.ppermute(w_piece, 'mz', [(i, (i - k) % groups) for i in range(groups)])]
  transfers between devices with their start and end apart: 51 -> 51, of which waited for: 25 -> 26; matrix products, arithmetic and copies ran while one was open for 0% -> 0% of each run, Pallas kernels for 12% -> 12%
where the time goes in v6:
time: 104 us
  starting transfers between devices  42.5 us (41%)
  waiting for transfers between devices  40.3 us (39%)
  Pallas kernels  19.8 us (19%)
    ppermute x45, starting transfers between devices, swap(): return lax.ppermute(value, axis, [(i, i ^ mask) for i in range(size)])  33.7 us
    ppermute x45, waiting for transfers between devices, swap(): return lax.ppermute(value, axis, [(i, i ^ mask) for i in range(size)])  28.3 us
    ppermute x6, waiting for transfers between devices, cross(): return lax.ppermute(value, ('mz', 'px'), pairs)  12 us
    ppermute x6, starting transfers between devices, cross(): return lax.ppermute(value, ('mz', 'px'), pairs)  8.87 us
    pallas_call x3, Pallas kernels, final_gather_call(): pl.pallas_call(functools.partial(final_gather_kernel, relatives, groups,...  5.25 us
    pallas_call x15, Pallas kernels, scatter_call(): pl.pallas_call(functools.partial(scatter_kernel, relatives, width), in_sp...  4.85 us
    pallas_call x6, Pallas kernels, gather_call(): pl.pallas_call(functools.partial(gather_kernel, relatives, before is not...  4.66 us
    pallas_call x1, Pallas kernels, split_call(): pl.pallas_call(functools.partial(split_kernel, step), in_specs=[pl.BlockS...  2.51 us
  transfers between devices with their start and end apart: 51, of which 26 were waited for; matrix products, arithmetic and copies ran while one was open for 0% of the time, Pallas kernels for 12%

profile of v6, /device:TPU:0, one launch (start us, length us, event | category | flops | bytes accessed | tf_op | source)
XLA Modules:
  0.0 103.7 jit_solution(6742784354415500794)
XLA Ops:
  0.6 3.1 %collective-permute-start = (f32[48,96]{1,0:T(8,128)}, f32[48,96]{1,0:T(8,128)S(1)}, u32[]{:S(2)}, u32[]{:S(2)}) collective-permute-start(f32[48,96]{1,0:T(8,128)} %refs_0_.1), channel_id=1, source_target_pairs={{0,8},{8,0},{16,24},{24,16},{1,9},{9,1},{17,25},{25,17},{2,10},{10... | collective-permute-start | bytes 55304 | tf_op jit(solution)/shard_map/ppermute | solution.py:381
  3.8 2.6 %collective-permute-start.1 = (f32[48,96]{1,0:T(8,128)}, f32[48,96]{1,0:T(8,128)S(1)}, u32[]{:S(2)}, u32[]{:S(2)}) collective-permute-start(f32[48,96]{1,0:T(8,128)} %refs_0_.1), channel_id=1, source_target_pairs={{0,16},{8,24},{16,0},{24,8},{1,17},{9,25},{17,1},{25,9},{2,18},{10... | collective-permute-start | bytes 55304 | tf_op jit(solution)/shard_map/ppermute | solution.py:381
  6.3 2.5 %split_spectra.1 = (f32[384,3072]{1,0:T(8,128)S(1)}, bf16[384,3072]{1,0:T(8,128)(2,1)S(1)}, bf16[384,3072]{1,0:T(8,128)(2,1)S(1)}) custom-call(f32[384,3072]{1,0:T(8,128)} %s_ref.1), custom_call_target="tpu_custom_call" | custom-call | flops 4718592 | bytes 14155776 | tf_op jit(solution)/shard_map/split_spectra/pallas_call | solution.py:110
  9.0 3.1 %collective-permute-done.2.refs_3_ = f32[48,96]{1,0:T(8,128)S(1)} collective-permute-done((f32[48,96]{1,0:T(8,128)}, f32[48,96]{1,0:T(8,128)S(1)}, u32[]{:S(2)}, u32[]{:S(2)}) %collective-permute-start.2) | collective-permute-done | bytes 18464 | tf_op jit(solution)/shard_map/ppermute | solution.py:381
  14.7 2.5 %collective-permute-start.5 = (f32[56,384]{1,0:T(8,128)S(1)}, f32[56,384]{1,0:T(8,128)S(1)}, u32[]{:S(2)}, u32[]{:S(2)}) collective-permute-start(f32[56,384]{1,0:T(8,128)S(1)} %pair_sums.6), channel_id=1, source_target_pairs={{0,6},{1,7},{2,4},{3,5},{4,2},{5,3},{6,0},{7,1},{8,14},{9,15},{10,... | collective-permute-start | bytes 258056 | tf_op jit(solution)/shard_map/ppermute | solution.py:381
  18.4 2.7 %collective-permute-done.5.refs_2_ = f32[56,384]{1,0:T(8,128)S(1)} collective-permute-done((f32[56,384]{1,0:T(8,128)S(1)}, f32[56,384]{1,0:T(8,128)S(1)}, u32[]{:S(2)}, u32[]{:S(2)}) %collective-permute-start.5) | collective-permute-done | bytes 86048 | tf_op jit(solution)/shard_map/ppermute | solution.py:381
  22.9 2.4 %collective-permute-start.9 = (f32[48,384]{1,0:T(8,128)S(1)}, f32[48,384]{1,0:T(8,128)S(1)}, u32[]{:S(2)}, u32[]{:S(2)}) collective-permute-start(f32[48,384]{1,0:T(8,128)S(1)} %update.5.refs_0_.factor_ref), channel_id=1, source_target_pairs={{0,6},{1,7},{2,4},{3,5},{4,2},{5,3},{6,0},{7,1},{8,14},{9,15},{10,... | collective-permute-start | bytes 221192 | tf_op jit(solution)/shard_map/ppermute | solution.py:381
  26.4 2.5 %collective-permute-done.9.refs_0_ = f32[48,384]{1,0:T(8,128)S(1)} collective-permute-done((f32[48,384]{1,0:T(8,128)S(1)}, f32[48,384]{1,0:T(8,128)S(1)}, u32[]{:S(2)}, u32[]{:S(2)}) %collective-permute-start.9) | collective-permute-done | bytes 73760 | tf_op jit(solution)/shard_map/ppermute | solution.py:381
  33.2 3.8 %collective-permute-start.18 = (f32[56,384]{1,0:T(8,128)S(1)}, f32[56,384]{1,0:T(8,128)S(1)}, u32[]{:S(2)}, u32[]{:S(2)}) collective-permute-start(f32[56,384]{1,0:T(8,128)S(1)} %spectra_times_components.8.refs_0_), channel_id=1, source_target_pairs={{0,8},{1,17},{2,10},{3,19},{4,12},{5,21},{6,14},{7,23},{8,0},{9,25... | collective-permute-start | bytes 258056 | tf_op jit(solution)/shard_map/ppermute | solution.py:390
  37.0 2.9 %collective-permute-done.16.refs_1_ = f32[56,384]{1,0:T(8,128)S(1)} collective-permute-done((f32[56,384]{1,0:T(8,128)S(1)}, f32[56,384]{1,0:T(8,128)S(1)}, u32[]{:S(2)}, u32[]{:S(2)}) %collective-permute-start.16) | collective-permute-done | bytes 86048 | tf_op jit(solution)/shard_map/ppermute | solution.py:390
  39.9 3.1 %collective-permute-done.17.refs_2_ = f32[56,384]{1,0:T(8,128)S(1)} collective-permute-done((f32[56,384]{1,0:T(8,128)S(1)}, f32[56,384]{1,0:T(8,128)S(1)}, u32[]{:S(2)}, u32[]{:S(2)}) %collective-permute-start.17) | collective-permute-done | bytes 86048 | tf_op jit(solution)/shard_map/ppermute | solution.py:390
  45.7 1.8 %collective-permute-start.21 = (f32[56,384]{1,0:T(8,128)S(1)}, f32[56,384]{1,0:T(8,128)S(1)}, u32[]{:S(2)}, u32[]{:S(2)}) collective-permute-start(f32[56,384]{1,0:T(8,128)S(1)} %pair_sums.8), channel_id=1, source_target_pairs={{0,6},{1,7},{2,4},{3,5},{4,2},{5,3},{6,0},{7,1},{8,14},{9,15},{10,... | collective-permute-start | bytes 258056 | tf_op jit(solution)/shard_map/ppermute | solution.py:381
  49.4 2.7 %collective-permute-done.21.refs_2_ = f32[56,384]{1,0:T(8,128)S(1)} collective-permute-done((f32[56,384]{1,0:T(8,128)S(1)}, f32[56,384]{1,0:T(8,128)S(1)}, u32[]{:S(2)}, u32[]{:S(2)}) %collective-permute-start.21) | collective-permute-done | bytes 86048 | tf_op jit(solution)/shard_map/ppermute | solution.py:381
  53.7 1.9 %collective-permute-start.25 = (f32[48,384]{1,0:T(8,128)S(1)}, f32[48,384]{1,0:T(8,128)S(1)}, u32[]{:S(2)}, u32[]{:S(2)}) collective-permute-start(f32[48,384]{1,0:T(8,128)S(1)} %update.7.refs_0_.factor_ref), channel_id=1, source_target_pairs={{0,6},{1,7},{2,4},{3,5},{4,2},{5,3},{6,0},{7,1},{8,14},{9,15},{10,... | collective-permute-start | bytes 221192 | tf_op jit(solution)/shard_map/ppermute | solution.py:381
  57.2 2.5 %collective-permute-done.25.refs_0_ = f32[48,384]{1,0:T(8,128)S(1)} collective-permute-done((f32[48,384]{1,0:T(8,128)S(1)}, f32[48,384]{1,0:T(8,128)S(1)}, u32[]{:S(2)}, u32[]{:S(2)}) %collective-permute-start.25) | collective-permute-done | bytes 73760 | tf_op jit(solution)/shard_map/ppermute | solution.py:381
  63.9 3.4 %collective-permute-start.34 = (f32[56,384]{1,0:T(8,128)S(1)}, f32[56,384]{1,0:T(8,128)S(1)}, u32[]{:S(2)}, u32[]{:S(2)}) collective-permute-start(f32[56,384]{1,0:T(8,128)S(1)} %spectra_times_components.11.refs_0_), channel_id=1, source_target_pairs={{0,8},{1,17},{2,10},{3,19},{4,12},{5,21},{6,14},{7,23},{8,0},{9,25... | collective-permute-start | bytes 258056 | tf_op jit(solution)/shard_map/ppermute | solution.py:390
  67.3 2.9 %collective-permute-done.32.refs_1_ = f32[56,384]{1,0:T(8,128)S(1)} collective-permute-done((f32[56,384]{1,0:T(8,128)S(1)}, f32[56,384]{1,0:T(8,128)S(1)}, u32[]{:S(2)}, u32[]{:S(2)}) %collective-permute-start.32) | collective-permute-done | bytes 86048 | tf_op jit(solution)/shard_map/ppermute | solution.py:390
  70.2 3.1 %collective-permute-done.33.refs_2_ = f32[56,384]{1,0:T(8,128)S(1)} collective-permute-done((f32[56,384]{1,0:T(8,128)S(1)}, f32[56,384]{1,0:T(8,128)S(1)}, u32[]{:S(2)}, u32[]{:S(2)}) %collective-permute-start.33) | collective-permute-done | bytes 86048 | tf_op jit(solution)/shard_map/ppermute | solution.py:390
  76.1 2.2 %collective-permute-start.37 = (f32[56,384]{1,0:T(8,128)S(1)}, f32[56,384]{1,0:T(8,128)S(1)}, u32[]{:S(2)}, u32[]{:S(2)}) collective-permute-start(f32[56,384]{1,0:T(8,128)S(1)} %pair_sums.10), channel_id=1, source_target_pairs={{0,6},{1,7},{2,4},{3,5},{4,2},{5,3},{6,0},{7,1},{8,14},{9,15},{10,... | collective-permute-start | bytes 258056 | tf_op jit(solution)/shard_map/ppermute | solution.py:381
  79.7 2.7 %collective-permute-done.37.refs_2_ = f32[56,384]{1,0:T(8,128)S(1)} collective-permute-done((f32[56,384]{1,0:T(8,128)S(1)}, f32[56,384]{1,0:T(8,128)S(1)}, u32[]{:S(2)}, u32[]{:S(2)}) %collective-permute-start.37) | collective-permute-done | bytes 86048 | tf_op jit(solution)/shard_map/ppermute | solution.py:381
  84.0 2.2 %collective-permute-start.41 = (f32[48,384]{1,0:T(8,128)S(1)}, f32[48,384]{1,0:T(8,128)S(1)}, u32[]{:S(2)}, u32[]{:S(2)}) collective-permute-start(f32[48,384]{1,0:T(8,128)S(1)} %update.9.refs_0_.h_ref), channel_id=1, source_target_pairs={{0,6},{1,7},{2,4},{3,5},{4,2},{5,3},{6,0},{7,1},{8,14},{9,15},{10,... | collective-permute-start | bytes 221192 | tf_op jit(solution)/shard_map/ppermute | solution.py:381
  87.6 2.4 %collective-permute-done.41.refs_0_ = f32[48,384]{1,0:T(8,128)S(1)} collective-permute-done((f32[48,384]{1,0:T(8,128)S(1)}, f32[48,384]{1,0:T(8,128)S(1)}, u32[]{:S(2)}, u32[]{:S(2)}) %collective-permute-start.41) | collective-permute-done | bytes 73760 | tf_op jit(solution)/shard_map/ppermute | solution.py:381
  92.4 1.9 %final_products.4 = (f32[48,384]{1,0:T(8,128)S(1)}, f32[384,128]{1,0:T(8,128)S(1)}, f32[48,256]{1,0:T(8,128)S(1)}) custom-call(f32[384,3072]{1,0:T(8,128)S(1)} %get-tuple-element.32.s_ref, f32[48,384]{1,0:T(8,128)S(1)} %update.8.w_ref, f32[48,384]{1,0:T(8,128)S(1)} %collective-permute-done.41.refs_0_, f32[48,384]{1,0:T(8,128)S(1)} %collective-permute-done.43.refs_1_, ...), custom_call_target="tpu_custom_call" | custom-call | flops 382205952 | bytes 3538944 | tf_op jit(solution)/shard_map/final_products/pallas_call | solution.py:307
  94.3 2.1 %final_products.5 = (f32[64,128]{1,0:T(8,128)S(1)}, f32[64,128]{1,0:T(8,128)S(1)}, f32[64,128]{1,0:T(8,128)S(1)}, f32[64,128]{1,0:T(8,128)S(1)}, f32[48,96]{1,0:T(8,128)S(1)}) custom-call(f32[384,3072]{1,0:T(8,128)S(1)} %get-tuple-element.32.s_ref, f32[48,384]{1,0:T(8,128)S(1)} %update.8.w_ref, f32[48,384]{1,0:T(8,128)S(1)} %collective-permute-done.42.refs_0_, ...), custom_call_target="tpu_custom_call" | custom-call | flops 382205952 | bytes 3538944 | tf_op jit(solution)/shard_map/final_products/pallas_call | solution.py:307
  (120 shorter events, 39.7 us)
Async XLA Ops:
  0.6 8.2 %collective-permute-start = (f32[48,96]{1,0:T(8,128)}, f32[48,96]{1,0:T(8,128)S(1)}, u32[]{:S(2)}, u32[]{:S(2)}) collective-permute-start(f32[48,96]{1,0:T(8,128)} %refs_0_.1), channel_id=1, source_target_pairs={{0,8},{8,0},{16,24},{24,16},{1,9},{9,1},{17,25},{25,17},{2,10},{10... | collective-permute-start | bytes 55304 | tf_op jit(solution)/shard_map/ppermute | solution.py:381
  3.8 5.3 %collective-permute-start.1 = (f32[48,96]{1,0:T(8,128)}, f32[48,96]{1,0:T(8,128)S(1)}, u32[]{:S(2)}, u32[]{:S(2)}) collective-permute-start(f32[48,96]{1,0:T(8,128)} %refs_0_.1), channel_id=1, source_target_pairs={{0,16},{8,24},{16,0},{24,8},{1,17},{9,25},{17,1},{25,9},{2,18},{10... | collective-permute-start | bytes 55304 | tf_op jit(solution)/shard_map/ppermute | solution.py:381
  6.3 5.8 %collective-permute-start.2 = (f32[48,96]{1,0:T(8,128)}, f32[48,96]{1,0:T(8,128)S(1)}, u32[]{:S(2)}, u32[]{:S(2)}) collective-permute-start(f32[48,96]{1,0:T(8,128)} %refs_0_.1), channel_id=1, source_target_pairs={{0,24},{8,16},{16,8},{24,0},{1,25},{9,17},{17,9},{25,1},{2,26},{10... | collective-permute-start | bytes 55304 | tf_op jit(solution)/shard_map/ppermute | solution.py:381
  12.7 4.6 %collective-permute-start.6 = (f32[2,56,384]{2,1,0:T(8,128)S(1)}, f32[2,56,384]{2,1,0:T(8,128)S(1)}, u32[]{:S(2)}, u32[]{:S(2)}) collective-permute-start(f32[2,56,384]{2,1,0:T(8,128)S(1)} %loadings_times_spectra.19), channel_id=1, source_target_pairs={{0,1},{1,0},{2,3},{3,2},{4,5},{5,4},{6,7},{7,6},{8,9},{9,8},{10,11... | collective-permute-start | bytes 516104 | tf_op jit(solution)/shard_map/ppermute | solution.py:381
  14.7 6.4 %collective-permute-start.5 = (f32[56,384]{1,0:T(8,128)S(1)}, f32[56,384]{1,0:T(8,128)S(1)}, u32[]{:S(2)}, u32[]{:S(2)}) collective-permute-start(f32[56,384]{1,0:T(8,128)S(1)} %pair_sums.6), channel_id=1, source_target_pairs={{0,6},{1,7},{2,4},{3,5},{4,2},{5,3},{6,0},{7,1},{8,14},{9,15},{10,... | collective-permute-start | bytes 258056 | tf_op jit(solution)/shard_map/ppermute | solution.py:381
  17.3 5.2 %collective-permute-start.7 = (f32[56,384]{1,0:T(8,128)S(1)}, f32[56,384]{1,0:T(8,128)S(1)}, u32[]{:S(2)}, u32[]{:S(2)}) collective-permute-start(f32[56,384]{1,0:T(8,128)S(1)} %get-tuple-element.37), channel_id=1, source_target_pairs={{0,2},{1,3},{2,0},{3,1},{4,6},{5,7},{6,4},{7,5},{8,10},{9,11},{10,... | collective-permute-start | bytes 258056 | tf_op jit(solution)/shard_map/ppermute | solution.py:381
  17.9 4.7 %collective-permute-start.8 = (f32[56,384]{1,0:T(8,128)S(1)}, f32[56,384]{1,0:T(8,128)S(1)}, u32[]{:S(2)}, u32[]{:S(2)}) collective-permute-start(f32[56,384]{1,0:T(8,128)S(1)} %get-tuple-element.38), channel_id=1, source_target_pairs={{0,4},{1,5},{2,6},{3,7},{4,0},{5,1},{6,2},{7,3},{8,12},{9,13},{10,... | collective-permute-start | bytes 258056 | tf_op jit(solution)/shard_map/ppermute | solution.py:381
  22.9 6.0 %collective-permute-start.9 = (f32[48,384]{1,0:T(8,128)S(1)}, f32[48,384]{1,0:T(8,128)S(1)}, u32[]{:S(2)}, u32[]{:S(2)}) collective-permute-start(f32[48,384]{1,0:T(8,128)S(1)} %update.5.refs_0_.factor_ref), channel_id=1, source_target_pairs={{0,6},{1,7},{2,4},{3,5},{4,2},{5,3},{6,0},{7,1},{8,14},{9,15},{10,... | collective-permute-start | bytes 221192 | tf_op jit(solution)/shard_map/ppermute | solution.py:381
  32.6 7.3 %collective-permute-start.16 = (f32[56,384]{1,0:T(8,128)S(1)}, f32[56,384]{1,0:T(8,128)S(1)}, u32[]{:S(2)}, u32[]{:S(2)}) collective-permute-start(f32[56,384]{1,0:T(8,128)S(1)} %spectra_times_components.8.refs_0_), channel_id=1, source_target_pairs={{0,24},{1,25},{2,26},{3,27},{4,28},{5,29},{6,30},{7,31},{8,16},{9,... | collective-permute-start | bytes 258056 | tf_op jit(solution)/shard_map/ppermute | solution.py:390
  33.2 9.8 %collective-permute-start.17 = (f32[56,384]{1,0:T(8,128)S(1)}, f32[56,384]{1,0:T(8,128)S(1)}, u32[]{:S(2)}, u32[]{:S(2)}) collective-permute-start(f32[56,384]{1,0:T(8,128)S(1)} %spectra_times_components.8.refs_0_), channel_id=1, source_target_pairs={{0,16},{1,9},{2,18},{3,11},{4,20},{5,13},{6,22},{7,15},{8,24},{9,1... | collective-permute-start | bytes 258056 | tf_op jit(solution)/shard_map/ppermute | solution.py:390
  33.2 9.8 %collective-permute-start.18 = (f32[56,384]{1,0:T(8,128)S(1)}, f32[56,384]{1,0:T(8,128)S(1)}, u32[]{:S(2)}, u32[]{:S(2)}) collective-permute-start(f32[56,384]{1,0:T(8,128)S(1)} %spectra_times_components.8.refs_0_), channel_id=1, source_target_pairs={{0,8},{1,17},{2,10},{3,19},{4,12},{5,21},{6,14},{7,23},{8,0},{9,25... | collective-permute-start | bytes 258056 | tf_op jit(solution)/shard_map/ppermute | solution.py:390
  45.7 6.3 %collective-permute-start.21 = (f32[56,384]{1,0:T(8,128)S(1)}, f32[56,384]{1,0:T(8,128)S(1)}, u32[]{:S(2)}, u32[]{:S(2)}) collective-permute-start(f32[56,384]{1,0:T(8,128)S(1)} %pair_sums.8), channel_id=1, source_target_pairs={{0,6},{1,7},{2,4},{3,5},{4,2},{5,3},{6,0},{7,1},{8,14},{9,15},{10,... | collective-permute-start | bytes 258056 | tf_op jit(solution)/shard_map/ppermute | solution.py:381
  47.6 5.1 %collective-permute-start.23 = (f32[56,384]{1,0:T(8,128)S(1)}, f32[56,384]{1,0:T(8,128)S(1)}, u32[]{:S(2)}, u32[]{:S(2)}) collective-permute-start(f32[56,384]{1,0:T(8,128)S(1)} %get-tuple-element.41), channel_id=1, source_target_pairs={{0,2},{1,3},{2,0},{3,1},{4,6},{5,7},{6,4},{7,5},{8,10},{9,11},{10,... | collective-permute-start | bytes 258056 | tf_op jit(solution)/shard_map/ppermute | solution.py:381
  48.2 5.2 %collective-permute-start.24 = (f32[56,384]{1,0:T(8,128)S(1)}, f32[56,384]{1,0:T(8,128)S(1)}, u32[]{:S(2)}, u32[]{:S(2)}) collective-permute-start(f32[56,384]{1,0:T(8,128)S(1)} %get-tuple-element.42), channel_id=1, source_target_pairs={{0,4},{1,5},{2,6},{3,7},{4,0},{5,1},{6,2},{7,3},{8,12},{9,13},{10,... | collective-permute-start | bytes 258056 | tf_op jit(solution)/shard_map/ppermute | solution.py:381
  53.7 6.1 %collective-permute-start.25 = (f32[48,384]{1,0:T(8,128)S(1)}, f32[48,384]{1,0:T(8,128)S(1)}, u32[]{:S(2)}, u32[]{:S(2)}) collective-permute-start(f32[48,384]{1,0:T(8,128)S(1)} %update.7.refs_0_.factor_ref), channel_id=1, source_target_pairs={{0,6},{1,7},{2,4},{3,5},{4,2},{5,3},{6,0},{7,1},{8,14},{9,15},{10,... | collective-permute-start | bytes 221192 | tf_op jit(solution)/shard_map/ppermute | solution.py:381
  62.8 7.3 %collective-permute-start.32 = (f32[56,384]{1,0:T(8,128)S(1)}, f32[56,384]{1,0:T(8,128)S(1)}, u32[]{:S(2)}, u32[]{:S(2)}) collective-permute-start(f32[56,384]{1,0:T(8,128)S(1)} %spectra_times_components.11.refs_0_), channel_id=1, source_target_pairs={{0,24},{1,25},{2,26},{3,27},{4,28},{5,29},{6,30},{7,31},{8,16},{9,... | collective-permute-start | bytes 258056 | tf_op jit(solution)/shard_map/ppermute | solution.py:390
  63.8 9.5 %collective-permute-start.33 = (f32[56,384]{1,0:T(8,128)S(1)}, f32[56,384]{1,0:T(8,128)S(1)}, u32[]{:S(2)}, u32[]{:S(2)}) collective-permute-start(f32[56,384]{1,0:T(8,128)S(1)} %spectra_times_components.11.refs_0_), channel_id=1, source_target_pairs={{0,16},{1,9},{2,18},{3,11},{4,20},{5,13},{6,22},{7,15},{8,24},{9,1... | collective-permute-start | bytes 258056 | tf_op jit(solution)/shard_map/ppermute | solution.py:390
  63.9 9.4 %collective-permute-start.34 = (f32[56,384]{1,0:T(8,128)S(1)}, f32[56,384]{1,0:T(8,128)S(1)}, u32[]{:S(2)}, u32[]{:S(2)}) collective-permute-start(f32[56,384]{1,0:T(8,128)S(1)} %spectra_times_components.11.refs_0_), channel_id=1, source_target_pairs={{0,8},{1,17},{2,10},{3,19},{4,12},{5,21},{6,14},{7,23},{8,0},{9,25... | collective-permute-start | bytes 258056 | tf_op jit(solution)/shard_map/ppermute | solution.py:390
  76.1 6.4 %collective-permute-start.37 = (f32[56,384]{1,0:T(8,128)S(1)}, f32[56,384]{1,0:T(8,128)S(1)}, u32[]{:S(2)}, u32[]{:S(2)}) collective-permute-start(f32[56,384]{1,0:T(8,128)S(1)} %pair_sums.10), channel_id=1, source_target_pairs={{0,6},{1,7},{2,4},{3,5},{4,2},{5,3},{6,0},{7,1},{8,14},{9,15},{10,... | collective-permute-start | bytes 258056 | tf_op jit(solution)/shard_map/ppermute | solution.py:381
  78.3 5.1 %collective-permute-start.39 = (f32[56,384]{1,0:T(8,128)S(1)}, f32[56,384]{1,0:T(8,128)S(1)}, u32[]{:S(2)}, u32[]{:S(2)}) collective-permute-start(f32[56,384]{1,0:T(8,128)S(1)} %get-tuple-element.45), channel_id=1, source_target_pairs={{0,2},{1,3},{2,0},{3,1},{4,6},{5,7},{6,4},{7,5},{8,10},{9,11},{10,... | collective-permute-start | bytes 258056 | tf_op jit(solution)/shard_map/ppermute | solution.py:381
  78.8 4.9 %collective-permute-start.40 = (f32[56,384]{1,0:T(8,128)S(1)}, f32[56,384]{1,0:T(8,128)S(1)}, u32[]{:S(2)}, u32[]{:S(2)}) collective-permute-start(f32[56,384]{1,0:T(8,128)S(1)} %get-tuple-element.46), channel_id=1, source_target_pairs={{0,4},{1,5},{2,6},{3,7},{4,0},{5,1},{6,2},{7,3},{8,12},{9,13},{10,... | collective-permute-start | bytes 258056 | tf_op jit(solution)/shard_map/ppermute | solution.py:381
  84.0 6.0 %collective-permute-start.41 = (f32[48,384]{1,0:T(8,128)S(1)}, f32[48,384]{1,0:T(8,128)S(1)}, u32[]{:S(2)}, u32[]{:S(2)}) collective-permute-start(f32[48,384]{1,0:T(8,128)S(1)} %update.9.refs_0_.h_ref), channel_id=1, source_target_pairs={{0,6},{1,7},{2,4},{3,5},{4,2},{5,3},{6,0},{7,1},{8,14},{9,15},{10,... | collective-permute-start | bytes 221192 | tf_op jit(solution)/shard_map/ppermute | solution.py:381
  96.4 5.1 %collective-permute-start.48 = (f32[64,128]{1,0:T(8,128)S(1)}, f32[64,128]{1,0:T(8,128)S(1)}, u32[]{:S(2)}, u32[]{:S(2)}) collective-permute-start(f32[64,128]{1,0:T(8,128)S(1)} %get-tuple-element.55), channel_id=1, source_target_pairs={{0,16},{8,24},{16,0},{24,8},{1,17},{9,25},{17,1},{25,9},{2,18},{10... | collective-permute-start | bytes 98312 | tf_op jit(solution)/shard_map/ppermute | solution.py:381
  97.0 5.7 %collective-permute-start.49 = (f32[64,128]{1,0:T(8,128)S(1)}, f32[64,128]{1,0:T(8,128)S(1)}, u32[]{:S(2)}, u32[]{:S(2)}) collective-permute-start(f32[64,128]{1,0:T(8,128)S(1)} %get-tuple-element.56), channel_id=1, source_target_pairs={{0,24},{8,16},{16,8},{24,0},{1,25},{9,17},{17,9},{25,1},{2,26},{10... | collective-permute-start | bytes 98312 | tf_op jit(solution)/shard_map/ppermute | solution.py:381
  (29 other events, 111.6 us)

commit v7 on v6

--- a/solution.py
+++ b/solution.py
@@ -390,7 +390,7 @@
     return lax.ppermute(value, ("mz", "px"), pairs)
 
 
-def spread(h_piece, owners, products):
+def spread(h_piece, owners, products, early=False):
     evens = [owners - 2, *range(2, owners - 2, 2)]
     mine = []
     for relative in evens:
@@ -400,7 +400,11 @@
     for piece in mine:
         theirs.append(swap(piece, "px", owners, 1))
     total = products([0, 1], [h_piece, beside], None, False)
-    total = products(evens, mine, total, False)
+    if early:
+        total = products(evens[:1], mine[:1], total, False)
+        total = products(evens[1:], mine[1:], total, False)
+    else:
+        total = products(evens, mine, total, False)
     return products([r + 1 for r in evens], theirs, total, True)
 
 
@@ -446,6 +450,7 @@
                 lambda relatives, pieces, before, last: final_gather_call(
                     relatives, groups, pieces, copy, w_block, before, last
                 ),
+                True,
             )
             sent = []
             for k in [*range(2, groups), 1]:

time: 104 us -> 104 us (level)
    pallas_call x3 -> x4, Pallas kernels: 5.25 us -> 5.61 us  [final_gather_call(): pl.pallas_call(functools.partial(final_gather_kernel, relatives, groups,...]
where the time goes in v7:
time: 104 us
  starting transfers between devices  42.5 us (41%)
  waiting for transfers between devices  40.4 us (39%)
  Pallas kernels  20.2 us (19%)
    ppermute x45, starting transfers between devices, swap(): return lax.ppermute(value, axis, [(i, i ^ mask) for i in range(size)])  33.7 us
    ppermute x45, waiting for transfers between devices, swap(): return lax.ppermute(value, axis, [(i, i ^ mask) for i in range(size)])  28.4 us
    ppermute x6, waiting for transfers between devices, cross(): return lax.ppermute(value, ('mz', 'px'), pairs)  12 us
    ppermute x6, starting transfers between devices, cross(): return lax.ppermute(value, ('mz', 'px'), pairs)  8.87 us
    pallas_call x4, Pallas kernels, final_gather_call(): pl.pallas_call(functools.partial(final_gather_kernel, relatives, groups,...  5.61 us
    pallas_call x15, Pallas kernels, scatter_call(): pl.pallas_call(functools.partial(scatter_kernel, relatives, width), in_sp...  4.85 us
    pallas_call x6, Pallas kernels, gather_call(): pl.pallas_call(functools.partial(gather_kernel, relatives, before is not...  4.66 us
    pallas_call x1, Pallas kernels, split_call(): pl.pallas_call(functools.partial(split_kernel, step), in_specs=[pl.BlockS...  2.51 us
  transfers between devices with their start and end apart: 51, of which 26 were waited for; matrix products, arithmetic and copies ran while one was open for 0% of the time, Pallas kernels for 12%

profile of v7, /device:TPU:0, one launch (start us, length us, event | category | flops | bytes accessed | tf_op | source)
XLA Modules:
  0.0 104.1 jit_solution(17201385836064726518)
XLA Ops:
  0.6 3.1 %collective-permute-start = (f32[48,96]{1,0:T(8,128)}, f32[48,96]{1,0:T(8,128)S(1)}, u32[]{:S(2)}, u32[]{:S(2)}) collective-permute-start(f32[48,96]{1,0:T(8,128)} %refs_0_.1), channel_id=1, source_target_pairs={{0,8},{8,0},{16,24},{24,16},{1,9},{9,1},{17,25},{25,17},{2,10},{10... | collective-permute-start | bytes 55304 | tf_op jit(solution)/shard_map/ppermute | solution.py:381
  3.8 2.6 %collective-permute-start.1 = (f32[48,96]{1,0:T(8,128)}, f32[48,96]{1,0:T(8,128)S(1)}, u32[]{:S(2)}, u32[]{:S(2)}) collective-permute-start(f32[48,96]{1,0:T(8,128)} %refs_0_.1), channel_id=1, source_target_pairs={{0,16},{8,24},{16,0},{24,8},{1,17},{9,25},{17,1},{25,9},{2,18},{10... | collective-permute-start | bytes 55304 | tf_op jit(solution)/shard_map/ppermute | solution.py:381
  6.3 2.5 %split_spectra.1 = (f32[384,3072]{1,0:T(8,128)S(1)}, bf16[384,3072]{1,0:T(8,128)(2,1)S(1)}, bf16[384,3072]{1,0:T(8,128)(2,1)S(1)}) custom-call(f32[384,3072]{1,0:T(8,128)} %s_ref.1), custom_call_target="tpu_custom_call" | custom-call | flops 4718592 | bytes 14155776 | tf_op jit(solution)/shard_map/split_spectra/pallas_call | solution.py:110
  9.0 3.1 %collective-permute-done.2.refs_3_ = f32[48,96]{1,0:T(8,128)S(1)} collective-permute-done((f32[48,96]{1,0:T(8,128)}, f32[48,96]{1,0:T(8,128)S(1)}, u32[]{:S(2)}, u32[]{:S(2)}) %collective-permute-start.2) | collective-permute-done | bytes 18464 | tf_op jit(solution)/shard_map/ppermute | solution.py:381
  14.7 2.5 %collective-permute-start.5 = (f32[56,384]{1,0:T(8,128)S(1)}, f32[56,384]{1,0:T(8,128)S(1)}, u32[]{:S(2)}, u32[]{:S(2)}) collective-permute-start(f32[56,384]{1,0:T(8,128)S(1)} %pair_sums.6), channel_id=1, source_target_pairs={{0,6},{1,7},{2,4},{3,5},{4,2},{5,3},{6,0},{7,1},{8,14},{9,15},{10,... | collective-permute-start | bytes 258056 | tf_op jit(solution)/shard_map/ppermute | solution.py:381
  18.4 2.7 %collective-permute-done.5.refs_2_ = f32[56,384]{1,0:T(8,128)S(1)} collective-permute-done((f32[56,384]{1,0:T(8,128)S(1)}, f32[56,384]{1,0:T(8,128)S(1)}, u32[]{:S(2)}, u32[]{:S(2)}) %collective-permute-start.5) | collective-permute-done | bytes 86048 | tf_op jit(solution)/shard_map/ppermute | solution.py:381
  22.9 2.4 %collective-permute-start.9 = (f32[48,384]{1,0:T(8,128)S(1)}, f32[48,384]{1,0:T(8,128)S(1)}, u32[]{:S(2)}, u32[]{:S(2)}) collective-permute-start(f32[48,384]{1,0:T(8,128)S(1)} %update.5.refs_0_.factor_ref), channel_id=1, source_target_pairs={{0,6},{1,7},{2,4},{3,5},{4,2},{5,3},{6,0},{7,1},{8,14},{9,15},{10,... | collective-permute-start | bytes 221192 | tf_op jit(solution)/shard_map/ppermute | solution.py:381
  26.4 2.5 %collective-permute-done.9.refs_0_ = f32[48,384]{1,0:T(8,128)S(1)} collective-permute-done((f32[48,384]{1,0:T(8,128)S(1)}, f32[48,384]{1,0:T(8,128)S(1)}, u32[]{:S(2)}, u32[]{:S(2)}) %collective-permute-start.9) | collective-permute-done | bytes 73760 | tf_op jit(solution)/shard_map/ppermute | solution.py:381
  33.2 3.8 %collective-permute-start.18 = (f32[56,384]{1,0:T(8,128)S(1)}, f32[56,384]{1,0:T(8,128)S(1)}, u32[]{:S(2)}, u32[]{:S(2)}) collective-permute-start(f32[56,384]{1,0:T(8,128)S(1)} %spectra_times_components.8.refs_0_), channel_id=1, source_target_pairs={{0,8},{1,17},{2,10},{3,19},{4,12},{5,21},{6,14},{7,23},{8,0},{9,25... | collective-permute-start | bytes 258056 | tf_op jit(solution)/shard_map/ppermute | solution.py:390
  37.0 2.9 %collective-permute-done.16.refs_1_ = f32[56,384]{1,0:T(8,128)S(1)} collective-permute-done((f32[56,384]{1,0:T(8,128)S(1)}, f32[56,384]{1,0:T(8,128)S(1)}, u32[]{:S(2)}, u32[]{:S(2)}) %collective-permute-start.16) | collective-permute-done | bytes 86048 | tf_op jit(solution)/shard_map/ppermute | solution.py:390
  39.9 3.1 %collective-permute-done.17.refs_2_ = f32[56,384]{1,0:T(8,128)S(1)} collective-permute-done((f32[56,384]{1,0:T(8,128)S(1)}, f32[56,384]{1,0:T(8,128)S(1)}, u32[]{:S(2)}, u32[]{:S(2)}) %collective-permute-start.17) | collective-permute-done | bytes 86048 | tf_op jit(solution)/shard_map/ppermute | solution.py:390
  45.7 1.8 %collective-permute-start.21 = (f32[56,384]{1,0:T(8,128)S(1)}, f32[56,384]{1,0:T(8,128)S(1)}, u32[]{:S(2)}, u32[]{:S(2)}) collective-permute-start(f32[56,384]{1,0:T(8,128)S(1)} %pair_sums.8), channel_id=1, source_target_pairs={{0,6},{1,7},{2,4},{3,5},{4,2},{5,3},{6,0},{7,1},{8,14},{9,15},{10,... | collective-permute-start | bytes 258056 | tf_op jit(solution)/shard_map/ppermute | solution.py:381
  49.4 2.7 %collective-permute-done.21.refs_2_ = f32[56,384]{1,0:T(8,128)S(1)} collective-permute-done((f32[56,384]{1,0:T(8,128)S(1)}, f32[56,384]{1,0:T(8,128)S(1)}, u32[]{:S(2)}, u32[]{:S(2)}) %collective-permute-start.21) | collective-permute-done | bytes 86048 | tf_op jit(solution)/shard_map/ppermute | solution.py:381
  53.7 1.9 %collective-permute-start.25 = (f32[48,384]{1,0:T(8,128)S(1)}, f32[48,384]{1,0:T(8,128)S(1)}, u32[]{:S(2)}, u32[]{:S(2)}) collective-permute-start(f32[48,384]{1,0:T(8,128)S(1)} %update.7.refs_0_.factor_ref), channel_id=1, source_target_pairs={{0,6},{1,7},{2,4},{3,5},{4,2},{5,3},{6,0},{7,1},{8,14},{9,15},{10,... | collective-permute-start | bytes 221192 | tf_op jit(solution)/shard_map/ppermute | solution.py:381
  57.2 2.5 %collective-permute-done.25.refs_0_ = f32[48,384]{1,0:T(8,128)S(1)} collective-permute-done((f32[48,384]{1,0:T(8,128)S(1)}, f32[48,384]{1,0:T(8,128)S(1)}, u32[]{:S(2)}, u32[]{:S(2)}) %collective-permute-start.25) | collective-permute-done | bytes 73760 | tf_op jit(solution)/shard_map/ppermute | solution.py:381
  63.9 3.4 %collective-permute-start.34 = (f32[56,384]{1,0:T(8,128)S(1)}, f32[56,384]{1,0:T(8,128)S(1)}, u32[]{:S(2)}, u32[]{:S(2)}) collective-permute-start(f32[56,384]{1,0:T(8,128)S(1)} %spectra_times_components.11.refs_0_), channel_id=1, source_target_pairs={{0,8},{1,17},{2,10},{3,19},{4,12},{5,21},{6,14},{7,23},{8,0},{9,25... | collective-permute-start | bytes 258056 | tf_op jit(solution)/shard_map/ppermute | solution.py:390
  67.3 2.9 %collective-permute-done.32.refs_1_ = f32[56,384]{1,0:T(8,128)S(1)} collective-permute-done((f32[56,384]{1,0:T(8,128)S(1)}, f32[56,384]{1,0:T(8,128)S(1)}, u32[]{:S(2)}, u32[]{:S(2)}) %collective-permute-start.32) | collective-permute-done | bytes 86048 | tf_op jit(solution)/shard_map/ppermute | solution.py:390
  70.2 3.1 %collective-permute-done.33.refs_2_ = f32[56,384]{1,0:T(8,128)S(1)} collective-permute-done((f32[56,384]{1,0:T(8,128)S(1)}, f32[56,384]{1,0:T(8,128)S(1)}, u32[]{:S(2)}, u32[]{:S(2)}) %collective-permute-start.33) | collective-permute-done | bytes 86048 | tf_op jit(solution)/shard_map/ppermute | solution.py:390
  76.1 2.2 %collective-permute-start.37 = (f32[56,384]{1,0:T(8,128)S(1)}, f32[56,384]{1,0:T(8,128)S(1)}, u32[]{:S(2)}, u32[]{:S(2)}) collective-permute-start(f32[56,384]{1,0:T(8,128)S(1)} %pair_sums.10), channel_id=1, source_target_pairs={{0,6},{1,7},{2,4},{3,5},{4,2},{5,3},{6,0},{7,1},{8,14},{9,15},{10,... | collective-permute-start | bytes 258056 | tf_op jit(solution)/shard_map/ppermute | solution.py:381
  79.7 2.7 %collective-permute-done.37.refs_2_ = f32[56,384]{1,0:T(8,128)S(1)} collective-permute-done((f32[56,384]{1,0:T(8,128)S(1)}, f32[56,384]{1,0:T(8,128)S(1)}, u32[]{:S(2)}, u32[]{:S(2)}) %collective-permute-start.37) | collective-permute-done | bytes 86048 | tf_op jit(solution)/shard_map/ppermute | solution.py:381
  84.0 2.2 %collective-permute-start.41 = (f32[48,384]{1,0:T(8,128)S(1)}, f32[48,384]{1,0:T(8,128)S(1)}, u32[]{:S(2)}, u32[]{:S(2)}) collective-permute-start(f32[48,384]{1,0:T(8,128)S(1)} %update.9.refs_0_.h_ref), channel_id=1, source_target_pairs={{0,6},{1,7},{2,4},{3,5},{4,2},{5,3},{6,0},{7,1},{8,14},{9,15},{10,... | collective-permute-start | bytes 221192 | tf_op jit(solution)/shard_map/ppermute | solution.py:381
  87.6 2.4 %collective-permute-done.41.refs_0_ = f32[48,384]{1,0:T(8,128)S(1)} collective-permute-done((f32[48,384]{1,0:T(8,128)S(1)}, f32[48,384]{1,0:T(8,128)S(1)}, u32[]{:S(2)}, u32[]{:S(2)}) %collective-permute-start.41) | collective-permute-done | bytes 73760 | tf_op jit(solution)/shard_map/ppermute | solution.py:381
  94.7 2.1 %final_products.7 = (f32[64,128]{1,0:T(8,128)S(1)}, f32[64,128]{1,0:T(8,128)S(1)}, f32[64,128]{1,0:T(8,128)S(1)}, f32[64,128]{1,0:T(8,128)S(1)}, f32[48,96]{1,0:T(8,128)S(1)}) custom-call(f32[384,3072]{1,0:T(8,128)S(1)} %get-tuple-element.35.s_ref, f32[48,384]{1,0:T(8,128)S(1)} %update.8.w_ref, f32[48,384]{1,0:T(8,128)S(1)} %collective-permute-done.42.refs_0_, ...), custom_call_target="tpu_custom_call" | custom-call | flops 382205952 | bytes 3538944 | tf_op jit(solution)/shard_map/final_products/pallas_call | solution.py:307
  98.6 1.7 %collective-permute-start.50 = (f32[64,128]{1,0:T(8,128)S(1)}, f32[64,128]{1,0:T(8,128)S(1)}, u32[]{:S(2)}, u32[]{:S(2)}) collective-permute-start(f32[64,128]{1,0:T(8,128)S(1)} %get-tuple-element.63), channel_id=1, source_target_pairs={{0,8},{8,0},{16,24},{24,16},{1,9},{9,1},{17,25},{25,17},{2,10},{10... | collective-permute-start | bytes 98312 | tf_op jit(solution)/shard_map/ppermute | solution.py:381
  (121 shorter events, 40.2 us)
Async XLA Ops:
  0.6 8.2 %collective-permute-start = (f32[48,96]{1,0:T(8,128)}, f32[48,96]{1,0:T(8,128)S(1)}, u32[]{:S(2)}, u32[]{:S(2)}) collective-permute-start(f32[48,96]{1,0:T(8,128)} %refs_0_.1), channel_id=1, source_target_pairs={{0,8},{8,0},{16,24},{24,16},{1,9},{9,1},{17,25},{25,17},{2,10},{10... | collective-permute-start | bytes 55304 | tf_op jit(solution)/shard_map/ppermute | solution.py:381
  3.8 5.3 %collective-permute-start.1 = (f32[48,96]{1,0:T(8,128)}, f32[48,96]{1,0:T(8,128)S(1)}, u32[]{:S(2)}, u32[]{:S(2)}) collective-permute-start(f32[48,96]{1,0:T(8,128)} %refs_0_.1), channel_id=1, source_target_pairs={{0,16},{8,24},{16,0},{24,8},{1,17},{9,25},{17,1},{25,9},{2,18},{10... | collective-permute-start | bytes 55304 | tf_op jit(solution)/shard_map/ppermute | solution.py:381
  6.3 5.8 %collective-permute-start.2 = (f32[48,96]{1,0:T(8,128)}, f32[48,96]{1,0:T(8,128)S(1)}, u32[]{:S(2)}, u32[]{:S(2)}) collective-permute-start(f32[48,96]{1,0:T(8,128)} %refs_0_.1), channel_id=1, source_target_pairs={{0,24},{8,16},{16,8},{24,0},{1,25},{9,17},{17,9},{25,1},{2,26},{10... | collective-permute-start | bytes 55304 | tf_op jit(solution)/shard_map/ppermute | solution.py:381
  14.7 6.4 %collective-permute-start.5 = (f32[56,384]{1,0:T(8,128)S(1)}, f32[56,384]{1,0:T(8,128)S(1)}, u32[]{:S(2)}, u32[]{:S(2)}) collective-permute-start(f32[56,384]{1,0:T(8,128)S(1)} %pair_sums.6), channel_id=1, source_target_pairs={{0,6},{1,7},{2,4},{3,5},{4,2},{5,3},{6,0},{7,1},{8,14},{9,15},{10,... | collective-permute-start | bytes 258056 | tf_op jit(solution)/shard_map/ppermute | solution.py:381
  17.3 5.2 %collective-permute-start.7 = (f32[56,384]{1,0:T(8,128)S(1)}, f32[56,384]{1,0:T(8,128)S(1)}, u32[]{:S(2)}, u32[]{:S(2)}) collective-permute-start(f32[56,384]{1,0:T(8,128)S(1)} %get-tuple-element.40), channel_id=1, source_target_pairs={{0,2},{1,3},{2,0},{3,1},{4,6},{5,7},{6,4},{7,5},{8,10},{9,11},{10,... | collective-permute-start | bytes 258056 | tf_op jit(solution)/shard_map/ppermute | solution.py:381
  17.9 4.7 %collective-permute-start.8 = (f32[56,384]{1,0:T(8,128)S(1)}, f32[56,384]{1,0:T(8,128)S(1)}, u32[]{:S(2)}, u32[]{:S(2)}) collective-permute-start(f32[56,384]{1,0:T(8,128)S(1)} %get-tuple-element.41), channel_id=1, source_target_pairs={{0,4},{1,5},{2,6},{3,7},{4,0},{5,1},{6,2},{7,3},{8,12},{9,13},{10,... | collective-permute-start | bytes 258056 | tf_op jit(solution)/shard_map/ppermute | solution.py:381
  22.9 6.0 %collective-permute-start.9 = (f32[48,384]{1,0:T(8,128)S(1)}, f32[48,384]{1,0:T(8,128)S(1)}, u32[]{:S(2)}, u32[]{:S(2)}) collective-permute-start(f32[48,384]{1,0:T(8,128)S(1)} %update.5.refs_0_.factor_ref), channel_id=1, source_target_pairs={{0,6},{1,7},{2,4},{3,5},{4,2},{5,3},{6,0},{7,1},{8,14},{9,15},{10,... | collective-permute-start | bytes 221192 | tf_op jit(solution)/shard_map/ppermute | solution.py:381
  32.6 7.3 %collective-permute-start.16 = (f32[56,384]{1,0:T(8,128)S(1)}, f32[56,384]{1,0:T(8,128)S(1)}, u32[]{:S(2)}, u32[]{:S(2)}) collective-permute-start(f32[56,384]{1,0:T(8,128)S(1)} %spectra_times_components.8.refs_0_), channel_id=1, source_target_pairs={{0,24},{1,25},{2,26},{3,27},{4,28},{5,29},{6,30},{7,31},{8,16},{9,... | collective-permute-start | bytes 258056 | tf_op jit(solution)/shard_map/ppermute | solution.py:390
  33.2 9.8 %collective-permute-start.17 = (f32[56,384]{1,0:T(8,128)S(1)}, f32[56,384]{1,0:T(8,128)S(1)}, u32[]{:S(2)}, u32[]{:S(2)}) collective-permute-start(f32[56,384]{1,0:T(8,128)S(1)} %spectra_times_components.8.refs_0_), channel_id=1, source_target_pairs={{0,16},{1,9},{2,18},{3,11},{4,20},{5,13},{6,22},{7,15},{8,24},{9,1... | collective-permute-start | bytes 258056 | tf_op jit(solution)/shard_map/ppermute | solution.py:390
  33.2 9.8 %collective-permute-start.18 = (f32[56,384]{1,0:T(8,128)S(1)}, f32[56,384]{1,0:T(8,128)S(1)}, u32[]{:S(2)}, u32[]{:S(2)}) collective-permute-start(f32[56,384]{1,0:T(8,128)S(1)} %spectra_times_components.8.refs_0_), channel_id=1, source_target_pairs={{0,8},{1,17},{2,10},{3,19},{4,12},{5,21},{6,14},{7,23},{8,0},{9,25... | collective-permute-start | bytes 258056 | tf_op jit(solution)/shard_map/ppermute | solution.py:390
  45.7 6.3 %collective-permute-start.21 = (f32[56,384]{1,0:T(8,128)S(1)}, f32[56,384]{1,0:T(8,128)S(1)}, u32[]{:S(2)}, u32[]{:S(2)}) collective-permute-start(f32[56,384]{1,0:T(8,128)S(1)} %pair_sums.8), channel_id=1, source_target_pairs={{0,6},{1,7},{2,4},{3,5},{4,2},{5,3},{6,0},{7,1},{8,14},{9,15},{10,... | collective-permute-start | bytes 258056 | tf_op jit(solution)/shard_map/ppermute | solution.py:381
  47.6 5.1 %collective-permute-start.23 = (f32[56,384]{1,0:T(8,128)S(1)}, f32[56,384]{1,0:T(8,128)S(1)}, u32[]{:S(2)}, u32[]{:S(2)}) collective-permute-start(f32[56,384]{1,0:T(8,128)S(1)} %get-tuple-element.44), channel_id=1, source_target_pairs={{0,2},{1,3},{2,0},{3,1},{4,6},{5,7},{6,4},{7,5},{8,10},{9,11},{10,... | collective-permute-start | bytes 258056 | tf_op jit(solution)/shard_map/ppermute | solution.py:381
  48.2 5.2 %collective-permute-start.24 = (f32[56,384]{1,0:T(8,128)S(1)}, f32[56,384]{1,0:T(8,128)S(1)}, u32[]{:S(2)}, u32[]{:S(2)}) collective-permute-start(f32[56,384]{1,0:T(8,128)S(1)} %get-tuple-element.45), channel_id=1, source_target_pairs={{0,4},{1,5},{2,6},{3,7},{4,0},{5,1},{6,2},{7,3},{8,12},{9,13},{10,... | collective-permute-start | bytes 258056 | tf_op jit(solution)/shard_map/ppermute | solution.py:381
  53.7 6.1 %collective-permute-start.25 = (f32[48,384]{1,0:T(8,128)S(1)}, f32[48,384]{1,0:T(8,128)S(1)}, u32[]{:S(2)}, u32[]{:S(2)}) collective-permute-start(f32[48,384]{1,0:T(8,128)S(1)} %update.7.refs_0_.factor_ref), channel_id=1, source_target_pairs={{0,6},{1,7},{2,4},{3,5},{4,2},{5,3},{6,0},{7,1},{8,14},{9,15},{10,... | collective-permute-start | bytes 221192 | tf_op jit(solution)/shard_map/ppermute | solution.py:381
  62.8 7.3 %collective-permute-start.32 = (f32[56,384]{1,0:T(8,128)S(1)}, f32[56,384]{1,0:T(8,128)S(1)}, u32[]{:S(2)}, u32[]{:S(2)}) collective-permute-start(f32[56,384]{1,0:T(8,128)S(1)} %spectra_times_components.11.refs_0_), channel_id=1, source_target_pairs={{0,24},{1,25},{2,26},{3,27},{4,28},{5,29},{6,30},{7,31},{8,16},{9,... | collective-permute-start | bytes 258056 | tf_op jit(solution)/shard_map/ppermute | solution.py:390
  63.8 9.5 %collective-permute-start.33 = (f32[56,384]{1,0:T(8,128)S(1)}, f32[56,384]{1,0:T(8,128)S(1)}, u32[]{:S(2)}, u32[]{:S(2)}) collective-permute-start(f32[56,384]{1,0:T(8,128)S(1)} %spectra_times_components.11.refs_0_), channel_id=1, source_target_pairs={{0,16},{1,9},{2,18},{3,11},{4,20},{5,13},{6,22},{7,15},{8,24},{9,1... | collective-permute-start | bytes 258056 | tf_op jit(solution)/shard_map/ppermute | solution.py:390
  63.9 9.4 %collective-permute-start.34 = (f32[56,384]{1,0:T(8,128)S(1)}, f32[56,384]{1,0:T(8,128)S(1)}, u32[]{:S(2)}, u32[]{:S(2)}) collective-permute-start(f32[56,384]{1,0:T(8,128)S(1)} %spectra_times_components.11.refs_0_), channel_id=1, source_target_pairs={{0,8},{1,17},{2,10},{3,19},{4,12},{5,21},{6,14},{7,23},{8,0},{9,25... | collective-permute-start | bytes 258056 | tf_op jit(solution)/shard_map/ppermute | solution.py:390
  76.1 6.4 %collective-permute-start.37 = (f32[56,384]{1,0:T(8,128)S(1)}, f32[56,384]{1,0:T(8,128)S(1)}, u32[]{:S(2)}, u32[]{:S(2)}) collective-permute-start(f32[56,384]{1,0:T(8,128)S(1)} %pair_sums.10), channel_id=1, source_target_pairs={{0,6},{1,7},{2,4},{3,5},{4,2},{5,3},{6,0},{7,1},{8,14},{9,15},{10,... | collective-permute-start | bytes 258056 | tf_op jit(solution)/shard_map/ppermute | solution.py:381
  78.3 5.1 %collective-permute-start.39 = (f32[56,384]{1,0:T(8,128)S(1)}, f32[56,384]{1,0:T(8,128)S(1)}, u32[]{:S(2)}, u32[]{:S(2)}) collective-permute-start(f32[56,384]{1,0:T(8,128)S(1)} %get-tuple-element.48), channel_id=1, source_target_pairs={{0,2},{1,3},{2,0},{3,1},{4,6},{5,7},{6,4},{7,5},{8,10},{9,11},{10,... | collective-permute-start | bytes 258056 | tf_op jit(solution)/shard_map/ppermute | solution.py:381
  78.8 4.9 %collective-permute-start.40 = (f32[56,384]{1,0:T(8,128)S(1)}, f32[56,384]{1,0:T(8,128)S(1)}, u32[]{:S(2)}, u32[]{:S(2)}) collective-permute-start(f32[56,384]{1,0:T(8,128)S(1)} %get-tuple-element.49), channel_id=1, source_target_pairs={{0,4},{1,5},{2,6},{3,7},{4,0},{5,1},{6,2},{7,3},{8,12},{9,13},{10,... | collective-permute-start | bytes 258056 | tf_op jit(solution)/shard_map/ppermute | solution.py:381
  84.0 6.0 %collective-permute-start.41 = (f32[48,384]{1,0:T(8,128)S(1)}, f32[48,384]{1,0:T(8,128)S(1)}, u32[]{:S(2)}, u32[]{:S(2)}) collective-permute-start(f32[48,384]{1,0:T(8,128)S(1)} %update.9.refs_0_.h_ref), channel_id=1, source_target_pairs={{0,6},{1,7},{2,4},{3,5},{4,2},{5,3},{6,0},{7,1},{8,14},{9,15},{10,... | collective-permute-start | bytes 221192 | tf_op jit(solution)/shard_map/ppermute | solution.py:381
  90.0 4.6 %collective-permute-start.42 = (f32[48,384]{1,0:T(8,128)S(1)}, f32[48,384]{1,0:T(8,128)S(1)}, u32[]{:S(2)}, u32[]{:S(2)}) collective-permute-start(f32[48,384]{1,0:T(8,128)S(1)} %collective-permute-done.41.refs_0_), channel_id=1, source_target_pairs={{0,1},{1,0},{2,3},{3,2},{4,5},{5,4},{6,7},{7,6},{8,9},{9,8},{10,11... | collective-permute-start | bytes 221192 | tf_op jit(solution)/shard_map/ppermute | solution.py:381
  96.8 5.1 %collective-permute-start.48 = (f32[64,128]{1,0:T(8,128)S(1)}, f32[64,128]{1,0:T(8,128)S(1)}, u32[]{:S(2)}, u32[]{:S(2)}) collective-permute-start(f32[64,128]{1,0:T(8,128)S(1)} %get-tuple-element.61), channel_id=1, source_target_pairs={{0,16},{8,24},{16,0},{24,8},{1,17},{9,25},{17,1},{25,9},{2,18},{10... | collective-permute-start | bytes 98312 | tf_op jit(solution)/shard_map/ppermute | solution.py:381
  97.4 5.7 %collective-permute-start.49 = (f32[64,128]{1,0:T(8,128)S(1)}, f32[64,128]{1,0:T(8,128)S(1)}, u32[]{:S(2)}, u32[]{:S(2)}) collective-permute-start(f32[64,128]{1,0:T(8,128)S(1)} %get-tuple-element.62), channel_id=1, source_target_pairs={{0,24},{8,16},{16,8},{24,0},{1,25},{9,17},{17,9},{25,1},{2,26},{10... | collective-permute-start | bytes 98312 | tf_op jit(solution)/shard_map/ppermute | solution.py:381
  (29 other events, 112.7 us)
